TPU v7x, 256 devices: a whole 4x4x8 slice. The times are simulated.
256 devices in a mesh: leaf: 64 (over x, z, core), rhs: 4 (over y).
Axes of the slice: x: 4, y: 4, z: 8, core: 2. Of those that a mesh axis runs over, the one named last changes fastest.
Arguments:
- rhs_vectors: bfloat16 [32, 131072], P('rhs', 'leaf'), may hold values from -6 to 6
- diag_inverse: bfloat16 [131072, 2048], P('leaf'), may hold values from -1 to 2
- left_factors: bfloat16 [131072, 384], P('leaf'), may hold values from -0.125 to 0.125
- right_factors: bfloat16 [131072, 384], P('leaf'), may hold values from -0.125 to 0.125
- ranks: int32 [6], replicated, may hold values from 32 to 64, as said below
Outputs:
- solution: float32 [32, 131072], P('rhs', 'leaf')
Inputs may be any that keep to these rules, and one draw needn't show every extreme that they name: `ranks`: some level has rank exactly 64.
All inputs are finite; a program needn't handle non-finite values.
Results may differ from a plain program's by a relative error of at most 0.0031.
Values sent between devices are 32-bit elements; how exact they have to be, the bound alone decides.
No kernel may reach another device: no remote copies, remote signals or barrier semaphores. Data moves between devices by JAX's collectives and lax.ppermute only.
A program may use at most 64 MiB of HBM per device.

v0:
```python
import jax
import jax.numpy as jnp
from jax import lax
from jax.sharding import PartitionSpec as P

best_precision = lax.Precision.HIGHEST


def swapped(x, axis, distance):
    return lax.ppermute(x, axis, [(i, i ^ 1 << distance) for i in range(lax.axis_size(axis))])


def compose(former, latter):
    joined_map = jnp.dot(latter[0], former[0], precision=best_precision)
    joined_shift = jnp.dot(latter[0], former[1], precision=best_precision) + latter[1]
    return (joined_map, joined_shift)


def on_device(rhs_vectors, diag_inverse, left_factors, right_factors, ranks):
    leaves = lax.axis_size("leaf")
    levels = leaves.bit_length() - 1
    state_rows = left_factors.shape[1]
    rank_top = state_rows // levels
    position = lax.axis_index("leaf")
    row_level = jnp.arange(state_rows, dtype=jnp.int32) // rank_top
    row_rank = jnp.arange(state_rows, dtype=jnp.int32) % rank_top
    level_table = jnp.arange(levels, dtype=jnp.int32)
    rank_of = jnp.sum(
        jnp.where(row_level[:, None] == level_table[None, :], ranks[None, :], 0), axis=1
    )
    column_keep = (row_rank < rank_of).astype(jnp.bfloat16)
    left_kept = left_factors * column_keep[None, :]
    right_kept = right_factors * column_keep[None, :]
    right_wide = right_kept.astype(jnp.float32)
    level_bit = (position >> row_level & 1).astype(jnp.float32)
    span_mask = jnp.left_shift(jnp.int32(2), row_level)
    reset_keep = jnp.where((position + 1) % span_mask == 0, 0.0, 1.0).astype(jnp.float32)
    mapped = jnp.dot(diag_inverse, left_kept, preferred_element_type=jnp.float32).astype(
        jnp.bfloat16
    )
    coupling = jnp.einsum("mr,ms->rs", right_kept, mapped, preferred_element_type=jnp.float32)
    identity = jnp.eye(state_rows, dtype=jnp.float32)
    open_rows = 1.0 - level_bit
    step_map = reset_keep[:, None] * (identity - open_rows[:, None] * coupling * level_bit[None, :])
    inverse_rhs = jnp.einsum(
        "km,nm->kn", rhs_vectors, diag_inverse, preferred_element_type=jnp.float32
    )
    projected = jnp.einsum("mr,km->rk", right_wide, inverse_rhs, precision=best_precision)
    step_shift = (reset_keep * open_rows)[:, None] * projected
    empty_shift = jnp.zeros_like(step_shift)
    total_map, total_shift = (step_map, step_shift)
    prefix_map, prefix_shift = (identity, empty_shift)
    for bit_level in range(levels):
        lowest = bit_level * rank_top
        got_map, got_shift = swapped((total_map[lowest:], total_shift[lowest:]), "leaf", bit_level)
        partner_map = jnp.concatenate(
            [jnp.zeros((lowest, state_rows), jnp.float32), got_map], axis=0
        )
        partner_shift = jnp.concatenate(
            [jnp.zeros((lowest, step_shift.shape[1]), jnp.float32), got_shift], axis=0
        )
        upper_half = position >> bit_level & 1 == 1
        after_map, after_shift = compose((partner_map, partner_shift), (total_map, total_shift))
        before_map, before_shift = compose((total_map, total_shift), (partner_map, partner_shift))
        joined_map, joined_shift = compose((partner_map, partner_shift), (prefix_map, prefix_shift))
        total_map = jnp.where(upper_half, after_map, before_map)
        total_shift = jnp.where(upper_half, after_shift, before_shift)
        prefix_map = jnp.where(upper_half, joined_map, prefix_map)
        prefix_shift = jnp.where(upper_half, joined_shift, prefix_shift)
    correction = jnp.einsum(
        "ms,sk->km",
        mapped.astype(jnp.float32),
        level_bit[:, None] * prefix_shift,
        precision=best_precision,
    )
    return inverse_rhs - correction


def solution(mesh):
    in_specs = (P("rhs", "leaf"), P("leaf", None), P("leaf", None), P("leaf", None), P())
    out_specs = P("rhs", "leaf")
    return jax.shard_map(
        on_device, mesh=mesh, in_specs=in_specs, out_specs=out_specs, check_vma=False
    )
```

profile of v0, /device:TPU:8, one launch (start us, length us, event | category | flops | bytes accessed | tf_op | source)
XLA Modules:
  0.0 105.4 jit_solution(13227227736498233069)
XLA Ops:
  0.0 0.7 select_reduce_fusion
  0.9 7.5 %convolution_convert_fusion = bf16[384,2048]{1,0:T(8,128)(2,1)S(1)} fusion(bf16[2048,2048]{1,0:T(8,128)(2,1)} %param.6, bf16[2048,384]{1,0:T(8,128)(2,1)} %param.7, bf16[384]{0:T(512)(128)(2,1)S(1)} %fusion.74), kind=kOutput, calls=%fused_computation | convolution fusion | flops 3222798336 | bytes 11535104 | tf_op jit(solution)/shard_map/dot_general | solution.py:38
  8.4 1.0 fusion.14
  9.6 2.3 %fusion.99 = f32[8,2048]{1,0:T(8,128)S(1)} fusion(bf16[8,2048]{1,0:T(8,128)(2,1)S(1)} %copy-done, bf16[2048,2048]{1,0:T(8,128)(2,1)S(1)} %copy-done.1), kind=kOutput, calls=%fused_computation.129 | convolution fusion | flops 67108864 | bytes 8486912 | tf_op jit(solution)/shard_map/km,nm->kn/dot_general | solution.py:45
  12.0 0.8 fusion.17
  12.8 0.5 collective-permute-start.5
  13.3 0.8 collective-permute-done.5
  14.4 0.6 convolution_add_fusion.11
  15.0 0.7 fusion.29
  15.8 2.1 %collective-permute-start.6 = (f32[320,8]{0,1:T(8,128)S(1)}, f32[320,8]{0,1:T(8,128)S(1)}, u32[]{:S(2)}, u32[]{:S(2)}) collective-permute-start(f32[320,8]{0,1:T(8,128)S(1)} %slice.40), channel_id=1, source_target_pairs={{0,8},{4,12},{8,0},{12,4},{16,24},{20,28},{24,16},{28,20},{32,40},... | collective-permute-start | bytes 30728 | tf_op jit(solution)/shard_map/ppermute | solution.py:10
  17.9 1.3 %fusion.100 = f32[384,384]{1,0:T(8,128)S(1)} fusion(f32[384,384]{1,0:T(8,128)S(1)} %collective-permute-done, f32[384,384]{1,0:T(8,128)S(1)} %fusion.14), kind=kOutput, calls=%fused_computation.130 | convolution fusion | flops 679477248 | bytes 1769472 | tf_op jit(solution)/shard_map/dot_general | solution.py:14
  19.2 1.3 %convolution_select_fusion.7 = f32[384,384]{1,0:T(8,128)S(1)} fusion(f32[384,384]{1,0:T(8,128)S(1)} %fusion.100, f32[384,384]{1,0:T(8,128)S(1)} %fusion.14, f32[384,384]{1,0:T(8,128)S(1)} %collective-permute-done, pred[]{:T(512)S(6)} %eq.73), kind=kOutput, calls=%fused_computation.16 | convolution fusion | flops 679624704 | bytes 2359297 | tf_op jit(solution)/shard_map/dot_general | solution.py:14
  20.7 0.8 convolution_select_fusion.8
  21.5 0.6 fusion.20
  22.1 11.7 %collective-permute-done.1 = f32[320,384]{1,0:T(8,128)S(1)} collective-permute-done((f32[320,384]{1,0:T(8,128)S(1)}, f32[320,384]{1,0:T(8,128)S(1)}, u32[]{:S(2)}, u32[]{:S(2)}) %collective-permute-start.1) | collective-permute-done | bytes 491552 | tf_op jit(solution)/shard_map/ppermute | solution.py:10
  33.8 0.6 convolution_add_fusion.9
  34.4 0.7 fusion.28
  35.1 3.4 %collective-permute-start.7 = (f32[256,8]{0,1:T(8,128)S(1)}, f32[256,8]{0,1:T(8,128)S(1)}, u32[]{:S(2)}, u32[]{:S(2)}) collective-permute-start(f32[256,8]{0,1:T(8,128)S(1)} %slice.41), channel_id=1, source_target_pairs={{0,16},{4,20},{8,24},{12,28},{16,0},{20,4},{24,8},{28,12},{32,48},... | collective-permute-start | bytes 24584 | tf_op jit(solution)/shard_map/ppermute | solution.py:10
  38.5 1.3 %fusion.47 = f32[384,384]{1,0:T(8,128)S(1)} fusion(f32[384,384]{1,0:T(8,128)S(1)} %convolution_select_fusion.7, f32[320,384]{1,0:T(8,128)S(1)} %collective-permute-done.1), kind=kOutput, calls=%fused_computation.62 | convolution fusion | flops 679477248 | bytes 1671168 | tf_op jit(solution)/shard_map/dot_general | solution.py:14
  39.7 1.3 %convolution_select_fusion.6 = f32[384,384]{1,0:T(8,128)S(1)} fusion(f32[384,384]{1,0:T(8,128)S(1)} %fusion.47, f32[384,384]{1,0:T(8,128)S(1)} %convolution_select_fusion.7, f32[320,384]{1,0:T(8,128)S(1)} %collective-permute-done.1, pred[]{:T(512)S(6)} %eq.72), kind=kOutput, calls=%fused_computation.15 | convolution fusion | flops 679624704 | bytes 2260993 | tf_op jit(solution)/shard_map/dot_general | solution.py:14
  41.2 1.3 %convolution_select_fusion.3 = f32[384,384]{1,0:T(8,128)S(1)} fusion(f32[384,384]{1,0:T(8,128)S(1)} %convolution_select_fusion.8, f32[320,384]{1,0:T(8,128)S(1)} %collective-permute-done.1, pred[]{:T(512)S(6)} %eq.72), kind=kOutput, calls=%fused_computation.10 | convolution fusion | flops 679624704 | bytes 1671169 | tf_op jit(solution)/shard_map/dot_general | solution.py:14
  42.4 0.6 fusion.21
  43.0 17.3 %collective-permute-done.2 = f32[256,384]{1,0:T(8,128)S(1)} collective-permute-done((f32[256,384]{1,0:T(8,128)S(1)}, f32[256,384]{1,0:T(8,128)S(1)}, u32[]{:S(2)}, u32[]{:S(2)}) %collective-permute-start.2) | collective-permute-done | bytes 393248 | tf_op jit(solution)/shard_map/ppermute | solution.py:10
  60.3 0.6 convolution_add_fusion.7
  60.9 0.7 fusion.27
  61.7 4.8 %collective-permute-start.8 = (f32[192,8]{0,1:T(8,128)S(1)}, f32[192,8]{0,1:T(8,128)S(1)}, u32[]{:S(2)}, u32[]{:S(2)}) collective-permute-start(f32[192,8]{0,1:T(8,128)S(1)} %slice.42), channel_id=1, source_target_pairs={{0,32},{4,36},{8,40},{12,44},{16,48},{20,52},{24,56},{28,60},{32,0... | collective-permute-start | bytes 18440 | tf_op jit(solution)/shard_map/ppermute | solution.py:10
  66.5 1.3 %fusion.39 = f32[384,384]{1,0:T(8,128)S(1)} fusion(f32[384,384]{1,0:T(8,128)S(1)} %convolution_select_fusion.6, f32[256,384]{1,0:T(8,128)S(1)} %collective-permute-done.2), kind=kOutput, calls=%fused_computation.54 | convolution fusion | flops 679477248 | bytes 1572864 | tf_op jit(solution)/shard_map/dot_general | solution.py:14
  67.8 1.3 %convolution_select_fusion.5 = f32[384,384]{1,0:T(8,128)S(1)} fusion(f32[384,384]{1,0:T(8,128)S(1)} %fusion.39, f32[384,384]{1,0:T(8,128)S(1)} %convolution_select_fusion.6, f32[256,384]{1,0:T(8,128)S(1)} %collective-permute-done.2, pred[]{:T(512)S(6)} %eq.71), kind=kOutput, calls=%fused_computation.14 | convolution fusion | flops 679624704 | bytes 2162689 | tf_op jit(solution)/shard_map/dot_general | solution.py:14
  69.1 1.4 %collective-permute-start.3 = (f32[192,384]{1,0:T(8,128)S(1)}, f32[192,384]{1,0:T(8,128)S(1)}, u32[]{:S(2)}, u32[]{:S(2)}) collective-permute-start(f32[192,384]{1,0:T(8,128)S(1)} %slice.38), channel_id=1, source_target_pairs={{0,32},{4,36},{8,40},{12,44},{16,48},{20,52},{24,56},{28,60},{32,0... | collective-permute-start | bytes 884744 | tf_op jit(solution)/shard_map/ppermute | solution.py:10
  70.5 1.3 %convolution_select_fusion.2 = f32[384,384]{1,0:T(8,128)S(1)} fusion(f32[384,384]{1,0:T(8,128)S(1)} %convolution_select_fusion.3, f32[256,384]{1,0:T(8,128)S(1)} %collective-permute-done.2, pred[]{:T(512)S(6)} %eq.71), kind=kOutput, calls=%fused_computation.9 | convolution fusion | flops 679624704 | bytes 1572865 | tf_op jit(solution)/shard_map/dot_general | solution.py:14
  71.8 0.6 fusion.22
  72.4 13.7 %collective-permute-done.3 = f32[192,384]{1,0:T(8,128)S(1)} collective-permute-done((f32[192,384]{1,0:T(8,128)S(1)}, f32[192,384]{1,0:T(8,128)S(1)}, u32[]{:S(2)}, u32[]{:S(2)}) %collective-permute-start.3) | collective-permute-done | bytes 294944 | tf_op jit(solution)/shard_map/ppermute | solution.py:10
  86.1 0.6 convolution_add_fusion.5
  86.7 0.7 fusion.26
  87.4 1.6 %collective-permute-start.9 = (f32[128,8]{0,1:T(8,128)S(1)}, f32[128,8]{0,1:T(8,128)S(1)}, u32[]{:S(2)}, u32[]{:S(2)}) collective-permute-start(f32[128,8]{0,1:T(8,128)S(1)} %slice.43), channel_id=1, source_target_pairs={{0,64},{4,68},{8,72},{12,76},{16,80},{20,84},{24,88},{28,92},{32,9... | collective-permute-start | bytes 12296 | tf_op jit(solution)/shard_map/ppermute | solution.py:10
  89.0 1.2 %fusion.31 = f32[384,384]{1,0:T(8,128)S(1)} fusion(f32[384,384]{1,0:T(8,128)S(1)} %convolution_select_fusion.5, f32[192,384]{1,0:T(8,128)S(1)} %collective-permute-done.3), kind=kOutput, calls=%fused_computation.46 | convolution fusion | flops 679477248 | bytes 1474560 | tf_op jit(solution)/shard_map/dot_general | solution.py:14
  90.2 1.2 %convolution_select_fusion.4 = f32[384,384]{1,0:T(8,128)S(1)} fusion(f32[384,384]{1,0:T(8,128)S(1)} %fusion.31, f32[384,384]{1,0:T(8,128)S(1)} %convolution_select_fusion.5, f32[192,384]{1,0:T(8,128)S(1)} %collective-permute-done.3, pred[]{:T(512)S(6)} %eq.70), kind=kOutput, calls=%fused_computation.13 | convolution fusion | flops 679624704 | bytes 2064385 | tf_op jit(solution)/shard_map/dot_general | solution.py:14
  91.5 0.6 collective-permute-start.4
  92.1 1.2 %convolution_select_fusion.1 = f32[384,384]{1,0:T(8,128)S(1)} fusion(f32[384,384]{1,0:T(8,128)S(1)} %convolution_select_fusion.2, f32[192,384]{1,0:T(8,128)S(1)} %collective-permute-done.3, pred[]{:T(512)S(6)} %eq.70), kind=kOutput, calls=%fused_computation.8 | convolution fusion | flops 679624704 | bytes 1474561 | tf_op jit(solution)/shard_map/dot_general | solution.py:14
  93.4 0.6 fusion.23
  93.9 0.6 fusion.52
  94.6 3.3 %collective-permute-done.4 = f32[128,384]{1,0:T(8,128)S(1)} collective-permute-done((f32[128,384]{1,0:T(8,128)S(1)}, f32[128,384]{1,0:T(8,128)S(1)}, u32[]{:S(2)}, u32[]{:S(2)}) %collective-permute-start.4) | collective-permute-done | bytes 196640 | tf_op jit(solution)/shard_map/ppermute | solution.py:10
  97.9 0.3 fusion.43
  98.3 2.8 %collective-permute-start.10 = (f32[64,8]{0,1:T(8,128)S(1)}, f32[64,8]{0,1:T(8,128)S(1)}, u32[]{:S(2)}, u32[]{:S(2)}) collective-permute-start(f32[64,8]{0,1:T(8,128)S(1)} %fusion.61), channel_id=1, source_target_pairs={{0,128},{4,132},{8,136},{12,140},{16,144},{20,148},{24,152},{28,15... | collective-permute-start | bytes 6152 | tf_op jit(solution)/shard_map/ppermute | solution.py:10
  101.0 1.2 %convolution_select_fusion = f32[384,384]{1,0:T(8,128)S(1)} fusion(f32[384,384]{1,0:T(8,128)S(1)} %convolution_select_fusion.1, f32[128,384]{1,0:T(8,128)S(1)} %collective-permute-done.4, pred[]{:T(512)S(6)} %eq.69), kind=kOutput, calls=%fused_computation.7 | convolution fusion | flops 679624704 | bytes 1376257 | tf_op jit(solution)/shard_map/dot_general | solution.py:14
  102.3 1.1 %collective-permute-done.10 = f32[64,8]{0,1:T(8,128)S(1)} collective-permute-done((f32[64,8]{0,1:T(8,128)S(1)}, f32[64,8]{0,1:T(8,128)S(1)}, u32[]{:S(2)}, u32[]{:S(2)}) %collective-permute-start.10) | collective-permute-done | bytes 2080 | tf_op jit(solution)/shard_map/ppermute | solution.py:10
  103.4 0.6 fusion.25
  104.0 1.4 %convolution_subtract_fusion = f32[8,2048]{1,0:T(8,128)} fusion(f32[8,2048]{1,0:T(8,128)S(1)} %fusion.99, f32[384,8]{0,1:T(8,128)S(1)} %fusion.25, bf16[384,2048]{1,0:T(8,128)(2,1)S(1)} %convolution_convert_fusion), kind=kOutput, calls=%fused_computation.1 | convolution fusion | flops 75513856 | bytes 1716224 | tf_op jit(solution)/shard_map/ms,sk->km/dot_general | solution.py:70
  (29 shorter events, 1.4 us)
Async XLA Ops:
  0.0 9.6 %copy-start = (bf16[8,2048]{1,0:T(8,128)(2,1)S(1)}, bf16[8,2048]{1,0:T(8,128)(2,1)}, u32[]{:S(2)}) copy-start(bf16[8,2048]{1,0:T(8,128)(2,1)} %param.5) | copy-start | bytes 98308
  0.9 7.5 %copy-start.2 = (bf16[2048,384]{1,0:T(8,128)(2,1)S(1)}, bf16[2048,384]{1,0:T(8,128)(2,1)}, u32[]{:S(2)}) copy-start(bf16[2048,384]{1,0:T(8,128)(2,1)} %param.8) | copy-start | bytes 4718596
  0.9 8.7 %copy-start.1 = (bf16[2048,2048]{1,0:T(8,128)(2,1)S(1)}, bf16[2048,2048]{1,0:T(8,128)(2,1)}, u32[]{:S(2)}) copy-start(bf16[2048,2048]{1,0:T(8,128)(2,1)} %param.6) | copy-start | bytes 25165828
  9.5 4.9 %collective-permute-start = (f32[384,384]{1,0:T(8,128)S(1)}, f32[384,384]{1,0:T(8,128)S(1)}, u32[]{:S(2)}, u32[]{:S(2)}) collective-permute-start(f32[384,384]{1,0:T(8,128)S(1)} %fusion.14), channel_id=1, source_target_pairs={{0,4},{4,0},{8,12},{12,8},{16,20},{20,16},{24,28},{28,24},{32,36},... | collective-permute-start | bytes 1769480 | tf_op jit(solution)/shard_map/ppermute | solution.py:10
  12.8 1.4 %collective-permute-start.5 = (f32[384,8]{0,1:T(8,128)S(1)}, f32[384,8]{0,1:T(8,128)S(1)}, u32[]{:S(2)}, u32[]{:S(2)}) collective-permute-start(f32[384,8]{0,1:T(8,128)S(1)} %fusion.17), channel_id=1, source_target_pairs={{0,4},{4,0},{8,12},{12,8},{16,20},{20,16},{24,28},{28,24},{32,36},... | collective-permute-start | bytes 36872 | tf_op jit(solution)/shard_map/ppermute | solution.py:10
  15.8 5.7 %collective-permute-start.6 = (f32[320,8]{0,1:T(8,128)S(1)}, f32[320,8]{0,1:T(8,128)S(1)}, u32[]{:S(2)}, u32[]{:S(2)}) collective-permute-start(f32[320,8]{0,1:T(8,128)S(1)} %slice.40), channel_id=1, source_target_pairs={{0,8},{4,12},{8,0},{12,4},{16,24},{20,28},{24,16},{28,20},{32,40},... | collective-permute-start | bytes 30728 | tf_op jit(solution)/shard_map/ppermute | solution.py:10
  20.5 13.3 %collective-permute-start.1 = (f32[320,384]{1,0:T(8,128)S(1)}, f32[320,384]{1,0:T(8,128)S(1)}, u32[]{:S(2)}, u32[]{:S(2)}) collective-permute-start(f32[320,384]{1,0:T(8,128)S(1)} %slice.36), channel_id=1, source_target_pairs={{0,8},{4,12},{8,0},{12,4},{16,24},{20,28},{24,16},{28,20},{32,40},... | collective-permute-start | bytes 1474568 | tf_op jit(solution)/shard_map/ppermute | solution.py:10
  35.1 7.3 %collective-permute-start.7 = (f32[256,8]{0,1:T(8,128)S(1)}, f32[256,8]{0,1:T(8,128)S(1)}, u32[]{:S(2)}, u32[]{:S(2)}) collective-permute-start(f32[256,8]{0,1:T(8,128)S(1)} %slice.41), channel_id=1, source_target_pairs={{0,16},{4,20},{8,24},{12,28},{16,0},{20,4},{24,8},{28,12},{32,48},... | collective-permute-start | bytes 24584 | tf_op jit(solution)/shard_map/ppermute | solution.py:10
  41.1 19.3 %collective-permute-start.2 = (f32[256,384]{1,0:T(8,128)S(1)}, f32[256,384]{1,0:T(8,128)S(1)}, u32[]{:S(2)}, u32[]{:S(2)}) collective-permute-start(f32[256,384]{1,0:T(8,128)S(1)} %slice.37), channel_id=1, source_target_pairs={{0,16},{4,20},{8,24},{12,28},{16,0},{20,4},{24,8},{28,12},{32,48},... | collective-permute-start | bytes 1179656 | tf_op jit(solution)/shard_map/ppermute | solution.py:10
  61.7 10.1 %collective-permute-start.8 = (f32[192,8]{0,1:T(8,128)S(1)}, f32[192,8]{0,1:T(8,128)S(1)}, u32[]{:S(2)}, u32[]{:S(2)}) collective-permute-start(f32[192,8]{0,1:T(8,128)S(1)} %slice.42), channel_id=1, source_target_pairs={{0,32},{4,36},{8,40},{12,44},{16,48},{20,52},{24,56},{28,60},{32,0... | collective-permute-start | bytes 18440 | tf_op jit(solution)/shard_map/ppermute | solution.py:10
  69.1 17.0 %collective-permute-start.3 = (f32[192,384]{1,0:T(8,128)S(1)}, f32[192,384]{1,0:T(8,128)S(1)}, u32[]{:S(2)}, u32[]{:S(2)}) collective-permute-start(f32[192,384]{1,0:T(8,128)S(1)} %slice.38), channel_id=1, source_target_pairs={{0,32},{4,36},{8,40},{12,44},{16,48},{20,52},{24,56},{28,60},{32,0... | collective-permute-start | bytes 884744 | tf_op jit(solution)/shard_map/ppermute | solution.py:10
  87.4 6.0 %collective-permute-start.9 = (f32[128,8]{0,1:T(8,128)S(1)}, f32[128,8]{0,1:T(8,128)S(1)}, u32[]{:S(2)}, u32[]{:S(2)}) collective-permute-start(f32[128,8]{0,1:T(8,128)S(1)} %slice.43), channel_id=1, source_target_pairs={{0,64},{4,68},{8,72},{12,76},{16,80},{20,84},{24,88},{28,92},{32,9... | collective-permute-start | bytes 12296 | tf_op jit(solution)/shard_map/ppermute | solution.py:10
  91.5 6.4 %collective-permute-start.4 = (f32[128,384]{1,0:T(8,128)S(1)}, f32[128,384]{1,0:T(8,128)S(1)}, u32[]{:S(2)}, u32[]{:S(2)}) collective-permute-start(f32[128,384]{1,0:T(8,128)S(1)} %slice.39), channel_id=1, source_target_pairs={{0,64},{4,68},{8,72},{12,76},{16,80},{20,84},{24,88},{28,92},{32,9... | collective-permute-start | bytes 589832 | tf_op jit(solution)/shard_map/ppermute | solution.py:10
  98.3 5.1 %collective-permute-start.10 = (f32[64,8]{0,1:T(8,128)S(1)}, f32[64,8]{0,1:T(8,128)S(1)}, u32[]{:S(2)}, u32[]{:S(2)}) collective-permute-start(f32[64,8]{0,1:T(8,128)S(1)} %fusion.61), channel_id=1, source_target_pairs={{0,128},{4,132},{8,136},{12,140},{16,144},{20,148},{24,152},{28,15... | collective-permute-start | bytes 6152 | tf_op jit(solution)/shard_map/ppermute | solution.py:10
where the time goes:
time: 106 us; the launch traced here: 105 us
  waiting for transfers between devices  47.9 us (45%)
  matrix products  38 us (36%)
  starting transfers between devices  17.7 us (17%)
  other arithmetic  1.1 us (1%)
    ppermute x11, waiting for transfers between devices, swapped(): lax.ppermute(x, axis, [(i, i ^ 1 << distance) for i in range(lax.axis_siz...  47.9 us
    ppermute x11, starting transfers between devices, swapped(): lax.ppermute(x, axis, [(i, i ^ 1 << distance) for i in range(lax.axis_siz...  17.7 us
    dot_general x13, matrix products, compose(): joined_map = jnp.dot(latter[0], former[0], precision=best_precision)  15.8 us
    dot_general x16, matrix products, compose(): jnp.dot(latter[0], former[1], precision=best_precision) + latter[1]  9.22 us
    dot_general x1, matrix products, on_device(): jnp.dot(diag_inverse, left_kept, preferred_element_type=jnp.float32)  7.48 us
    dot_general x1, matrix products, on_device(): jnp.einsum('km,nm->kn', rhs_vectors, diag_inverse, preferred_element_type...  2.26 us
  transfers between devices with their start and end apart: 11, of which 6 were waited for; matrix products, arithmetic and copies ran while one was open for 21% of the time, Pallas kernels for 0%

commit v1 on v0

v1 whole, which is shorter than its diff:
```python
import jax
import jax.numpy as jnp
from jax import lax
from jax.experimental import pallas as pl
from jax.experimental.pallas import tpu as pltpu
from jax.sharding import PartitionSpec as P

f32 = jnp.float32
bf16 = jnp.bfloat16
NN = (((1,), (0,)), ((), ()))
NT = (((1,), (1,)), ((), ()))
RANK = 64
LEVELS = 6
STATE = RANK * LEVELS
CHUNK = 512
PARTNER = (1, 2, 4, 12, 16, 48)


def mul(a, b, dims=NN):
    return lax.dot_general(a, b, dims, preferred_element_type=f32)


def halves(x):
    high = x.astype(bf16)
    return high, (x - high.astype(f32)).astype(bf16)


def thirds(x):
    high, low = halves(x)
    rest = x - high.astype(f32) - low.astype(f32)
    return high, low, rest.astype(bf16)


def wide_mul(a, b):
    a_high, a_low = halves(a)
    b_high, b_low = halves(b)
    return mul(
        jnp.concatenate([a_high, a_high, a_low], axis=1),
        jnp.concatenate([b_high, b_low, b_high], axis=0),
    )


def upper(level):
    return (lax.axis_index("leaf") >> level & 1) == 1


def side_by_side(x, blocks):
    return jnp.concatenate([x[RANK * j : RANK * (j + 1)] for j in range(blocks)], axis=1)


def stacked(x, blocks):
    return jnp.concatenate([x[:, RANK * j : RANK * (j + 1)] for j in range(blocks)], axis=0)


def outgoing(level, state, send):
    blocks = LEVELS - 1 - level
    is_upper = upper(level)
    if level == LEVELS - 1:
        send[...] = jnp.concatenate([state[RANK:, RANK : 2 * RANK]] * 2, axis=1)
    elif level % 2 == 0:
        pivot = state[:RANK, RANK:]
        packed = jnp.concatenate([stacked(pivot, blocks), state[RANK * (blocks + 1) :, :RANK]], axis=0)
        first = jnp.where(is_upper, packed, state[RANK:, :RANK])
        send[:, : 2 * RANK] = jnp.concatenate([first, state[RANK:, RANK : 2 * RANK]], axis=1)
        if blocks > 1:
            send[:, 2 * RANK :] = state[RANK:, 2 * RANK :]
    else:
        rows = RANK * blocks + 8
        send[:rows] = state[RANK:, 2 * RANK :]
        left = state[RANK:, RANK : 2 * RANK]
        packed = side_by_side(left, blocks)
        send[rows : rows + RANK] = jnp.where(is_upper, state[:RANK, 2 * RANK :], packed)
        send[rows + RANK :] = jnp.concatenate([left[RANK * blocks :]] * blocks, axis=1)


def pivots(level, got):
    blocks = LEVELS - 1 - level
    if level % 2 == 0:
        return got[:, :RANK]
    rows = RANK * blocks + 8
    return jnp.concatenate([stacked(got[rows : rows + RANK], blocks), got[rows + RANK :, :RANK]], axis=0)


def first_kernel(ranks, b_hbm, d_hbm, u_hbm, v_hbm, mapped, base, state, send, d, u, v, b, x, acc, sems):
    size = d.shape[0]
    n = size // CHUNK
    copies = [
        pltpu.make_async_copy(d_hbm.at[pl.ds(CHUNK * i, CHUNK)], d.at[pl.ds(CHUNK * i, CHUNK)], sems.at[i])
        for i in range(n)
    ]
    copy_u = pltpu.make_async_copy(u_hbm, u, sems.at[n])
    copy_b = pltpu.make_async_copy(b_hbm, b, sems.at[n + 1])
    copy_v = pltpu.make_async_copy(v_hbm, v, sems.at[n + 2])
    copy_u.start()
    copy_b.start()
    copies[0].start()
    copy_v.start()
    for c in copies[1:]:
        c.start()
    lane = lax.broadcasted_iota(jnp.int32, (1, STATE), 1)
    keep = jnp.zeros((1, STATE), f32)
    for level in range(LEVELS):
        inside = (lane >= RANK * level) & (lane < RANK * level + jnp.minimum(ranks[level], RANK))
        keep = jnp.where(inside, 1.0, keep)
    copy_u.wait()
    copy_b.wait()
    x[:STATE] = (u[...] * keep.astype(bf16)).T
    x[STATE:] = jnp.concatenate([b[...], jnp.zeros((8, size), bf16)], axis=0)
    for i in range(n):
        rows = slice(CHUNK * i, CHUNK * (i + 1))
        copies[i].wait()
        if i == 0:
            copy_v.wait()
        product = mul(x[...], d[rows], NT)
        rounded = product[:STATE].astype(bf16)
        mapped[:, rows] = rounded
        part = product[STATE : STATE + 8]
        base[:, rows] = part
        joined = jnp.concatenate([rounded, *thirds(part)], axis=0)
        total = mul(joined, v[rows])
        if i == 0:
            acc[...] = total
        else:
            acc[...] += total
    state[:STATE] = acc[:STATE] * keep
    state[STATE:] = (acc[STATE : STATE + 8] + acc[STATE + 8 : STATE + 16] + acc[STATE + 16 :]) * keep
    outgoing(0, state[...], send)


def level_kernel(level, own, got, state, send):
    blocks = LEVELS - 1 - level
    is_upper = upper(level)
    skip = RANK if level % 2 else 0
    first = 2 * skip
    own_left = own[RANK:, skip : skip + RANK]
    own_right = own[:RANK, first:]
    arrived = got[...]
    left = jnp.where(is_upper, pivots(level, arrived), own_left)
    if level % 2 == 0:
        bulk = arrived
        right = jnp.concatenate([own_right[:, :RANK], side_by_side(arrived[:, :RANK], blocks)], axis=1)
    else:
        rows = RANK * blocks + 8
        bulk = arrived[:rows]
        right = arrived[rows : rows + RANK]
    right = jnp.where(is_upper, own_right, right)
    state[...] = own[RANK:, first:] + bulk - wide_mul(left, right)
    outgoing(level + 1, state[...], send)


def coefficients(level, got, t):
    blocks = LEVELS - 1 - level
    left = jnp.where(upper(level), pivots(level, got), 0.0)
    done = -left
    if t is None:
        return done
    done = jnp.concatenate([t[RANK:] - wide_mul(left, t[:RANK]), done], axis=1)
    return done


def coefficient_kernel(levels, *refs):
    count = len(levels)
    t = refs[count][...] if len(refs) == count + 2 else None
    for level, got in zip(levels, refs):
        t = coefficients(level, got[...], t)
    refs[-1][...] = t


def basis_kernel(got, t_ref, mapped, base, out):
    t = coefficients(3, got[...], t_ref[...])
    w = mapped[...]
    high, low = halves(t)
    rows = t.shape[0]
    product = mul(jnp.concatenate([high, low], axis=0), w[: t.shape[1]])
    product = product[:rows] + product[rows:]
    out[: 2 * RANK] = w[4 * RANK :].astype(f32) + product[: 2 * RANK]
    out[2 * RANK :] = base[...] + product[2 * RANK :]


def late_kernel(got, basis, high_low, shifted):
    left = jnp.where(upper(4), pivots(4, got[...]), 0.0)
    update = basis[RANK:] - wide_mul(left, basis[:RANK])
    high, low = halves(update[:RANK])
    high_low[:RANK] = high
    high_low[RANK : 2 * RANK] = low
    high_low[2 * RANK :] = high
    shifted[...] = update[RANK:]


def last_kernel(got, high_low, shifted, out):
    value = jnp.where(upper(5), got[:, :RANK], 0.0)
    high, low = halves(value)
    out[...] = shifted[...] - mul(jnp.concatenate([high, high, low], axis=1), high_low[...])


def send_shape(level):
    blocks = LEVELS - 1 - level
    if level == LEVELS - 1:
        return (8, 2 * RANK)
    if level % 2 == 0:
        return (RANK * blocks + 8, RANK * (blocks + 1))
    return (RANK * (blocks + 1) + 16, RANK * blocks)


def state_shape(level):
    return (RANK * (LEVELS - level) + 8, STATE - 2 * RANK * (level // 2))


def call(kernel, name, outs, *args):
    vmem = pl.BlockSpec(memory_space=pltpu.VMEM)
    return pl.pallas_call(
        kernel,
        name=name,
        in_specs=[vmem] * len(args),
        out_specs=[vmem] * len(outs),
        out_shape=[jax.ShapeDtypeStruct(s, t) for s, t in outs],
    )(*args)


def on_device(rhs_vectors, diag_inverse, left_factors, right_factors, ranks):
    size = diag_inverse.shape[0]
    vmem = pl.BlockSpec(memory_space=pltpu.VMEM)
    hbm = pl.BlockSpec(memory_space=pl.ANY)
    mapped, base, state, send = pl.pallas_call(
        first_kernel,
        name="first",
        in_specs=[pl.BlockSpec(memory_space=pltpu.SMEM), hbm, hbm, hbm, hbm],
        out_specs=[vmem] * 4,
        out_shape=[
            jax.ShapeDtypeStruct((STATE, size), bf16),
            jax.ShapeDtypeStruct((8, size), f32),
            jax.ShapeDtypeStruct(state_shape(0), f32),
            jax.ShapeDtypeStruct(send_shape(0), f32),
        ],
        scratch_shapes=[
            pltpu.VMEM((size, size), bf16),
            pltpu.VMEM((size, STATE), bf16),
            pltpu.VMEM((size, STATE), bf16),
            pltpu.VMEM((8, size), bf16),
            pltpu.VMEM((STATE + 16, size), bf16),
            pltpu.VMEM((STATE + 24, STATE), f32),
            pltpu.SemaphoreType.DMA((size // CHUNK + 3,)),
        ],
    )(ranks, rhs_vectors, diag_inverse, left_factors, right_factors)
    got = []
    t = None
    for level in range(LEVELS):
        pairs = [(i, i ^ PARTNER[level]) for i in range(lax.axis_size("leaf"))]
        got.append(lax.ppermute(send, "leaf", pairs))
        if level < LEVELS - 1:
            state, send = call(
                lambda *refs, level=level: level_kernel(level, *refs),
                f"level_{level}",
                [(state_shape(level + 1), f32), (send_shape(level + 1), f32)],
                state,
                got[level],
            )
    (t,) = call(
        lambda *refs: coefficient_kernel((0, 1, 2), *refs),
        "coefficients",
        [((3 * RANK + 8, 3 * RANK), f32)],
        *got[:3],
    )
    (basis,) = call(basis_kernel, "basis", [((2 * RANK + 8, size), f32)], got[3], t, mapped, base)
    high_low, shifted = call(late_kernel, "late", [((3 * RANK, size), bf16), ((8, size), f32)], got[4], basis)
    (out,) = call(last_kernel, "last", [((8, size), f32)], got[5], high_low, shifted)
    return out


def solution(mesh):
    in_specs = (P("rhs", "leaf"), P("leaf", None), P("leaf", None), P("leaf", None), P())
    out_specs = P("rhs", "leaf")
    return jax.shard_map(
        on_device, mesh=mesh, in_specs=in_specs, out_specs=out_specs, check_vma=False
    )
```

time: 106 us -> 75.6 us (0.71)
  the two profiles are of different devices: /device:TPU:8 before, /device:TPU:32 now
where the time goes in v1:
time: 75.6 us; the launch traced here: 75.1 us
  Pallas kernels  30.4 us (40%)
  waiting for transfers between devices  27.8 us (37%)
  starting transfers between devices  12.8 us (17%)
  local copies, waits for them, and re-layouts  4.03 us (5%)
    ppermute x6, waiting for transfers between devices, on_device(): got.append(lax.ppermute(send, 'leaf', pairs))  27.8 us
    pallas_call x9, Pallas kernels, call(): pl.pallas_call(kernel, name=name, in_specs=[vmem] * len(args), out_specs=...  20.7 us
    ppermute x6, starting transfers between devices, on_device(): got.append(lax.ppermute(send, 'leaf', pairs))  12.8 us
    pallas_call x1, Pallas kernels, on_device(): pl.pallas_call(first_kernel, name='first', in_specs=[pl.BlockSpec(memory_...  9.69 us
    unnamed x12, local copies, waits for them, and re-layouts  4.03 us
  transfers between devices with their start and end apart: 6, of which 5 were waited for; matrix products, arithmetic and copies ran while one was open for 0% of the time, Pallas kernels for 11%

profile of v1, /device:TPU:32, one launch (start us, length us, event | category | flops | bytes accessed | tf_op | source)
XLA Modules:
  0.0 75.1 jit_solution(305645133102357935)
XLA Ops:
  0.0 9.7 %first.1 = (bf16[384,2048]{1,0:T(8,128)(2,1)}, f32[8,2048]{1,0:T(8,128)}, f32[392,384]{1,0:T(8,128)}, f32[328,384]{1,0:T(8,128)}) custom-call(s32[6]{0:T(128)} %ranks.1, bf16[8,2048]{1,0:T(8,128)(2,1)} %b_hbm.1, bf16[2048,2048]{1,0:T(8,128)(2,1)} %d_hbm.1, bf16[2048,384]{1,0:T(8,128)(2,1)} %u_hbm.1, bf16[2048,384]{1,0:T(8,128)(2,1)} %v_hbm.1), custom_call_target="tpu_custom_call" | custom-call | tf_op jit(solution)/shard_map/first/pallas_call | solution.py:224
  9.7 0.1 collective-permute-start
  9.8 2.1 %collective-permute-done.refs_1_.refs_0_ = f32[328,384]{1,0:T(8,128)S(1)} collective-permute-done((f32[328,384]{1,0:T(8,128)}, f32[328,384]{1,0:T(8,128)S(1)}, u32[]{:S(2)}, u32[]{:S(2)}) %collective-permute-start) | collective-permute-done | bytes 503840 | tf_op jit(solution)/shard_map/ppermute | solution.py:249
  11.9 0.0 copy-start
  11.9 0.8 %copy-done = f32[328,384]{1,0:T(8,128)} copy-done((f32[328,384]{1,0:T(8,128)}, f32[328,384]{1,0:T(8,128)S(1)}, u32[]{:S(2)}) %copy-start) | copy-done | bytes 503832
  12.7 2.5 %level_0.1 = (f32[328,384]{1,0:T(8,128)}, f32[336,256]{1,0:T(8,128)}) custom-call(f32[392,384]{1,0:T(8,128)} %get-tuple-element.20.refs_0_, f32[328,384]{1,0:T(8,128)} %copy-done), custom_call_target="tpu_custom_call" | custom-call | tf_op jit(solution)/shard_map/level_0/pallas_call | solution.py:211
  15.2 1.8 %collective-permute-start.1 = (f32[336,256]{1,0:T(8,128)}, f32[336,256]{1,0:T(8,128)S(1)}, u32[]{:S(2)}, u32[]{:S(2)}) collective-permute-start(f32[336,256]{1,0:T(8,128)} %get-tuple-element.23), channel_id=1, source_target_pairs={{0,8},{4,12},{8,0},{12,4},{16,24},{20,28},{24,16},{28,20},{32,40},... | collective-permute-start | bytes 1032200 | tf_op jit(solution)/shard_map/ppermute | solution.py:249
  17.0 8.6 %collective-permute-done.1.refs_1_ = f32[336,256]{1,0:T(8,128)S(1)} collective-permute-done((f32[336,256]{1,0:T(8,128)}, f32[336,256]{1,0:T(8,128)S(1)}, u32[]{:S(2)}, u32[]{:S(2)}) %collective-permute-start.1) | collective-permute-done | bytes 344096 | tf_op jit(solution)/shard_map/ppermute | solution.py:249
  25.6 0.0 copy-start.1
  25.6 0.7 copy-done.1
  26.3 2.3 %level_1.1 = (f32[264,256]{1,0:T(8,128)}, f32[200,256]{1,0:T(8,128)}) custom-call(f32[328,384]{1,0:T(8,128)} %get-tuple-element.22.refs_0_, f32[336,256]{1,0:T(8,128)} %copy-done.1), custom_call_target="tpu_custom_call" | custom-call | tf_op jit(solution)/shard_map/level_1/pallas_call | solution.py:211
  28.6 3.2 %collective-permute-start.2 = (f32[200,256]{1,0:T(8,128)}, f32[200,256]{1,0:T(8,128)S(1)}, u32[]{:S(2)}, u32[]{:S(2)}) collective-permute-start(f32[200,256]{1,0:T(8,128)} %get-tuple-element.25), channel_id=1, source_target_pairs={{0,16},{4,20},{8,24},{12,28},{16,0},{20,4},{24,8},{28,12},{32,48},... | collective-permute-start | bytes 614408 | tf_op jit(solution)/shard_map/ppermute | solution.py:249
  31.8 8.4 %collective-permute-done.2.refs_1_.refs_2_ = f32[200,256]{1,0:T(8,128)S(1)} collective-permute-done((f32[200,256]{1,0:T(8,128)}, f32[200,256]{1,0:T(8,128)S(1)}, u32[]{:S(2)}, u32[]{:S(2)}) %collective-permute-start.2) | collective-permute-done | bytes 204832 | tf_op jit(solution)/shard_map/ppermute | solution.py:249
  40.1 0.0 copy-start.2
  40.1 0.7 copy-done.2
  40.8 2.1 %level_2.1 = (f32[200,256]{1,0:T(8,128)}, f32[208,128]{1,0:T(8,128)}) custom-call(f32[264,256]{1,0:T(8,128)} %get-tuple-element.24.refs_0_, f32[200,256]{1,0:T(8,128)} %copy-done.2), custom_call_target="tpu_custom_call" | custom-call | tf_op jit(solution)/shard_map/level_2/pallas_call | solution.py:211
  42.9 5.5 %collective-permute-start.3 = (f32[208,128]{1,0:T(8,128)}, f32[208,128]{1,0:T(8,128)S(1)}, u32[]{:S(2)}, u32[]{:S(2)}) collective-permute-start(f32[208,128]{1,0:T(8,128)} %get-tuple-element.27), channel_id=1, source_target_pairs={{0,48},{4,52},{8,56},{12,60},{16,32},{20,36},{24,40},{28,44},{32,1... | collective-permute-start | bytes 319496 | tf_op jit(solution)/shard_map/ppermute | solution.py:249
  48.4 5.1 %collective-permute-done.3.refs_1_.got = f32[208,128]{1,0:T(8,128)S(1)} collective-permute-done((f32[208,128]{1,0:T(8,128)}, f32[208,128]{1,0:T(8,128)S(1)}, u32[]{:S(2)}, u32[]{:S(2)}) %collective-permute-start.3) | collective-permute-done | bytes 106528 | tf_op jit(solution)/shard_map/ppermute | solution.py:249
  53.5 0.0 copy-start.3
  53.5 0.6 copy-done.3
  54.1 2.0 %level_3.1 = (f32[136,128]{1,0:T(8,128)}, f32[72,128]{1,0:T(8,128)}) custom-call(f32[200,256]{1,0:T(8,128)} %get-tuple-element.26.refs_0_, f32[208,128]{1,0:T(8,128)} %copy-done.3), custom_call_target="tpu_custom_call" | custom-call | tf_op jit(solution)/shard_map/level_3/pallas_call | solution.py:211
  56.2 0.4 collective-permute-start.4
  56.6 3.7 %collective-permute-done.4.refs_1_.got = f32[72,128]{1,0:T(8,128)S(1)} collective-permute-done((f32[72,128]{1,0:T(8,128)}, f32[72,128]{1,0:T(8,128)S(1)}, u32[]{:S(2)}, u32[]{:S(2)}) %collective-permute-start.4) | collective-permute-done | bytes 36896 | tf_op jit(solution)/shard_map/ppermute | solution.py:249
  60.3 0.0 copy-start.4
  60.3 0.6 copy-done.4
  60.9 1.8 %level_4.1 = (f32[72,128]{1,0:T(8,128)}, f32[8,128]{1,0:T(8,128)}) custom-call(f32[136,128]{1,0:T(8,128)} %get-tuple-element.28.refs_0_, f32[72,128]{1,0:T(8,128)} %copy-done.4), custom_call_target="tpu_custom_call" | custom-call | tf_op jit(solution)/shard_map/level_4/pallas_call | solution.py:211
  62.7 1.8 %collective-permute-start.5 = (f32[8,128]{1,0:T(8,128)}, f32[8,128]{1,0:T(8,128)S(1)}, u32[]{:S(2)}, u32[]{:S(2)}) collective-permute-start(f32[8,128]{1,0:T(8,128)} %get-tuple-element.30), channel_id=1, source_target_pairs={{0,192},{4,196},{8,200},{12,204},{16,208},{20,212},{24,216},{28,22... | collective-permute-start | bytes 12296 | tf_op jit(solution)/shard_map/ppermute | solution.py:249
  64.5 2.3 %coefficients.1.t_ref = f32[200,192]{1,0:T(8,128)} custom-call(f32[328,384]{1,0:T(8,128)} %copy-done, f32[336,256]{1,0:T(8,128)} %copy-done.1, f32[200,256]{1,0:T(8,128)} %copy-done.2), custom_call_target="tpu_custom_call" | custom-call | tf_op jit(solution)/shard_map/coefficients/pallas_call | solution.py:211
  66.7 3.2 %basis.1 = f32[136,2048]{1,0:T(8,128)} custom-call(f32[208,128]{1,0:T(8,128)} %copy-done.3, f32[200,192]{1,0:T(8,128)} %coefficients.1.t_ref, bf16[384,2048]{1,0:T(8,128)(2,1)} %get-tuple-element.31.mapped, f32[8,2048]{1,0:T(8,128)} %get-tuple-element.32.base), custom_call_target="tpu_custom_call" | custom-call | tf_op jit(solution)/shard_map/basis/pallas_call | solution.py:211
  70.0 2.5 %late.1 = (bf16[192,2048]{1,0:T(8,128)(2,1)}, f32[8,2048]{1,0:T(8,128)}) custom-call(f32[72,128]{1,0:T(8,128)} %copy-done.4, f32[136,2048]{1,0:T(8,128)} %basis.1), custom_call_target="tpu_custom_call" | custom-call | tf_op jit(solution)/shard_map/late/pallas_call | solution.py:211
  72.5 0.0 collective-permute-done.5.got
  72.5 0.0 copy-start.5
  72.5 0.6 copy-done.5
  73.1 2.0 %last.1 = f32[8,2048]{1,0:T(8,128)} custom-call(f32[8,128]{1,0:T(8,128)} %copy-done.5, bf16[192,2048]{1,0:T(8,128)(2,1)} %get-tuple-element.33.high_low, f32[8,2048]{1,0:T(8,128)} %get-tuple-element.34.shifted), custom_call_target="tpu_custom_call" | custom-call | tf_op jit(solution)/shard_map/last/pallas_call | solution.py:211
Async XLA Ops:
  9.7 2.2 %collective-permute-start = (f32[328,384]{1,0:T(8,128)}, f32[328,384]{1,0:T(8,128)S(1)}, u32[]{:S(2)}, u32[]{:S(2)}) collective-permute-start(f32[328,384]{1,0:T(8,128)} %get-tuple-element.21), channel_id=1, source_target_pairs={{0,4},{4,0},{8,12},{12,8},{16,20},{20,16},{24,28},{28,24},{32,36},... | collective-permute-start | bytes 1511432 | tf_op jit(solution)/shard_map/ppermute | solution.py:249
  11.9 0.8 %copy-start = (f32[328,384]{1,0:T(8,128)}, f32[328,384]{1,0:T(8,128)S(1)}, u32[]{:S(2)}) copy-start(f32[328,384]{1,0:T(8,128)S(1)} %collective-permute-done.refs_1_.refs_0_) | copy-start | bytes 1511428
  15.2 10.4 %collective-permute-start.1 = (f32[336,256]{1,0:T(8,128)}, f32[336,256]{1,0:T(8,128)S(1)}, u32[]{:S(2)}, u32[]{:S(2)}) collective-permute-start(f32[336,256]{1,0:T(8,128)} %get-tuple-element.23), channel_id=1, source_target_pairs={{0,8},{4,12},{8,0},{12,4},{16,24},{20,28},{24,16},{28,20},{32,40},... | collective-permute-start | bytes 1032200 | tf_op jit(solution)/shard_map/ppermute | solution.py:249
  25.6 0.7 copy-start.1
  28.6 11.6 %collective-permute-start.2 = (f32[200,256]{1,0:T(8,128)}, f32[200,256]{1,0:T(8,128)S(1)}, u32[]{:S(2)}, u32[]{:S(2)}) collective-permute-start(f32[200,256]{1,0:T(8,128)} %get-tuple-element.25), channel_id=1, source_target_pairs={{0,16},{4,20},{8,24},{12,28},{16,0},{20,4},{24,8},{28,12},{32,48},... | collective-permute-start | bytes 614408 | tf_op jit(solution)/shard_map/ppermute | solution.py:249
  40.1 0.7 copy-start.2
  42.9 10.6 %collective-permute-start.3 = (f32[208,128]{1,0:T(8,128)}, f32[208,128]{1,0:T(8,128)S(1)}, u32[]{:S(2)}, u32[]{:S(2)}) collective-permute-start(f32[208,128]{1,0:T(8,128)} %get-tuple-element.27), channel_id=1, source_target_pairs={{0,48},{4,52},{8,56},{12,60},{16,32},{20,36},{24,40},{28,44},{32,1... | collective-permute-start | bytes 319496 | tf_op jit(solution)/shard_map/ppermute | solution.py:249
  53.5 0.6 copy-start.3
  56.2 4.2 %collective-permute-start.4 = (f32[72,128]{1,0:T(8,128)}, f32[72,128]{1,0:T(8,128)S(1)}, u32[]{:S(2)}, u32[]{:S(2)}) collective-permute-start(f32[72,128]{1,0:T(8,128)} %get-tuple-element.29), channel_id=1, source_target_pairs={{0,64},{4,68},{8,72},{12,76},{16,80},{20,84},{24,88},{28,92},{32,9... | collective-permute-start | bytes 110600 | tf_op jit(solution)/shard_map/ppermute | solution.py:249
  60.3 0.6 copy-start.4
  62.7 9.8 %collective-permute-start.5 = (f32[8,128]{1,0:T(8,128)}, f32[8,128]{1,0:T(8,128)S(1)}, u32[]{:S(2)}, u32[]{:S(2)}) collective-permute-start(f32[8,128]{1,0:T(8,128)} %get-tuple-element.30), channel_id=1, source_target_pairs={{0,192},{4,196},{8,200},{12,204},{16,208},{20,212},{24,216},{28,22... | collective-permute-start | bytes 12296 | tf_op jit(solution)/shard_map/ppermute | solution.py:249
  72.5 0.6 copy-start.5

commit v2 on v1

--- a/solution.py
+++ b/solution.py
@@ -127,7 +127,8 @@
     outgoing(0, state[...], send)
 
 
-def level_kernel(level, own, got, state, send):
+def level_kernel(level, own, got, *refs):
+    send = refs[-1]
     blocks = LEVELS - 1 - level
     is_upper = upper(level)
     skip = RANK if level % 2 else 0
@@ -144,8 +145,10 @@
         bulk = arrived[:rows]
         right = arrived[rows : rows + RANK]
     right = jnp.where(is_upper, own_right, right)
-    state[...] = own[RANK:, first:] + bulk - wide_mul(left, right)
-    outgoing(level + 1, state[...], send)
+    total = own[RANK:, first:] + bulk - wide_mul(left, right)
+    if level < LEVELS - 2:
+        refs[-2][...] = total
+    outgoing(level + 1, total, send)
 
 
 def coefficients(level, got, t):
@@ -206,21 +209,27 @@
     return (RANK * (LEVELS - level) + 8, STATE - 2 * RANK * (level // 2))
 
 
-def call(kernel, name, outs, *args):
+def call(kernel, name, outs, *args, after=()):
     vmem = pl.BlockSpec(memory_space=pltpu.VMEM)
+    count = len(args)
+
+    def body(*refs):
+        kernel(*refs[:count], *refs[count + len(after) :])
+
     return pl.pallas_call(
-        kernel,
+        body,
         name=name,
-        in_specs=[vmem] * len(args),
+        in_specs=[vmem] * count + [pl.BlockSpec(memory_space=pl.ANY)] * len(after),
         out_specs=[vmem] * len(outs),
         out_shape=[jax.ShapeDtypeStruct(s, t) for s, t in outs],
-    )(*args)
+        compiler_params=pltpu.CompilerParams(vmem_limit_bytes=16 << 20),
+    )(*args, *after)
 
 
 def on_device(rhs_vectors, diag_inverse, left_factors, right_factors, ranks):
     size = diag_inverse.shape[0]
     vmem = pl.BlockSpec(memory_space=pltpu.VMEM)
-    hbm = pl.BlockSpec(memory_space=pl.ANY)
+    hbm = pl.BlockSpec(memory_space=pltpu.HBM)
     mapped, base, state, send = pl.pallas_call(
         first_kernel,
         name="first",
@@ -241,27 +250,42 @@
             pltpu.VMEM((STATE + 24, STATE), f32),
             pltpu.SemaphoreType.DMA((size // CHUNK + 3,)),
         ],
-    )(ranks, rhs_vectors, diag_inverse, left_factors, right_factors)
+        compiler_params=pltpu.CompilerParams(vmem_limit_bytes=40 << 20),
+    )(
+        *(
+            pltpu.with_memory_space_constraint(a, pltpu.HBM)
+            for a in (ranks, rhs_vectors, diag_inverse, left_factors, right_factors)
+        ),
+    )
     got = []
-    t = None
     for level in range(LEVELS):
         pairs = [(i, i ^ PARTNER[level]) for i in range(lax.axis_size("leaf"))]
         got.append(lax.ppermute(send, "leaf", pairs))
+        after = ()
+        if level == 3:
+            (t,) = after = call(
+                lambda *refs: coefficient_kernel((0, 1, 2), *refs),
+                "coefficients",
+                [((3 * RANK + 8, 3 * RANK), f32)],
+                *got[:3],
+            )
+        if level == 4:
+            (basis,) = after = call(
+                basis_kernel, "basis", [((2 * RANK + 8, size), f32)], got[3], t, mapped, base
+            )
         if level < LEVELS - 1:
-            state, send = call(
+            outs = [(send_shape(level + 1), f32)]
+            if level < LEVELS - 2:
+                outs.insert(0, (state_shape(level + 1), f32))
+            *states, send = call(
                 lambda *refs, level=level: level_kernel(level, *refs),
                 f"level_{level}",
-                [(state_shape(level + 1), f32), (send_shape(level + 1), f32)],
+                outs,
                 state,
                 got[level],
+                after=after,
             )
-    (t,) = call(
-        lambda *refs: coefficient_kernel((0, 1, 2), *refs),
-        "coefficients",
-        [((3 * RANK + 8, 3 * RANK), f32)],
-        *got[:3],
-    )
-    (basis,) = call(basis_kernel, "basis", [((2 * RANK + 8, size), f32)], got[3], t, mapped, base)
+            state = states[0] if states else None
     high_low, shifted = call(late_kernel, "late", [((3 * RANK, size), bf16), ((8, size), f32)], got[4], basis)
     (out,) = call(last_kernel, "last", [((8, size), f32)], got[5], high_low, shifted)
     return out

time: 75.6 us -> 54.5 us (0.72)
  Pallas kernels: 30.4 us -> 12.7 us
  local copies, waits for them, and re-layouts: 4.03 us -> 0 us
    pallas_call x9, Pallas kernels: 20.7 us -> 4.16 us  [call(): pl.pallas_call(body, name=name, in_specs=[vmem] * count + [pl.BlockSpec(m...]
    unnamed x12 -> x0, local copies, waits for them, and re-layouts: 4.03 us -> none
    pallas_call x1, Pallas kernels: 9.69 us -> 8.55 us  [on_device(): pl.pallas_call(first_kernel, name='first', in_specs=[pl.BlockSpec(memory_...]
  transfers between devices with their start and end apart: 6 -> 6, of which waited for: 5 -> 6; matrix products, arithmetic and copies ran while one was open for 0% -> 0% of each run, Pallas kernels for 11% -> 3%
where the time goes in v2:
time: 54.5 us; the launch traced here: 54.4 us
  waiting for transfers between devices  28.2 us (52%)
  starting transfers between devices  13.5 us (25%)
  Pallas kernels  12.7 us (23%)
    ppermute x6, waiting for transfers between devices, on_device(): got.append(lax.ppermute(send, 'leaf', pairs))  28.2 us
    ppermute x6, starting transfers between devices, on_device(): got.append(lax.ppermute(send, 'leaf', pairs))  13.5 us
    pallas_call x1, Pallas kernels, on_device(): pl.pallas_call(first_kernel, name='first', in_specs=[pl.BlockSpec(memory_...  8.55 us
    pallas_call x9, Pallas kernels, call(): pl.pallas_call(body, name=name, in_specs=[vmem] * count + [pl.BlockSpec(m...  4.16 us
  transfers between devices with their start and end apart: 6, of which 6 were waited for; matrix products, arithmetic and copies ran while one was open for 0% of the time, Pallas kernels for 3%

profile of v2, /device:TPU:32, one launch (start us, length us, event | category | flops | bytes accessed | tf_op | source)
XLA Modules:
  0.0 54.4 jit_solution(5079831539262365716)
XLA Ops:
  0.0 8.6 %first.1 = (bf16[384,2048]{1,0:T(8,128)(2,1)S(1)}, f32[8,2048]{1,0:T(8,128)S(1)}, f32[392,384]{1,0:T(8,128)S(1)}, f32[328,384]{1,0:T(8,128)S(1)}) custom-call(s32[6]{0:T(128)} %ranks.1, bf16[8,2048]{1,0:T(8,128)(2,1)} %b_hbm.1, bf16[2048,2048]{1,0:T(8,128)(2,1)} %d_hbm.1, bf16[2048,384]{1,0:T(8,128)(2,1)} %u_hbm.1, bf16[2048,384]{1,0:T(8,128)(2,1)} %v_hbm.1), custom_call_target="tpu_custom_call" | custom-call | tf_op jit(solution)/shard_map/first/pallas_call | solution.py:233
  8.6 0.1 collective-permute-start
  8.7 1.9 %collective-permute-done.refs_1_.refs_0_ = f32[328,384]{1,0:T(8,128)S(1)} collective-permute-done((f32[328,384]{1,0:T(8,128)S(1)}, f32[328,384]{1,0:T(8,128)S(1)}, u32[]{:S(2)}, u32[]{:S(2)}) %collective-permute-start) | collective-permute-done | bytes 503840 | tf_op jit(solution)/shard_map/ppermute | solution.py:263
  10.5 0.5 level_0.1
  11.0 1.9 %collective-permute-start.1 = (f32[336,256]{1,0:T(8,128)S(1)}, f32[336,256]{1,0:T(8,128)S(1)}, u32[]{:S(2)}, u32[]{:S(2)}) collective-permute-start(f32[336,256]{1,0:T(8,128)S(1)} %get-tuple-element.22), channel_id=1, source_target_pairs={{0,8},{4,12},{8,0},{12,4},{16,24},{20,28},{24,16},{28,20},{32,40},... | collective-permute-start | bytes 1032200 | tf_op jit(solution)/shard_map/ppermute | solution.py:263
  12.9 8.4 %collective-permute-done.1.refs_1_ = f32[336,256]{1,0:T(8,128)S(1)} collective-permute-done((f32[336,256]{1,0:T(8,128)S(1)}, f32[336,256]{1,0:T(8,128)S(1)}, u32[]{:S(2)}, u32[]{:S(2)}) %collective-permute-start.1) | collective-permute-done | bytes 344096 | tf_op jit(solution)/shard_map/ppermute | solution.py:263
  21.2 0.4 level_1.1
  21.7 3.3 %collective-permute-start.2 = (f32[200,256]{1,0:T(8,128)S(1)}, f32[200,256]{1,0:T(8,128)S(1)}, u32[]{:S(2)}, u32[]{:S(2)}) collective-permute-start(f32[200,256]{1,0:T(8,128)S(1)} %get-tuple-element.24), channel_id=1, source_target_pairs={{0,16},{4,20},{8,24},{12,28},{16,0},{20,4},{24,8},{28,12},{32,48},... | collective-permute-start | bytes 614408 | tf_op jit(solution)/shard_map/ppermute | solution.py:263
  25.0 8.1 %collective-permute-done.2.refs_1_.refs_2_ = f32[200,256]{1,0:T(8,128)S(1)} collective-permute-done((f32[200,256]{1,0:T(8,128)S(1)}, f32[200,256]{1,0:T(8,128)S(1)}, u32[]{:S(2)}, u32[]{:S(2)}) %collective-permute-start.2) | collective-permute-done | bytes 204832 | tf_op jit(solution)/shard_map/ppermute | solution.py:263
  33.1 0.4 level_2.1
  33.5 5.7 %collective-permute-start.3 = (f32[208,128]{1,0:T(8,128)S(1)}, f32[208,128]{1,0:T(8,128)S(1)}, u32[]{:S(2)}, u32[]{:S(2)}) collective-permute-start(f32[208,128]{1,0:T(8,128)S(1)} %get-tuple-element.26), channel_id=1, source_target_pairs={{0,48},{4,52},{8,56},{12,60},{16,32},{20,36},{24,40},{28,44},{32,1... | collective-permute-start | bytes 319496 | tf_op jit(solution)/shard_map/ppermute | solution.py:263
  39.1 0.4 coefficients.1.refs_2_.refs_1_
  39.5 4.4 %collective-permute-done.3.refs_1_.refs_0_ = f32[208,128]{1,0:T(8,128)S(1)} collective-permute-done((f32[208,128]{1,0:T(8,128)S(1)}, f32[208,128]{1,0:T(8,128)S(1)}, u32[]{:S(2)}, u32[]{:S(2)}) %collective-permute-start.3) | collective-permute-done | bytes 106528 | tf_op jit(solution)/shard_map/ppermute | solution.py:263
  44.0 0.4 level_3.1
  44.4 0.6 %collective-permute-start.4 = (f32[72,128]{1,0:T(8,128)S(1)}, f32[72,128]{1,0:T(8,128)S(1)}, u32[]{:S(2)}, u32[]{:S(2)}) collective-permute-start(f32[72,128]{1,0:T(8,128)S(1)} %get-tuple-element.28), channel_id=1, source_target_pairs={{0,64},{4,68},{8,72},{12,76},{16,80},{20,84},{24,88},{28,92},{32,9... | collective-permute-start | bytes 110600 | tf_op jit(solution)/shard_map/ppermute | solution.py:263
  45.0 0.7 %basis.1.refs_2_.refs_1_ = f32[136,2048]{1,0:T(8,128)S(1)} custom-call(f32[208,128]{1,0:T(8,128)S(1)} %collective-permute-done.3.refs_1_.refs_0_, f32[200,192]{1,0:T(8,128)S(1)} %coefficients.1.refs_2_.refs_1_, bf16[384,2048]{1,0:T(8,128)(2,1)S(1)} %get-tuple-element.29.refs_2_, f32[8,2048]{1,0:T(8,128)S(1)} %get-tuple-element.30.refs_3_), custom_call_target="tpu_custom_call" | custom-call | tf_op jit(solution)/shard_map/basis/pallas_call | solution.py:219
  45.7 2.8 %collective-permute-done.4.refs_1_.refs_0_ = f32[72,128]{1,0:T(8,128)S(1)} collective-permute-done((f32[72,128]{1,0:T(8,128)S(1)}, f32[72,128]{1,0:T(8,128)S(1)}, u32[]{:S(2)}, u32[]{:S(2)}) %collective-permute-start.4) | collective-permute-done | bytes 36896 | tf_op jit(solution)/shard_map/ppermute | solution.py:263
  48.4 0.2 level_4.1
  48.6 1.9 %collective-permute-start.5 = (f32[8,128]{1,0:T(8,128)S(1)}, f32[8,128]{1,0:T(8,128)S(1)}, u32[]{:S(2)}, u32[]{:S(2)}) collective-permute-start(f32[8,128]{1,0:T(8,128)S(1)} %level_4.1), channel_id=1, source_target_pairs={{0,192},{4,196},{8,200},{12,204},{16,208},{20,212},{24,216},{28,22... | collective-permute-start | bytes 12296 | tf_op jit(solution)/shard_map/ppermute | solution.py:263
  50.5 0.3 late.1
  50.8 2.7 %collective-permute-done.5.refs_0_ = f32[8,128]{1,0:T(8,128)S(1)} collective-permute-done((f32[8,128]{1,0:T(8,128)S(1)}, f32[8,128]{1,0:T(8,128)S(1)}, u32[]{:S(2)}, u32[]{:S(2)}) %collective-permute-start.5) | collective-permute-done | bytes 4128 | tf_op jit(solution)/shard_map/ppermute | solution.py:263
  53.5 0.9 %last.1 = f32[8,2048]{1,0:T(8,128)} custom-call(f32[8,128]{1,0:T(8,128)S(1)} %collective-permute-done.5.refs_0_, bf16[192,2048]{1,0:T(8,128)(2,1)S(1)} %get-tuple-element.31.refs_1_, f32[8,2048]{1,0:T(8,128)S(1)} %get-tuple-element.32.refs_2_), custom_call_target="tpu_custom_call" | custom-call | tf_op jit(solution)/shard_map/last/pallas_call | solution.py:219
Async XLA Ops:
  8.6 2.0 %collective-permute-start = (f32[328,384]{1,0:T(8,128)S(1)}, f32[328,384]{1,0:T(8,128)S(1)}, u32[]{:S(2)}, u32[]{:S(2)}) collective-permute-start(f32[328,384]{1,0:T(8,128)S(1)} %get-tuple-element.20), channel_id=1, source_target_pairs={{0,4},{4,0},{8,12},{12,8},{16,20},{20,16},{24,28},{28,24},{32,36},... | collective-permute-start | bytes 1511432 | tf_op jit(solution)/shard_map/ppermute | solution.py:263
  11.0 10.3 %collective-permute-start.1 = (f32[336,256]{1,0:T(8,128)S(1)}, f32[336,256]{1,0:T(8,128)S(1)}, u32[]{:S(2)}, u32[]{:S(2)}) collective-permute-start(f32[336,256]{1,0:T(8,128)S(1)} %get-tuple-element.22), channel_id=1, source_target_pairs={{0,8},{4,12},{8,0},{12,4},{16,24},{20,28},{24,16},{28,20},{32,40},... | collective-permute-start | bytes 1032200 | tf_op jit(solution)/shard_map/ppermute | solution.py:263
  21.7 11.4 %collective-permute-start.2 = (f32[200,256]{1,0:T(8,128)S(1)}, f32[200,256]{1,0:T(8,128)S(1)}, u32[]{:S(2)}, u32[]{:S(2)}) collective-permute-start(f32[200,256]{1,0:T(8,128)S(1)} %get-tuple-element.24), channel_id=1, source_target_pairs={{0,16},{4,20},{8,24},{12,28},{16,0},{20,4},{24,8},{28,12},{32,48},... | collective-permute-start | bytes 614408 | tf_op jit(solution)/shard_map/ppermute | solution.py:263
  33.5 10.5 %collective-permute-start.3 = (f32[208,128]{1,0:T(8,128)S(1)}, f32[208,128]{1,0:T(8,128)S(1)}, u32[]{:S(2)}, u32[]{:S(2)}) collective-permute-start(f32[208,128]{1,0:T(8,128)S(1)} %get-tuple-element.26), channel_id=1, source_target_pairs={{0,48},{4,52},{8,56},{12,60},{16,32},{20,36},{24,40},{28,44},{32,1... | collective-permute-start | bytes 319496 | tf_op jit(solution)/shard_map/ppermute | solution.py:263
  44.4 4.0 %collective-permute-start.4 = (f32[72,128]{1,0:T(8,128)S(1)}, f32[72,128]{1,0:T(8,128)S(1)}, u32[]{:S(2)}, u32[]{:S(2)}) collective-permute-start(f32[72,128]{1,0:T(8,128)S(1)} %get-tuple-element.28), channel_id=1, source_target_pairs={{0,64},{4,68},{8,72},{12,76},{16,80},{20,84},{24,88},{28,92},{32,9... | collective-permute-start | bytes 110600 | tf_op jit(solution)/shard_map/ppermute | solution.py:263
  48.6 4.9 %collective-permute-start.5 = (f32[8,128]{1,0:T(8,128)S(1)}, f32[8,128]{1,0:T(8,128)S(1)}, u32[]{:S(2)}, u32[]{:S(2)}) collective-permute-start(f32[8,128]{1,0:T(8,128)S(1)} %level_4.1), channel_id=1, source_target_pairs={{0,192},{4,196},{8,200},{12,204},{16,208},{20,212},{24,216},{28,22... | collective-permute-start | bytes 12296 | tf_op jit(solution)/shard_map/ppermute | solution.py:263

commit v3 on v2

--- a/solution.py
+++ b/solution.py
@@ -14,6 +14,7 @@
 STATE = RANK * LEVELS
 CHUNK = 512
 PARTNER = (1, 2, 4, 12, 16, 48)
+SPLIT = (1, 2, 3)
 
 
 def mul(a, b, dims=NN):
@@ -52,32 +53,44 @@
     return jnp.concatenate([x[:, RANK * j : RANK * (j + 1)] for j in range(blocks)], axis=0)
 
 
-def outgoing(level, state, send):
+def outgoing(level, state):
     blocks = LEVELS - 1 - level
     is_upper = upper(level)
     if level == LEVELS - 1:
-        send[...] = jnp.concatenate([state[RANK:, RANK : 2 * RANK]] * 2, axis=1)
-    elif level % 2 == 0:
-        pivot = state[:RANK, RANK:]
-        packed = jnp.concatenate([stacked(pivot, blocks), state[RANK * (blocks + 1) :, :RANK]], axis=0)
+        return jnp.concatenate([state[RANK:, RANK : 2 * RANK]] * 2, axis=1)
+    if level % 2 == 0:
+        packed = jnp.concatenate([stacked(state[:RANK, RANK:], blocks), state[RANK * (blocks + 1) :, :RANK]], axis=0)
         first = jnp.where(is_upper, packed, state[RANK:, :RANK])
-        send[:, : 2 * RANK] = jnp.concatenate([first, state[RANK:, RANK : 2 * RANK]], axis=1)
+        tiles = [jnp.concatenate([first, state[RANK:, RANK : 2 * RANK]], axis=1)]
         if blocks > 1:
-            send[:, 2 * RANK :] = state[RANK:, 2 * RANK :]
+            tiles.append(state[RANK:, 2 * RANK :])
+        message = jnp.concatenate(tiles, axis=1)
     else:
-        rows = RANK * blocks + 8
-        send[:rows] = state[RANK:, 2 * RANK :]
         left = state[RANK:, RANK : 2 * RANK]
-        packed = side_by_side(left, blocks)
-        send[rows : rows + RANK] = jnp.where(is_upper, state[:RANK, 2 * RANK :], packed)
-        send[rows + RANK :] = jnp.concatenate([left[RANK * blocks :]] * blocks, axis=1)
+        pivot = jnp.where(is_upper, state[:RANK, 2 * RANK :], side_by_side(left, blocks))
+        rest = jnp.concatenate([left[RANK * blocks :]] * blocks, axis=1)
+        message = jnp.concatenate([state[RANK:, 2 * RANK :], pivot, rest], axis=0)
+    short = whole_rows(level) - message.shape[0]
+    if short:
+        message = jnp.concatenate([message, jnp.zeros((short, message.shape[1]), f32)], axis=0)
+    return message
+
+
+def post(level, state, send, full):
+    message = outgoing(level, state)
+    if level in SPLIT:
+        full[...] = message
+        half = send.shape[0]
+        send[...] = full[pl.ds(half * (lax.axis_index("leaf") & 1), half)]
+    else:
+        send[...] = message
 
 
 def pivots(level, got):
     blocks = LEVELS - 1 - level
+    rows = RANK * blocks + 8
     if level % 2 == 0:
-        return got[:, :RANK]
-    rows = RANK * blocks + 8
+        return got[:rows, :RANK]
     return jnp.concatenate([stacked(got[rows : rows + RANK], blocks), got[rows + RANK :, :RANK]], axis=0)
 
 
@@ -124,53 +137,58 @@
             acc[...] += total
     state[:STATE] = acc[:STATE] * keep
     state[STATE:] = (acc[STATE : STATE + 8] + acc[STATE + 8 : STATE + 16] + acc[STATE + 16 :]) * keep
-    outgoing(0, state[...], send)
-
-
-def level_kernel(level, own, got, *refs):
-    send = refs[-1]
-    blocks = LEVELS - 1 - level
+    post(0, state[...], send, None)
+
+
+def level_kernel(level, *refs):
+    parts = 2 if level in SPLIT else 1
+    own, got, refs = refs[0], refs[1 : 1 + parts], list(refs[1 + parts :])
+    received, sent = refs[-2:]
+    blocks = LEVELS - 1 - level
+    rows = RANK * blocks + 8
     is_upper = upper(level)
+    if parts == 2:
+        half = got[0].shape[0]
+        core = lax.axis_index("leaf") & 1
+        received[pl.ds(half * core, half)] = got[0][...]
+        received[pl.ds(half * (1 - core), half)] = got[1][...]
+        arrived = received[...]
+    else:
+        arrived = got[0][...]
     skip = RANK if level % 2 else 0
     first = 2 * skip
     own_left = own[RANK:, skip : skip + RANK]
     own_right = own[:RANK, first:]
-    arrived = got[...]
-    left = jnp.where(is_upper, pivots(level, arrived), own_left)
+    theirs = pivots(level, arrived)
+    left = jnp.where(is_upper, theirs, own_left)
+    bulk = arrived[:rows]
     if level % 2 == 0:
-        bulk = arrived
         right = jnp.concatenate([own_right[:, :RANK], side_by_side(arrived[:, :RANK], blocks)], axis=1)
     else:
-        rows = RANK * blocks + 8
-        bulk = arrived[:rows]
         right = arrived[rows : rows + RANK]
     right = jnp.where(is_upper, own_right, right)
     total = own[RANK:, first:] + bulk - wide_mul(left, right)
+    post(level + 1, total, refs[0], sent)
+    refs[1][...] = jnp.where(is_upper, theirs, 0.0)
     if level < LEVELS - 2:
-        refs[-2][...] = total
-    outgoing(level + 1, total, send)
-
-
-def coefficients(level, got, t):
-    blocks = LEVELS - 1 - level
-    left = jnp.where(upper(level), pivots(level, got), 0.0)
-    done = -left
+        refs[2][...] = total
+
+
+def coefficients(left, t):
     if t is None:
-        return done
-    done = jnp.concatenate([t[RANK:] - wide_mul(left, t[:RANK]), done], axis=1)
-    return done
-
-
-def coefficient_kernel(levels, *refs):
-    count = len(levels)
-    t = refs[count][...] if len(refs) == count + 2 else None
-    for level, got in zip(levels, refs):
-        t = coefficients(level, got[...], t)
+        return -left
+    return jnp.concatenate([t[RANK:] - wide_mul(left, t[:RANK]), -left], axis=1)
+
+
+def coefficient_kernel(*refs):
+    t = None
+    for left in refs[:-1]:
+        t = coefficients(left[...], t)
     refs[-1][...] = t
 
 
-def basis_kernel(got, t_ref, mapped, base, out):
-    t = coefficients(3, got[...], t_ref[...])
+def basis_kernel(left, t_ref, mapped, base, out):
+    t = coefficients(left[...], t_ref[...])
     w = mapped[...]
     high, low = halves(t)
     rows = t.shape[0]
@@ -180,9 +198,8 @@
     out[2 * RANK :] = base[...] + product[2 * RANK :]
 
 
-def late_kernel(got, basis, high_low, shifted):
-    left = jnp.where(upper(4), pivots(4, got[...]), 0.0)
-    update = basis[RANK:] - wide_mul(left, basis[:RANK])
+def late_kernel(left, basis, high_low, shifted):
+    update = basis[RANK:] - wide_mul(left[...], basis[:RANK])
     high, low = halves(update[:RANK])
     high_low[:RANK] = high
     high_low[RANK : 2 * RANK] = low
@@ -196,20 +213,31 @@
     out[...] = shifted[...] - mul(jnp.concatenate([high, high, low], axis=1), high_low[...])
 
 
-def send_shape(level):
+def whole_rows(level):
+    blocks = LEVELS - 1 - level
+    if level == LEVELS - 1:
+        return 8
+    rows = RANK * blocks + 8 if level % 2 == 0 else RANK * (blocks + 1) + 16
+    return -(-rows // 16) * 16 if level in SPLIT else rows
+
+
+def whole_shape(level):
     blocks = LEVELS - 1 - level
     if level == LEVELS - 1:
         return (8, 2 * RANK)
-    if level % 2 == 0:
-        return (RANK * blocks + 8, RANK * (blocks + 1))
-    return (RANK * (blocks + 1) + 16, RANK * blocks)
+    return (whole_rows(level), RANK * (blocks + 1 - level % 2))
+
+
+def send_shape(level):
+    rows, lanes = whole_shape(level)
+    return (rows // 2 if level in SPLIT else rows, lanes)
 
 
 def state_shape(level):
     return (RANK * (LEVELS - level) + 8, STATE - 2 * RANK * (level // 2))
 
 
-def call(kernel, name, outs, *args, after=()):
+def call(kernel, name, outs, *args, after=(), scratch=()):
     vmem = pl.BlockSpec(memory_space=pltpu.VMEM)
     count = len(args)
 
@@ -222,8 +250,13 @@
         in_specs=[vmem] * count + [pl.BlockSpec(memory_space=pl.ANY)] * len(after),
         out_specs=[vmem] * len(outs),
         out_shape=[jax.ShapeDtypeStruct(s, t) for s, t in outs],
+        scratch_shapes=[pltpu.VMEM(s, f32) for s in scratch],
         compiler_params=pltpu.CompilerParams(vmem_limit_bytes=16 << 20),
     )(*args, *after)
+
+
+def swapped(x, distance):
+    return lax.ppermute(x, "leaf", [(i, i ^ distance) for i in range(lax.axis_size("leaf"))])
 
 
 def on_device(rhs_vectors, diag_inverse, left_factors, right_factors, ranks):
@@ -257,37 +290,38 @@
             for a in (ranks, rhs_vectors, diag_inverse, left_factors, right_factors)
         ),
     )
-    got = []
-    for level in range(LEVELS):
-        pairs = [(i, i ^ PARTNER[level]) for i in range(lax.axis_size("leaf"))]
-        got.append(lax.ppermute(send, "leaf", pairs))
+    lefts = []
+    basis = t = None
+    for level in range(LEVELS - 1):
+        got = [swapped(send, PARTNER[level])]
+        if level in SPLIT:
+            got.append(swapped(got[0], 1))
         after = ()
         if level == 3:
-            (t,) = after = call(
-                lambda *refs: coefficient_kernel((0, 1, 2), *refs),
-                "coefficients",
-                [((3 * RANK + 8, 3 * RANK), f32)],
-                *got[:3],
-            )
+            (t,) = after = call(coefficient_kernel, "coefficients", [((3 * RANK + 8, 3 * RANK), f32)], *lefts)
         if level == 4:
             (basis,) = after = call(
-                basis_kernel, "basis", [((2 * RANK + 8, size), f32)], got[3], t, mapped, base
+                basis_kernel, "basis", [((2 * RANK + 8, size), f32)], lefts[3], t, mapped, base
             )
-        if level < LEVELS - 1:
-            outs = [(send_shape(level + 1), f32)]
-            if level < LEVELS - 2:
-                outs.insert(0, (state_shape(level + 1), f32))
-            *states, send = call(
-                lambda *refs, level=level: level_kernel(level, *refs),
-                f"level_{level}",
-                outs,
-                state,
-                got[level],
-                after=after,
-            )
-            state = states[0] if states else None
-    high_low, shifted = call(late_kernel, "late", [((3 * RANK, size), bf16), ((8, size), f32)], got[4], basis)
-    (out,) = call(last_kernel, "last", [((8, size), f32)], got[5], high_low, shifted)
+        outs = [send_shape(level + 1), (RANK * (LEVELS - 1 - level) + 8, RANK)]
+        if level < LEVELS - 2:
+            outs.append(state_shape(level + 1))
+        send, left, *state = call(
+            lambda *refs, level=level: level_kernel(level, *refs),
+            f"level_{level}",
+            [(s, f32) for s in outs],
+            state,
+            *got,
+            after=after,
+            scratch=[whole_shape(level), whole_shape(level + 1)],
+        )
+        state = state[0] if state else None
+        lefts.append(left)
+    got = swapped(send, PARTNER[LEVELS - 1])
+    high_low, shifted = call(
+        late_kernel, "late", [((3 * RANK, size), bf16), ((8, size), f32)], lefts[4], basis
+    )
+    (out,) = call(last_kernel, "last", [((8, size), f32)], got, high_low, shifted)
     return out
 
 

time: 54.5 us -> 49.7 us (0.912)
  waiting for transfers between devices: 28.2 us -> 22.5 us
  starting transfers between devices: 13.5 us -> 14.3 us
    ppermute x6 -> x9, waiting for transfers between devices: 28.2 us -> 22.5 us  [swapped(): lax.ppermute(x, 'leaf', [(i, i ^ distance) for i in range(lax.axis_size('...]
    ppermute x6 -> x9, starting transfers between devices: 13.5 us -> 14.3 us  [swapped(): lax.ppermute(x, 'leaf', [(i, i ^ distance) for i in range(lax.axis_size('...]
  transfers between devices with their start and end apart: 6 -> 9, of which waited for: 6 -> 9; matrix products, arithmetic and copies ran while one was open for 0% -> 0% of each run, Pallas kernels for 3% -> 3%
where the time goes in v3:
time: 49.7 us; the launch traced here: 49.6 us
  waiting for transfers between devices  22.5 us (45%)
  starting transfers between devices  14.3 us (29%)
  Pallas kernels  12.7 us (26%)
    ppermute x9, waiting for transfers between devices, swapped(): lax.ppermute(x, 'leaf', [(i, i ^ distance) for i in range(lax.axis_size('...  22.5 us
    ppermute x9, starting transfers between devices, swapped(): lax.ppermute(x, 'leaf', [(i, i ^ distance) for i in range(lax.axis_size('...  14.3 us
    pallas_call x1, Pallas kernels, on_device(): pl.pallas_call(first_kernel, name='first', in_specs=[pl.BlockSpec(memory_...  8.55 us
    pallas_call x9, Pallas kernels, call(): pl.pallas_call(body, name=name, in_specs=[vmem] * count + [pl.BlockSpec(m...  4.14 us
  transfers between devices with their start and end apart: 9, of which 9 were waited for; matrix products, arithmetic and copies ran while one was open for 0% of the time, Pallas kernels for 3%

profile of v3, /device:TPU:32, one launch (start us, length us, event | category | flops | bytes accessed | tf_op | source)
XLA Modules:
  0.0 49.6 jit_solution(10431679521608580878)
XLA Ops:
  0.0 8.6 %first.1 = (bf16[384,2048]{1,0:T(8,128)(2,1)S(1)}, f32[8,2048]{1,0:T(8,128)S(1)}, f32[392,384]{1,0:T(8,128)S(1)}, f32[328,384]{1,0:T(8,128)S(1)}) custom-call(s32[6]{0:T(128)} %ranks.1, bf16[8,2048]{1,0:T(8,128)(2,1)} %b_hbm.1, bf16[2048,2048]{1,0:T(8,128)(2,1)} %d_hbm.1, bf16[2048,384]{1,0:T(8,128)(2,1)} %u_hbm.1, bf16[2048,384]{1,0:T(8,128)(2,1)} %v_hbm.1), custom_call_target="tpu_custom_call" | custom-call | tf_op jit(solution)/shard_map/first/pallas_call | solution.py:266
  8.6 0.1 collective-permute-start
  8.7 1.9 %collective-permute-done.refs_1_ = f32[328,384]{1,0:T(8,128)S(1)} collective-permute-done((f32[328,384]{1,0:T(8,128)S(1)}, f32[328,384]{1,0:T(8,128)S(1)}, u32[]{:S(2)}, u32[]{:S(2)}) %collective-permute-start) | collective-permute-done | bytes 503840 | tf_op jit(solution)/shard_map/ppermute | solution.py:259
  10.5 0.5 level_0.1
  11.0 1.9 %collective-permute-start.1 = (f32[168,256]{1,0:T(8,128)S(1)}, f32[168,256]{1,0:T(8,128)S(1)}, u32[]{:S(2)}, u32[]{:S(2)}) collective-permute-start(f32[168,256]{1,0:T(8,128)S(1)} %get-tuple-element.28), channel_id=1, source_target_pairs={{0,8},{4,12},{8,0},{12,4},{16,24},{20,28},{24,16},{28,20},{32,40},... | collective-permute-start | bytes 516104 | tf_op jit(solution)/shard_map/ppermute | solution.py:259
  12.9 4.7 %collective-permute-done.1.refs_1_ = f32[168,256]{1,0:T(8,128)S(1)} collective-permute-done((f32[168,256]{1,0:T(8,128)S(1)}, f32[168,256]{1,0:T(8,128)S(1)}, u32[]{:S(2)}, u32[]{:S(2)}) %collective-permute-start.1) | collective-permute-done | bytes 172064 | tf_op jit(solution)/shard_map/ppermute | solution.py:259
  17.6 0.0 collective-permute-start.2
  17.6 1.4 %collective-permute-done.2.refs_2_ = f32[168,256]{1,0:T(8,128)S(1)} collective-permute-done((f32[168,256]{1,0:T(8,128)S(1)}, f32[168,256]{1,0:T(8,128)S(1)}, u32[]{:S(2)}, u32[]{:S(2)}) %collective-permute-start.2) | collective-permute-done | bytes 172064 | tf_op jit(solution)/shard_map/ppermute | solution.py:259
  19.0 0.5 level_1.1
  19.5 3.3 %collective-permute-start.3 = (f32[104,256]{1,0:T(8,128)S(1)}, f32[104,256]{1,0:T(8,128)S(1)}, u32[]{:S(2)}, u32[]{:S(2)}) collective-permute-start(f32[104,256]{1,0:T(8,128)S(1)} %get-tuple-element.30), channel_id=1, source_target_pairs={{0,16},{4,20},{8,24},{12,28},{16,0},{20,4},{24,8},{28,12},{32,48},... | collective-permute-start | bytes 319496 | tf_op jit(solution)/shard_map/ppermute | solution.py:259
  22.7 4.5 %collective-permute-done.3.refs_1_ = f32[104,256]{1,0:T(8,128)S(1)} collective-permute-done((f32[104,256]{1,0:T(8,128)S(1)}, f32[104,256]{1,0:T(8,128)S(1)}, u32[]{:S(2)}, u32[]{:S(2)}) %collective-permute-start.3) | collective-permute-done | bytes 106528 | tf_op jit(solution)/shard_map/ppermute | solution.py:259
  27.3 0.0 collective-permute-start.4
  27.3 1.3 %collective-permute-done.4.refs_2_ = f32[104,256]{1,0:T(8,128)S(1)} collective-permute-done((f32[104,256]{1,0:T(8,128)S(1)}, f32[104,256]{1,0:T(8,128)S(1)}, u32[]{:S(2)}, u32[]{:S(2)}) %collective-permute-start.4) | collective-permute-done | bytes 106528 | tf_op jit(solution)/shard_map/ppermute | solution.py:259
  28.6 0.4 level_2.1
  29.0 5.9 %collective-permute-start.5 = (f32[104,128]{1,0:T(8,128)S(1)}, f32[104,128]{1,0:T(8,128)S(1)}, u32[]{:S(2)}, u32[]{:S(2)}) collective-permute-start(f32[104,128]{1,0:T(8,128)S(1)} %get-tuple-element.32), channel_id=1, source_target_pairs={{0,48},{4,52},{8,56},{12,60},{16,32},{20,36},{24,40},{28,44},{32,1... | collective-permute-start | bytes 159752 | tf_op jit(solution)/shard_map/ppermute | solution.py:259
  34.9 3.0 %collective-permute-done.5.refs_1_ = f32[104,128]{1,0:T(8,128)S(1)} collective-permute-done((f32[104,128]{1,0:T(8,128)S(1)}, f32[104,128]{1,0:T(8,128)S(1)}, u32[]{:S(2)}, u32[]{:S(2)}) %collective-permute-start.5) | collective-permute-done | bytes 53280 | tf_op jit(solution)/shard_map/ppermute | solution.py:259
  37.9 0.0 collective-permute-start.6
  37.9 0.4 coefficients.1.refs_3_.refs_1_
  38.3 0.8 %collective-permute-done.6.refs_2_ = f32[104,128]{1,0:T(8,128)S(1)} collective-permute-done((f32[104,128]{1,0:T(8,128)S(1)}, f32[104,128]{1,0:T(8,128)S(1)}, u32[]{:S(2)}, u32[]{:S(2)}) %collective-permute-start.6) | collective-permute-done | bytes 53280 | tf_op jit(solution)/shard_map/ppermute | solution.py:259
  39.1 0.4 level_3.1
  39.5 0.9 %collective-permute-start.7 = (f32[72,128]{1,0:T(8,128)S(1)}, f32[72,128]{1,0:T(8,128)S(1)}, u32[]{:S(2)}, u32[]{:S(2)}) collective-permute-start(f32[72,128]{1,0:T(8,128)S(1)} %get-tuple-element.37), channel_id=1, source_target_pairs={{0,64},{4,68},{8,72},{12,76},{16,80},{20,84},{24,88},{28,92},{32,9... | collective-permute-start | bytes 110600 | tf_op jit(solution)/shard_map/ppermute | solution.py:259
  40.5 0.6 %basis.1.refs_2_.refs_1_ = f32[136,2048]{1,0:T(8,128)S(1)} custom-call(f32[136,64]{1,0:T(8,128)S(1)} %get-tuple-element.38.refs_0_, f32[200,192]{1,0:T(8,128)S(1)} %coefficients.1.refs_3_.refs_1_, bf16[384,2048]{1,0:T(8,128)(2,1)S(1)} %get-tuple-element.39.refs_2_, f32[8,2048]{1,0:T(8,128)S(1)} %get-tuple-element.40.refs_3_), custom_call_target="tpu_custom_call" | custom-call | tf_op jit(solution)/shard_map/basis/pallas_call | solution.py:247
  41.1 2.5 %collective-permute-done.7.refs_1_ = f32[72,128]{1,0:T(8,128)S(1)} collective-permute-done((f32[72,128]{1,0:T(8,128)S(1)}, f32[72,128]{1,0:T(8,128)S(1)}, u32[]{:S(2)}, u32[]{:S(2)}) %collective-permute-start.7) | collective-permute-done | bytes 36896 | tf_op jit(solution)/shard_map/ppermute | solution.py:259
  43.6 0.2 level_4.1
  43.8 2.2 %collective-permute-start.8 = (f32[8,128]{1,0:T(8,128)S(1)}, f32[8,128]{1,0:T(8,128)S(1)}, u32[]{:S(2)}, u32[]{:S(2)}) collective-permute-start(f32[8,128]{1,0:T(8,128)S(1)} %get-tuple-element.41), channel_id=1, source_target_pairs={{0,192},{4,196},{8,200},{12,204},{16,208},{20,212},{24,216},{28,22... | collective-permute-start | bytes 12296 | tf_op jit(solution)/shard_map/ppermute | solution.py:259
  46.0 0.3 late.1
  46.3 2.4 %collective-permute-done.8.refs_0_ = f32[8,128]{1,0:T(8,128)S(1)} collective-permute-done((f32[8,128]{1,0:T(8,128)S(1)}, f32[8,128]{1,0:T(8,128)S(1)}, u32[]{:S(2)}, u32[]{:S(2)}) %collective-permute-start.8) | collective-permute-done | bytes 4128 | tf_op jit(solution)/shard_map/ppermute | solution.py:259
  48.7 0.9 %last.1 = f32[8,2048]{1,0:T(8,128)} custom-call(f32[8,128]{1,0:T(8,128)S(1)} %collective-permute-done.8.refs_0_, bf16[192,2048]{1,0:T(8,128)(2,1)S(1)} %get-tuple-element.43.refs_1_, f32[8,2048]{1,0:T(8,128)S(1)} %get-tuple-element.44.refs_2_), custom_call_target="tpu_custom_call" | custom-call | tf_op jit(solution)/shard_map/last/pallas_call | solution.py:247
Async XLA Ops:
  8.6 2.0 %collective-permute-start = (f32[328,384]{1,0:T(8,128)S(1)}, f32[328,384]{1,0:T(8,128)S(1)}, u32[]{:S(2)}, u32[]{:S(2)}) collective-permute-start(f32[328,384]{1,0:T(8,128)S(1)} %get-tuple-element.26), channel_id=1, source_target_pairs={{0,4},{4,0},{8,12},{12,8},{16,20},{20,16},{24,28},{28,24},{32,36},... | collective-permute-start | bytes 1511432 | tf_op jit(solution)/shard_map/ppermute | solution.py:259
  11.0 6.6 %collective-permute-start.1 = (f32[168,256]{1,0:T(8,128)S(1)}, f32[168,256]{1,0:T(8,128)S(1)}, u32[]{:S(2)}, u32[]{:S(2)}) collective-permute-start(f32[168,256]{1,0:T(8,128)S(1)} %get-tuple-element.28), channel_id=1, source_target_pairs={{0,8},{4,12},{8,0},{12,4},{16,24},{20,28},{24,16},{28,20},{32,40},... | collective-permute-start | bytes 516104 | tf_op jit(solution)/shard_map/ppermute | solution.py:259
  17.6 1.4 %collective-permute-start.2 = (f32[168,256]{1,0:T(8,128)S(1)}, f32[168,256]{1,0:T(8,128)S(1)}, u32[]{:S(2)}, u32[]{:S(2)}) collective-permute-start(f32[168,256]{1,0:T(8,128)S(1)} %collective-permute-done.1.refs_1_), channel_id=1, source_target_pairs={{0,4},{4,0},{8,12},{12,8},{16,20},{20,16},{24,28},{28,24},{32,36},... | collective-permute-start | bytes 516104 | tf_op jit(solution)/shard_map/ppermute | solution.py:259
  19.5 7.8 %collective-permute-start.3 = (f32[104,256]{1,0:T(8,128)S(1)}, f32[104,256]{1,0:T(8,128)S(1)}, u32[]{:S(2)}, u32[]{:S(2)}) collective-permute-start(f32[104,256]{1,0:T(8,128)S(1)} %get-tuple-element.30), channel_id=1, source_target_pairs={{0,16},{4,20},{8,24},{12,28},{16,0},{20,4},{24,8},{28,12},{32,48},... | collective-permute-start | bytes 319496 | tf_op jit(solution)/shard_map/ppermute | solution.py:259
  27.3 1.3 %collective-permute-start.4 = (f32[104,256]{1,0:T(8,128)S(1)}, f32[104,256]{1,0:T(8,128)S(1)}, u32[]{:S(2)}, u32[]{:S(2)}) collective-permute-start(f32[104,256]{1,0:T(8,128)S(1)} %collective-permute-done.3.refs_1_), channel_id=1, source_target_pairs={{0,4},{4,0},{8,12},{12,8},{16,20},{20,16},{24,28},{28,24},{32,36},... | collective-permute-start | bytes 319496 | tf_op jit(solution)/shard_map/ppermute | solution.py:259
  29.0 8.9 %collective-permute-start.5 = (f32[104,128]{1,0:T(8,128)S(1)}, f32[104,128]{1,0:T(8,128)S(1)}, u32[]{:S(2)}, u32[]{:S(2)}) collective-permute-start(f32[104,128]{1,0:T(8,128)S(1)} %get-tuple-element.32), channel_id=1, source_target_pairs={{0,48},{4,52},{8,56},{12,60},{16,32},{20,36},{24,40},{28,44},{32,1... | collective-permute-start | bytes 159752 | tf_op jit(solution)/shard_map/ppermute | solution.py:259
  37.9 1.2 %collective-permute-start.6 = (f32[104,128]{1,0:T(8,128)S(1)}, f32[104,128]{1,0:T(8,128)S(1)}, u32[]{:S(2)}, u32[]{:S(2)}) collective-permute-start(f32[104,128]{1,0:T(8,128)S(1)} %collective-permute-done.5.refs_1_), channel_id=1, source_target_pairs={{0,4},{4,0},{8,12},{12,8},{16,20},{20,16},{24,28},{28,24},{32,36},... | collective-permute-start | bytes 159752 | tf_op jit(solution)/shard_map/ppermute | solution.py:259
  39.5 4.0 %collective-permute-start.7 = (f32[72,128]{1,0:T(8,128)S(1)}, f32[72,128]{1,0:T(8,128)S(1)}, u32[]{:S(2)}, u32[]{:S(2)}) collective-permute-start(f32[72,128]{1,0:T(8,128)S(1)} %get-tuple-element.37), channel_id=1, source_target_pairs={{0,64},{4,68},{8,72},{12,76},{16,80},{20,84},{24,88},{28,92},{32,9... | collective-permute-start | bytes 110600 | tf_op jit(solution)/shard_map/ppermute | solution.py:259
  43.8 4.9 %collective-permute-start.8 = (f32[8,128]{1,0:T(8,128)S(1)}, f32[8,128]{1,0:T(8,128)S(1)}, u32[]{:S(2)}, u32[]{:S(2)}) collective-permute-start(f32[8,128]{1,0:T(8,128)S(1)} %get-tuple-element.41), channel_id=1, source_target_pairs={{0,192},{4,196},{8,200},{12,204},{16,208},{20,212},{24,216},{28,22... | collective-permute-start | bytes 12296 | tf_op jit(solution)/shard_map/ppermute | solution.py:259

commit v4 on v3

v4 whole, which is shorter than its diff:
```python
import jax
import jax.numpy as jnp
from jax import lax
from jax.experimental import pallas as pl
from jax.experimental.pallas import tpu as pltpu
from jax.sharding import PartitionSpec as P

f32 = jnp.float32
bf16 = jnp.bfloat16
NN = (((1,), (0,)), ((), ()))
NT = (((1,), (1,)), ((), ()))
RANK = 64
LEVELS = 6
STATE = RANK * LEVELS
CHUNK = 512
PARTNER = (1, 2, 4, 12, 16, 48)
PIECES = (9, 6, 4, 2, 1, 0)


def mul(a, b, dims=NN):
    return lax.dot_general(a, b, dims, preferred_element_type=f32)


def halves(x):
    high = x.astype(bf16)
    return high, (x - high.astype(f32)).astype(bf16)


def thirds(x):
    high, low = halves(x)
    rest = x - high.astype(f32) - low.astype(f32)
    return high, low, rest.astype(bf16)


def wide_mul(a, b):
    a_high, a_low = halves(a)
    b_high, b_low = halves(b)
    return mul(
        jnp.concatenate([a_high, a_high, a_low], axis=1),
        jnp.concatenate([b_high, b_low, b_high], axis=0),
    )


def upper(level):
    return (lax.axis_index("leaf") >> level & 1) == 1


def folded(x):
    return jnp.concatenate([x[: RANK // 2], x[RANK // 2 :]], axis=1)


def unfolded(x):
    return jnp.concatenate([x[:, :RANK], x[:, RANK:]], axis=0)


class Places:
    def __init__(self, level):
        self.count = LEVELS - 1 - level
        leaf = lax.axis_index("leaf")
        self.bits = [(leaf >> (level + 1 + k)) & 1 for k in range(self.count)]
        self.ones_before = [sum(self.bits[:k], jnp.int32(0)) for k in range(self.count + 1)]
        self.ones = self.ones_before[-1]
        self.zeros = self.count - self.ones
        self.inner = self.ones * self.zeros

    def next_piece(self, position):
        own = self.bits[0]
        ones, zeros = self.ones - own, self.zeros - (1 - own)
        inner = ones * zeros
        within = position < inner
        a = sum([(position >= t * zeros).astype(jnp.int32) for t in range(1, self.count)], jnp.int32(0))
        b = position - a * zeros
        rest = position - inner
        a = jnp.where(within, a + own, jnp.where(own == 1, 0, rest))
        b = jnp.where(within, b + 1 - own, jnp.where(own == 1, rest, 0))
        valid = (a < self.ones) & (b < self.zeros)
        return jnp.where(valid, a, 0), jnp.where(valid, b, 0), valid

    def nth(self, n, bit):
        found = jnp.int32(0)
        for k in range(self.count):
            before = self.ones_before[k] if bit else k - self.ones_before[k]
            found = jnp.where((before == n) & (self.bits[k] == bit), k, found)
        return found


def piece(ref, index, limit):
    index = jnp.minimum(index, limit - 1)
    return ref[pl.ds(pl.multiple_of(RANK // 2 * index, RANK // 2), RANK // 2)]


def first_kernel(ranks, b_hbm, d_hbm, u_hbm, v_hbm, mapped, base, send, d, u, v, b, x, acc, keeps, sems):
    size = d.shape[0]
    n = size // CHUNK
    copies = [
        pltpu.make_async_copy(d_hbm.at[pl.ds(CHUNK * i, CHUNK)], d.at[pl.ds(CHUNK * i, CHUNK)], sems.at[i])
        for i in range(n)
    ]
    copy_u = pltpu.make_async_copy(u_hbm, u, sems.at[n])
    copy_b = pltpu.make_async_copy(b_hbm, b, sems.at[n + 1])
    copy_v = pltpu.make_async_copy(v_hbm, v, sems.at[n + 2])
    copy_u.start()
    copy_b.start()
    copies[0].start()
    copy_v.start()
    for c in copies[1:]:
        c.start()
    lane = lax.broadcasted_iota(jnp.int32, (1, STATE), 1)
    keep = jnp.zeros((1, STATE), f32)
    for level in range(LEVELS):
        inside = (lane >= RANK * level) & (lane < RANK * level + jnp.minimum(ranks[level], RANK))
        keep = jnp.where(inside, 1.0, keep)
    keeps[...] = jnp.broadcast_to(keep, keeps.shape)
    copy_u.wait()
    copy_b.wait()
    x[:STATE] = (u[...] * keep.astype(bf16)).T
    x[STATE:] = jnp.concatenate([b[...], jnp.zeros((8, size), bf16)], axis=0)
    for i in range(n):
        rows = slice(CHUNK * i, CHUNK * (i + 1))
        copies[i].wait()
        if i == 0:
            copy_v.wait()
        product = mul(x[...], d[rows], NT)
        rounded = product[:STATE].astype(bf16)
        mapped[:, rows] = rounded
        part = product[STATE : STATE + 8]
        base[:, rows] = part
        joined = jnp.concatenate([rounded, *thirds(part)], axis=0)
        total = mul(joined, v[rows])
        if i == 0:
            acc[...] = total
        else:
            acc[...] += total
    rhs = (acc[STATE : STATE + 8] + acc[STATE + 8 : STATE + 16] + acc[STATE + 16 :]) * keep
    places = Places(-1)
    for position in range(PIECES[0]):
        one, zero, valid = places.next_piece(position)
        m, lane_piece = places.nth(one, 1), places.nth(zero, 0)
        rows = pl.ds(pl.multiple_of(RANK * m, RANK), RANK)
        lanes = pl.ds(pl.multiple_of(2 * RANK * (lane_piece // 2), 2 * RANK), 2 * RANK)
        tile = acc[rows, lanes] * keeps[:1, lanes]
        block = jnp.where(lane_piece % 2 == 1, tile[:, RANK:], tile[:, :RANK])
        send[RANK // 2 * position : RANK // 2 * (position + 1)] = folded(jnp.where(valid, block, 0.0))
    for tile in range(LEVELS // 2):
        row = RANK // 2 * PIECES[0] + 8 * tile
        send[row : row + 8] = rhs[:, 2 * RANK * tile : 2 * RANK * (tile + 1)]


def level_kernel(level, own, got, send, left):
    places = Places(level)
    is_upper = upper(level)
    count = PIECES[level]
    rhs_row = RANK // 2 * count
    tiles = LEVELS // 2 - level // 2
    lower_of = lambda index: unfolded(
        jnp.where(is_upper, piece(got, index, count), piece(own, index, count))
    )
    upper_of = lambda index: unfolded(
        jnp.where(is_upper, piece(own, index, count), piece(got, index, count))
    )
    own_rhs = jnp.concatenate([own[rhs_row + 8 * t : rhs_row + 8 * t + 8] for t in range(tiles)], axis=1)
    got_rhs = jnp.concatenate([got[rhs_row + 8 * t : rhs_row + 8 * t + 8] for t in range(tiles)], axis=1)
    skip = RANK * (level % 2)
    pivot_rhs = jnp.where(is_upper, got_rhs, own_rhs)[:, skip : skip + RANK]
    for position in range(PIECES[level + 1]):
        one, zero, valid = places.next_piece(position)
        index = one * places.zeros + zero
        product = wide_mul(lower_of(places.inner + one), upper_of(places.inner + zero))
        block = piece(own, index, count) + piece(got, index, count) - folded(product)
        send[RANK // 2 * position : RANK // 2 * (position + 1)] = jnp.where(valid, block, 0.0)
    rights = []
    lefts = []
    for k in range(places.count):
        zeros_before = k - places.ones_before[k]
        right = upper_of(places.inner + zeros_before)
        rights.append(jnp.where(places.bits[k] == 0, right, 0.0))
        theirs = unfolded(piece(got, places.inner + places.ones_before[k], count))
        lefts.append(jnp.where(is_upper & (places.bits[k] == 1), theirs, 0.0))
    blank = jnp.zeros((RANK, RANK + skip), f32)
    product = wide_mul(pivot_rhs, jnp.concatenate([blank, *rights], axis=1))
    rhs = own_rhs + got_rhs - product
    skip_tiles = level % 2
    for t in range(skip_tiles, tiles):
        row = RANK // 2 * PIECES[level + 1] + 8 * (t - skip_tiles)
        send[row : row + 8] = rhs[:, 2 * RANK * t : 2 * RANK * (t + 1)]
    lefts.append(jnp.where(is_upper, pivot_rhs, 0.0))
    left[...] = jnp.concatenate(lefts, axis=0)


def coefficients(left, t):
    if t is None:
        return -left
    return jnp.concatenate([t[RANK:] - wide_mul(left, t[:RANK]), -left], axis=1)


def coefficient_kernel(*refs):
    t = None
    for left in refs[:-1]:
        t = coefficients(left[...], t)
    refs[-1][...] = t


def basis_kernel(left, t_ref, mapped, base, out):
    t = coefficients(left[...], t_ref[...])
    w = mapped[...]
    high, low = halves(t)
    rows = t.shape[0]
    product = mul(jnp.concatenate([high, low], axis=0), w[: t.shape[1]])
    product = product[:rows] + product[rows:]
    out[: 2 * RANK] = w[4 * RANK :].astype(f32) + product[: 2 * RANK]
    out[2 * RANK :] = base[...] + product[2 * RANK :]


def late_kernel(left, basis, high_low, shifted):
    update = basis[RANK:] - wide_mul(left[...], basis[:RANK])
    high, low = halves(update[:RANK])
    high_low[:RANK] = high
    high_low[RANK : 2 * RANK] = low
    high_low[2 * RANK :] = high
    shifted[...] = update[RANK:]


def last_kernel(got, high_low, shifted, out):
    value = jnp.where(upper(5), got[:, RANK:], 0.0)
    high, low = halves(value)
    out[...] = shifted[...] - mul(jnp.concatenate([high, high, low], axis=1), high_low[...])


def send_shape(level):
    return (RANK // 2 * PIECES[level] + 8 * (LEVELS // 2 - level // 2), 2 * RANK)


def call(kernel, name, outs, *args, after=()):
    vmem = pl.BlockSpec(memory_space=pltpu.VMEM)
    count = len(args)

    def body(*refs):
        kernel(*refs[:count], *refs[count + len(after) :])

    return pl.pallas_call(
        body,
        name=name,
        in_specs=[vmem] * count + [pl.BlockSpec(memory_space=pl.ANY)] * len(after),
        out_specs=[vmem] * len(outs),
        out_shape=[jax.ShapeDtypeStruct(s, t) for s, t in outs],
        compiler_params=pltpu.CompilerParams(vmem_limit_bytes=16 << 20),
    )(*args, *after)


def swapped(x, distance):
    return lax.ppermute(x, "leaf", [(i, i ^ distance) for i in range(lax.axis_size("leaf"))])


def on_device(rhs_vectors, diag_inverse, left_factors, right_factors, ranks):
    size = diag_inverse.shape[0]
    vmem = pl.BlockSpec(memory_space=pltpu.VMEM)
    hbm = pl.BlockSpec(memory_space=pltpu.HBM)
    mapped, base, send = pl.pallas_call(
        first_kernel,
        name="first",
        in_specs=[pl.BlockSpec(memory_space=pltpu.SMEM), hbm, hbm, hbm, hbm],
        out_specs=[vmem] * 3,
        out_shape=[
            jax.ShapeDtypeStruct((STATE, size), bf16),
            jax.ShapeDtypeStruct((8, size), f32),
            jax.ShapeDtypeStruct(send_shape(0), f32),
        ],
        scratch_shapes=[
            pltpu.VMEM((size, size), bf16),
            pltpu.VMEM((size, STATE), bf16),
            pltpu.VMEM((size, STATE), bf16),
            pltpu.VMEM((8, size), bf16),
            pltpu.VMEM((STATE + 16, size), bf16),
            pltpu.VMEM((STATE + 24, STATE), f32),
            pltpu.VMEM((8, STATE), f32),
            pltpu.SemaphoreType.DMA((size // CHUNK + 3,)),
        ],
        compiler_params=pltpu.CompilerParams(vmem_limit_bytes=40 << 20),
    )(
        *(
            pltpu.with_memory_space_constraint(a, pltpu.HBM)
            for a in (ranks, rhs_vectors, diag_inverse, left_factors, right_factors)
        ),
    )
    lefts = []
    basis = t = None
    for level in range(LEVELS - 1):
        got = swapped(send, PARTNER[level])
        after = ()
        if level == 3:
            (t,) = after = call(coefficient_kernel, "coefficients", [((3 * RANK + 8, 3 * RANK), f32)], *lefts)
        if level == 4:
            (basis,) = after = call(
                basis_kernel, "basis", [((2 * RANK + 8, size), f32)], lefts[3], t, mapped, base
            )
        send, left = call(
            lambda *refs, level=level: level_kernel(level, *refs),
            f"level_{level}",
            [(send_shape(level + 1), f32), ((RANK * (LEVELS - 1 - level) + 8, RANK), f32)],
            send,
            got,
            after=after,
        )
        lefts.append(left)
    got = swapped(send, PARTNER[LEVELS - 1])
    high_low, shifted = call(
        late_kernel, "late", [((3 * RANK, size), bf16), ((8, size), f32)], lefts[4], basis
    )
    (out,) = call(last_kernel, "last", [((8, size), f32)], got, high_low, shifted)
    return out


def solution(mesh):
    in_specs = (P("rhs", "leaf"), P("leaf", None), P("leaf", None), P("leaf", None), P())
    out_specs = P("rhs", "leaf")
    return jax.shard_map(
        on_device, mesh=mesh, in_specs=in_specs, out_specs=out_specs, check_vma=False
    )
```

time: 49.7 us -> 40.5 us (0.81)
  waiting for transfers between devices: 22.5 us -> 13 us
  starting transfers between devices: 14.3 us -> 15.1 us
    ppermute x9 -> x6, waiting for transfers between devices: 22.5 us -> 13 us  [swapped(): lax.ppermute(x, 'leaf', [(i, i ^ distance) for i in range(lax.axis_size('...]
    ppermute x9 -> x6, starting transfers between devices: 14.3 us -> 15.1 us  [swapped(): lax.ppermute(x, 'leaf', [(i, i ^ distance) for i in range(lax.axis_size('...]
  transfers between devices with their start and end apart: 9 -> 6, of which waited for: 9 -> 6; matrix products, arithmetic and copies ran while one was open for 0% -> 0% of each run, Pallas kernels for 3% -> 3%
where the time goes in v4:
time: 40.5 us; the launch traced here: 40.4 us
  starting transfers between devices  15.1 us (37%)
  waiting for transfers between devices  13 us (32%)
  Pallas kernels  12.3 us (30%)
    ppermute x6, starting transfers between devices, swapped(): lax.ppermute(x, 'leaf', [(i, i ^ distance) for i in range(lax.axis_size('...  15.1 us
    ppermute x6, waiting for transfers between devices, swapped(): lax.ppermute(x, 'leaf', [(i, i ^ distance) for i in range(lax.axis_size('...  13 us
    pallas_call x1, Pallas kernels, on_device(): pl.pallas_call(first_kernel, name='first', in_specs=[pl.BlockSpec(memory_...  8.38 us
    pallas_call x9, Pallas kernels, call(): pl.pallas_call(body, name=name, in_specs=[vmem] * count + [pl.BlockSpec(m...  3.9 us
  transfers between devices with their start and end apart: 6, of which 6 were waited for; matrix products, arithmetic and copies ran while one was open for 0% of the time, Pallas kernels for 3%

profile of v4, /device:TPU:32, one launch (start us, length us, event | category | flops | bytes accessed | tf_op | source)
XLA Modules:
  0.0 40.4 jit_solution(8497263293888179145)
XLA Ops:
  0.0 8.4 %first.1 = (bf16[384,2048]{1,0:T(8,128)(2,1)S(1)}, f32[8,2048]{1,0:T(8,128)S(1)}, f32[312,128]{1,0:T(8,128)S(1)}) custom-call(s32[6]{0:T(128)} %ranks.1, bf16[8,2048]{1,0:T(8,128)(2,1)} %b_hbm.1, bf16[2048,2048]{1,0:T(8,128)(2,1)} %d_hbm.1, bf16[2048,384]{1,0:T(8,128)(2,1)} %u_hbm.1, bf16[2048,384]{1,0:T(8,128)(2,1)} %v_hbm.1), custom_call_target="tpu_custom_call" | custom-call | tf_op jit(solution)/shard_map/first/pallas_call | solution.py:258
  8.4 0.1 collective-permute-start
  8.5 1.4 %collective-permute-done.refs_1_ = f32[312,128]{1,0:T(8,128)S(1)} collective-permute-done((f32[312,128]{1,0:T(8,128)S(1)}, f32[312,128]{1,0:T(8,128)S(1)}, u32[]{:S(2)}, u32[]{:S(2)}) %collective-permute-start) | collective-permute-done | bytes 159776 | tf_op jit(solution)/shard_map/ppermute | solution.py:251
  9.9 0.4 %level_0.1 = (f32[216,128]{1,0:T(8,128)S(1)}, f32[328,64]{1,0:T(8,128)S(1)}) custom-call(f32[312,128]{1,0:T(8,128)S(1)} %get-tuple-element.20.refs_0_, f32[312,128]{1,0:T(8,128)S(1)} %collective-permute-done.refs_1_), custom_call_target="tpu_custom_call" | custom-call | tf_op jit(solution)/shard_map/level_0/pallas_call | solution.py:240
  10.3 1.9 %collective-permute-start.1 = (f32[216,128]{1,0:T(8,128)S(1)}, f32[216,128]{1,0:T(8,128)S(1)}, u32[]{:S(2)}, u32[]{:S(2)}) collective-permute-start(f32[216,128]{1,0:T(8,128)S(1)} %get-tuple-element.21.refs_0_), channel_id=1, source_target_pairs={{0,8},{4,12},{8,0},{12,4},{16,24},{20,28},{24,16},{28,20},{32,40},... | collective-permute-start | bytes 331784 | tf_op jit(solution)/shard_map/ppermute | solution.py:251
  12.2 3.4 %collective-permute-done.1.refs_1_ = f32[216,128]{1,0:T(8,128)S(1)} collective-permute-done((f32[216,128]{1,0:T(8,128)S(1)}, f32[216,128]{1,0:T(8,128)S(1)}, u32[]{:S(2)}, u32[]{:S(2)}) %collective-permute-start.1) | collective-permute-done | bytes 110624 | tf_op jit(solution)/shard_map/ppermute | solution.py:251
  15.6 0.4 level_1.1
  15.9 3.3 %collective-permute-start.2 = (f32[144,128]{1,0:T(8,128)S(1)}, f32[144,128]{1,0:T(8,128)S(1)}, u32[]{:S(2)}, u32[]{:S(2)}) collective-permute-start(f32[144,128]{1,0:T(8,128)S(1)} %get-tuple-element.22.refs_0_), channel_id=1, source_target_pairs={{0,16},{4,20},{8,24},{12,28},{16,0},{20,4},{24,8},{28,12},{32,48},... | collective-permute-start | bytes 221192 | tf_op jit(solution)/shard_map/ppermute | solution.py:251
  19.2 2.5 %collective-permute-done.2.refs_1_ = f32[144,128]{1,0:T(8,128)S(1)} collective-permute-done((f32[144,128]{1,0:T(8,128)S(1)}, f32[144,128]{1,0:T(8,128)S(1)}, u32[]{:S(2)}, u32[]{:S(2)}) %collective-permute-start.2) | collective-permute-done | bytes 73760 | tf_op jit(solution)/shard_map/ppermute | solution.py:251
  21.7 0.3 level_2.1
  22.0 5.9 %collective-permute-start.3 = (f32[80,128]{1,0:T(8,128)S(1)}, f32[80,128]{1,0:T(8,128)S(1)}, u32[]{:S(2)}, u32[]{:S(2)}) collective-permute-start(f32[80,128]{1,0:T(8,128)S(1)} %get-tuple-element.23.refs_0_), channel_id=1, source_target_pairs={{0,48},{4,52},{8,56},{12,60},{16,32},{20,36},{24,40},{28,44},{32,1... | collective-permute-start | bytes 122888 | tf_op jit(solution)/shard_map/ppermute | solution.py:251
  27.9 0.4 coefficients.1.refs_2_.refs_1_
  28.3 1.9 %collective-permute-done.3.refs_1_ = f32[80,128]{1,0:T(8,128)S(1)} collective-permute-done((f32[80,128]{1,0:T(8,128)S(1)}, f32[80,128]{1,0:T(8,128)S(1)}, u32[]{:S(2)}, u32[]{:S(2)}) %collective-permute-start.3) | collective-permute-done | bytes 40992 | tf_op jit(solution)/shard_map/ppermute | solution.py:251
  30.2 0.3 level_3.1
  30.5 1.4 %collective-permute-start.4 = (f32[40,128]{1,0:T(8,128)S(1)}, f32[40,128]{1,0:T(8,128)S(1)}, u32[]{:S(2)}, u32[]{:S(2)}) collective-permute-start(f32[40,128]{1,0:T(8,128)S(1)} %get-tuple-element.27.refs_0_), channel_id=1, source_target_pairs={{0,64},{4,68},{8,72},{12,76},{16,80},{20,84},{24,88},{28,92},{32,9... | collective-permute-start | bytes 61448 | tf_op jit(solution)/shard_map/ppermute | solution.py:251
  31.9 0.6 %basis.1.refs_2_.refs_1_ = f32[136,2048]{1,0:T(8,128)S(1)} custom-call(f32[136,64]{1,0:T(8,128)S(1)} %get-tuple-element.28.refs_0_, f32[200,192]{1,0:T(8,128)S(1)} %coefficients.1.refs_2_.refs_1_, bf16[384,2048]{1,0:T(8,128)(2,1)S(1)} %get-tuple-element.29.refs_2_, f32[8,2048]{1,0:T(8,128)S(1)} %get-tuple-element.30.refs_3_), custom_call_target="tpu_custom_call" | custom-call | tf_op jit(solution)/shard_map/basis/pallas_call | solution.py:240
  32.5 1.9 %collective-permute-done.4.refs_1_ = f32[40,128]{1,0:T(8,128)S(1)} collective-permute-done((f32[40,128]{1,0:T(8,128)S(1)}, f32[40,128]{1,0:T(8,128)S(1)}, u32[]{:S(2)}, u32[]{:S(2)}) %collective-permute-start.4) | collective-permute-done | bytes 20512 | tf_op jit(solution)/shard_map/ppermute | solution.py:251
  34.4 0.3 level_4.1
  34.7 2.5 %collective-permute-start.5 = (f32[8,128]{1,0:T(8,128)S(1)}, f32[8,128]{1,0:T(8,128)S(1)}, u32[]{:S(2)}, u32[]{:S(2)}) collective-permute-start(f32[8,128]{1,0:T(8,128)S(1)} %get-tuple-element.31), channel_id=1, source_target_pairs={{0,192},{4,196},{8,200},{12,204},{16,208},{20,212},{24,216},{28,22... | collective-permute-start | bytes 12296 | tf_op jit(solution)/shard_map/ppermute | solution.py:251
  37.2 0.3 late.1
  37.5 2.0 %collective-permute-done.5.refs_0_ = f32[8,128]{1,0:T(8,128)S(1)} collective-permute-done((f32[8,128]{1,0:T(8,128)S(1)}, f32[8,128]{1,0:T(8,128)S(1)}, u32[]{:S(2)}, u32[]{:S(2)}) %collective-permute-start.5) | collective-permute-done | bytes 4128 | tf_op jit(solution)/shard_map/ppermute | solution.py:251
  39.5 0.9 %last.1 = f32[8,2048]{1,0:T(8,128)} custom-call(f32[8,128]{1,0:T(8,128)S(1)} %collective-permute-done.5.refs_0_, bf16[192,2048]{1,0:T(8,128)(2,1)S(1)} %get-tuple-element.33.refs_1_, f32[8,2048]{1,0:T(8,128)S(1)} %get-tuple-element.34.refs_2_), custom_call_target="tpu_custom_call" | custom-call | tf_op jit(solution)/shard_map/last/pallas_call | solution.py:240
Async XLA Ops:
  8.4 1.5 %collective-permute-start = (f32[312,128]{1,0:T(8,128)S(1)}, f32[312,128]{1,0:T(8,128)S(1)}, u32[]{:S(2)}, u32[]{:S(2)}) collective-permute-start(f32[312,128]{1,0:T(8,128)S(1)} %get-tuple-element.20.refs_0_), channel_id=1, source_target_pairs={{0,4},{4,0},{8,12},{12,8},{16,20},{20,16},{24,28},{28,24},{32,36},... | collective-permute-start | bytes 479240 | tf_op jit(solution)/shard_map/ppermute | solution.py:251
  10.3 5.3 %collective-permute-start.1 = (f32[216,128]{1,0:T(8,128)S(1)}, f32[216,128]{1,0:T(8,128)S(1)}, u32[]{:S(2)}, u32[]{:S(2)}) collective-permute-start(f32[216,128]{1,0:T(8,128)S(1)} %get-tuple-element.21.refs_0_), channel_id=1, source_target_pairs={{0,8},{4,12},{8,0},{12,4},{16,24},{20,28},{24,16},{28,20},{32,40},... | collective-permute-start | bytes 331784 | tf_op jit(solution)/shard_map/ppermute | solution.py:251
  15.9 5.7 %collective-permute-start.2 = (f32[144,128]{1,0:T(8,128)S(1)}, f32[144,128]{1,0:T(8,128)S(1)}, u32[]{:S(2)}, u32[]{:S(2)}) collective-permute-start(f32[144,128]{1,0:T(8,128)S(1)} %get-tuple-element.22.refs_0_), channel_id=1, source_target_pairs={{0,16},{4,20},{8,24},{12,28},{16,0},{20,4},{24,8},{28,12},{32,48},... | collective-permute-start | bytes 221192 | tf_op jit(solution)/shard_map/ppermute | solution.py:251
  22.0 8.2 %collective-permute-start.3 = (f32[80,128]{1,0:T(8,128)S(1)}, f32[80,128]{1,0:T(8,128)S(1)}, u32[]{:S(2)}, u32[]{:S(2)}) collective-permute-start(f32[80,128]{1,0:T(8,128)S(1)} %get-tuple-element.23.refs_0_), channel_id=1, source_target_pairs={{0,48},{4,52},{8,56},{12,60},{16,32},{20,36},{24,40},{28,44},{32,1... | collective-permute-start | bytes 122888 | tf_op jit(solution)/shard_map/ppermute | solution.py:251
  30.5 3.9 %collective-permute-start.4 = (f32[40,128]{1,0:T(8,128)S(1)}, f32[40,128]{1,0:T(8,128)S(1)}, u32[]{:S(2)}, u32[]{:S(2)}) collective-permute-start(f32[40,128]{1,0:T(8,128)S(1)} %get-tuple-element.27.refs_0_), channel_id=1, source_target_pairs={{0,64},{4,68},{8,72},{12,76},{16,80},{20,84},{24,88},{28,92},{32,9... | collective-permute-start | bytes 61448 | tf_op jit(solution)/shard_map/ppermute | solution.py:251
  34.7 4.8 %collective-permute-start.5 = (f32[8,128]{1,0:T(8,128)S(1)}, f32[8,128]{1,0:T(8,128)S(1)}, u32[]{:S(2)}, u32[]{:S(2)}) collective-permute-start(f32[8,128]{1,0:T(8,128)S(1)} %get-tuple-element.31), channel_id=1, source_target_pairs={{0,192},{4,196},{8,200},{12,204},{16,208},{20,212},{24,216},{28,22... | collective-permute-start | bytes 12296 | tf_op jit(solution)/shard_map/ppermute | solution.py:251

commit v5 on v4

--- a/solution.py
+++ b/solution.py
@@ -13,8 +13,8 @@
 LEVELS = 6
 STATE = RANK * LEVELS
 CHUNK = 512
-PARTNER = (1, 2, 4, 12, 16, 48)
-PIECES = (9, 6, 4, 2, 1, 0)
+PARTNER = (1, 2, 4, 12)
+PIECES = (9, 6, 4, 2, 1)
 
 
 def mul(a, b, dims=NN):
@@ -200,30 +200,35 @@
     refs[-1][...] = t
 
 
-def basis_kernel(left, t_ref, mapped, base, out):
+def basis_kernel(left, t_ref, mapped, base, high_low, shifted):
     t = coefficients(left[...], t_ref[...])
     w = mapped[...]
     high, low = halves(t)
     rows = t.shape[0]
     product = mul(jnp.concatenate([high, low], axis=0), w[: t.shape[1]])
     product = product[:rows] + product[rows:]
-    out[: 2 * RANK] = w[4 * RANK :].astype(f32) + product[: 2 * RANK]
-    out[2 * RANK :] = base[...] + product[2 * RANK :]
-
-
-def late_kernel(left, basis, high_low, shifted):
-    update = basis[RANK:] - wide_mul(left[...], basis[:RANK])
-    high, low = halves(update[:RANK])
-    high_low[:RANK] = high
-    high_low[RANK : 2 * RANK] = low
-    high_low[2 * RANK :] = high
-    shifted[...] = update[RANK:]
-
-
-def last_kernel(got, high_low, shifted, out):
-    value = jnp.where(upper(5), got[:, RANK:], 0.0)
-    high, low = halves(value)
-    out[...] = shifted[...] - mul(jnp.concatenate([high, high, low], axis=1), high_low[...])
+    high, low = halves(w[4 * RANK :].astype(f32) + product[: 2 * RANK])
+    high_low[: 2 * RANK] = high
+    high_low[2 * RANK :] = low
+    shifted[...] = base[...] + product[2 * RANK :]
+
+
+def last_kernel(near, far, across, high_low, shifted, out):
+    group = lax.axis_index("leaf") >> 4 & 3
+    half = RANK // 2
+    zero = jnp.where(group == 1, near[half:], jnp.where(group == 2, far[half:], across[half:]))
+    one = jnp.where(group == 2, across[...], far[...])
+    two = near[...]
+    value_5 = zero[:, RANK:] + one[half:, RANK:] - wide_mul(zero[:, :RANK], unfolded(one[:half]))
+    value_5 = jnp.where(group >= 2, value_5, 0.0)
+    value_4 = two[half:, :RANK] - wide_mul(value_5, unfolded(two[:half]))
+    value_4 = jnp.where(group == 3, value_4, jnp.where(group == 1, zero[:, :RANK], 0.0))
+    high, low = halves(jnp.concatenate([value_4, value_5], axis=1))
+    joined = jnp.concatenate(
+        [jnp.concatenate([high, high], axis=1), jnp.concatenate([low, low], axis=1)], axis=0
+    )
+    product = mul(joined, high_low[...])
+    out[...] = shifted[...] - (product[:8] + product[8:])
 
 
 def send_shape(level):
@@ -249,6 +254,11 @@
 
 def swapped(x, distance):
     return lax.ppermute(x, "leaf", [(i, i ^ distance) for i in range(lax.axis_size("leaf"))])
+
+
+def raised(x, distance):
+    pairs = [(i, i ^ distance) for i in range(lax.axis_size("leaf"))]
+    return lax.ppermute(x, "leaf", [(i, j) for i, j in pairs if i < j])
 
 
 def on_device(rhs_vectors, diag_inverse, left_factors, right_factors, ranks):
@@ -283,16 +293,11 @@
         ),
     )
     lefts = []
-    basis = t = None
-    for level in range(LEVELS - 1):
+    for level in range(4):
         got = swapped(send, PARTNER[level])
         after = ()
         if level == 3:
             (t,) = after = call(coefficient_kernel, "coefficients", [((3 * RANK + 8, 3 * RANK), f32)], *lefts)
-        if level == 4:
-            (basis,) = after = call(
-                basis_kernel, "basis", [((2 * RANK + 8, size), f32)], lefts[3], t, mapped, base
-            )
         send, left = call(
             lambda *refs, level=level: level_kernel(level, *refs),
             f"level_{level}",
@@ -302,11 +307,11 @@
             after=after,
         )
         lefts.append(left)
-    got = swapped(send, PARTNER[LEVELS - 1])
+    far, across, near = raised(send, 32), raised(send, 48), raised(send, 16)
     high_low, shifted = call(
-        late_kernel, "late", [((3 * RANK, size), bf16), ((8, size), f32)], lefts[4], basis
-    )
-    (out,) = call(last_kernel, "last", [((8, size), f32)], got, high_low, shifted)
+        basis_kernel, "basis", [((4 * RANK, size), bf16), ((8, size), f32)], lefts[3], t, mapped, base
+    )
+    (out,) = call(last_kernel, "last", [((8, size), f32)], near, far, across, high_low, shifted)
     return out
 
 

time: 40.5 us -> 42.8 us (1.057)
  the two profiles are of different devices: /device:TPU:32 before, /device:TPU:10 now
where the time goes in v5:
time: 42.8 us; the launch traced here: 42.7 us
  starting transfers between devices  16.7 us (39%)
  waiting for transfers between devices  13.7 us (32%)
  Pallas kernels  12.2 us (29%)
    ppermute x4, starting transfers between devices, swapped(): lax.ppermute(x, 'leaf', [(i, i ^ distance) for i in range(lax.axis_size('...  10.1 us
    ppermute x4, waiting for transfers between devices, swapped(): lax.ppermute(x, 'leaf', [(i, i ^ distance) for i in range(lax.axis_size('...  10 us
    pallas_call x1, Pallas kernels, on_device(): pl.pallas_call(first_kernel, name='first', in_specs=[pl.BlockSpec(memory_...  8.38 us
    ppermute x3, starting transfers between devices, raised(): return lax.ppermute(x, 'leaf', [(i, j) for i, j in pairs if i < j])  6.64 us
    pallas_call x7, Pallas kernels, call(): pl.pallas_call(body, name=name, in_specs=[vmem] * count + [pl.BlockSpec(m...  3.78 us
    ppermute x3, waiting for transfers between devices, raised(): return lax.ppermute(x, 'leaf', [(i, j) for i, j in pairs if i < j])  3.7 us
  transfers between devices with their start and end apart: 7, of which 5 were waited for; matrix products, arithmetic and copies ran while one was open for 0% of the time, Pallas kernels for 2%

profile of v5, /device:TPU:10, one launch (start us, length us, event | category | flops | bytes accessed | tf_op | source)
XLA Modules:
  0.0 42.7 jit_solution(2358090944923287358)
XLA Ops:
  0.0 8.4 %first.1 = (bf16[384,2048]{1,0:T(8,128)(2,1)S(1)}, f32[8,2048]{1,0:T(8,128)S(1)}, f32[312,128]{1,0:T(8,128)S(1)}) custom-call(s32[6]{0:T(128)} %ranks.1, bf16[8,2048]{1,0:T(8,128)(2,1)} %b_hbm.1, bf16[2048,2048]{1,0:T(8,128)(2,1)} %d_hbm.1, bf16[2048,384]{1,0:T(8,128)(2,1)} %u_hbm.1, bf16[2048,384]{1,0:T(8,128)(2,1)} %v_hbm.1), custom_call_target="tpu_custom_call" | custom-call | tf_op jit(solution)/shard_map/first/pallas_call | solution.py:268
  8.4 0.1 collective-permute-start
  8.5 1.4 %collective-permute-done.refs_1_ = f32[312,128]{1,0:T(8,128)S(1)} collective-permute-done((f32[312,128]{1,0:T(8,128)S(1)}, f32[312,128]{1,0:T(8,128)S(1)}, u32[]{:S(2)}, u32[]{:S(2)}) %collective-permute-start) | collective-permute-done | bytes 159776 | tf_op jit(solution)/shard_map/ppermute | solution.py:256
  9.9 0.4 level_0.1
  10.3 2.0 %collective-permute-start.1 = (f32[216,128]{1,0:T(8,128)S(1)}, f32[216,128]{1,0:T(8,128)S(1)}, u32[]{:S(2)}, u32[]{:S(2)}) collective-permute-start(f32[216,128]{1,0:T(8,128)S(1)} %get-tuple-element.19.refs_0_), channel_id=1, source_target_pairs={{0,8},{4,12},{8,0},{12,4},{16,24},{20,28},{24,16},{28,20},{32,40},... | collective-permute-start | bytes 331784 | tf_op jit(solution)/shard_map/ppermute | solution.py:256
  12.3 3.4 %collective-permute-done.1.refs_1_ = f32[216,128]{1,0:T(8,128)S(1)} collective-permute-done((f32[216,128]{1,0:T(8,128)S(1)}, f32[216,128]{1,0:T(8,128)S(1)}, u32[]{:S(2)}, u32[]{:S(2)}) %collective-permute-start.1) | collective-permute-done | bytes 110624 | tf_op jit(solution)/shard_map/ppermute | solution.py:256
  15.7 0.4 level_1.1
  16.0 3.4 %collective-permute-start.2 = (f32[144,128]{1,0:T(8,128)S(1)}, f32[144,128]{1,0:T(8,128)S(1)}, u32[]{:S(2)}, u32[]{:S(2)}) collective-permute-start(f32[144,128]{1,0:T(8,128)S(1)} %get-tuple-element.20.refs_0_), channel_id=1, source_target_pairs={{0,16},{4,20},{8,24},{12,28},{16,0},{20,4},{24,8},{28,12},{32,48},... | collective-permute-start | bytes 221192 | tf_op jit(solution)/shard_map/ppermute | solution.py:256
  19.4 3.7 %collective-permute-done.2.refs_1_ = f32[144,128]{1,0:T(8,128)S(1)} collective-permute-done((f32[144,128]{1,0:T(8,128)S(1)}, f32[144,128]{1,0:T(8,128)S(1)}, u32[]{:S(2)}, u32[]{:S(2)}) %collective-permute-start.2) | collective-permute-done | bytes 73760 | tf_op jit(solution)/shard_map/ppermute | solution.py:256
  23.1 0.3 level_2.1
  23.4 4.6 %collective-permute-start.3 = (f32[80,128]{1,0:T(8,128)S(1)}, f32[80,128]{1,0:T(8,128)S(1)}, u32[]{:S(2)}, u32[]{:S(2)}) collective-permute-start(f32[80,128]{1,0:T(8,128)S(1)} %get-tuple-element.21.refs_0_), channel_id=1, source_target_pairs={{0,48},{4,52},{8,56},{12,60},{16,32},{20,36},{24,40},{28,44},{32,1... | collective-permute-start | bytes 122888 | tf_op jit(solution)/shard_map/ppermute | solution.py:256
  28.0 0.4 coefficients.1.refs_2_.refs_1_
  28.4 1.6 %collective-permute-done.3.refs_1_ = f32[80,128]{1,0:T(8,128)S(1)} collective-permute-done((f32[80,128]{1,0:T(8,128)S(1)}, f32[80,128]{1,0:T(8,128)S(1)}, u32[]{:S(2)}, u32[]{:S(2)}) %collective-permute-start.3) | collective-permute-done | bytes 40992 | tf_op jit(solution)/shard_map/ppermute | solution.py:256
  30.0 0.3 level_3.1
  30.3 3.4 %collective-permute-start.6 = (f32[40,128]{1,0:T(8,128)S(1)}, f32[40,128]{1,0:T(8,128)S(1)}, u32[]{:S(2)}, u32[]{:S(2)}) collective-permute-start(f32[40,128]{1,0:T(8,128)S(1)} %get-tuple-element.25), channel_id=1, source_target_pairs={{0,192},{4,196},{8,200},{12,204},{16,208},{20,212},{24,216},{28,22... | collective-permute-start | bytes 61448 | tf_op jit(solution)/shard_map/ppermute | solution.py:261
  33.7 1.9 %collective-permute-start.5 = (f32[40,128]{1,0:T(8,128)S(1)}, f32[40,128]{1,0:T(8,128)S(1)}, u32[]{:S(2)}, u32[]{:S(2)}) collective-permute-start(f32[40,128]{1,0:T(8,128)S(1)} %get-tuple-element.25), channel_id=1, source_target_pairs={{0,128},{4,132},{8,136},{12,140},{16,144},{20,148},{24,152},{28,15... | collective-permute-start | bytes 61448 | tf_op jit(solution)/shard_map/ppermute | solution.py:261
  35.7 1.3 %collective-permute-start.4 = (f32[40,128]{1,0:T(8,128)S(1)}, f32[40,128]{1,0:T(8,128)S(1)}, u32[]{:S(2)}, u32[]{:S(2)}) collective-permute-start(f32[40,128]{1,0:T(8,128)S(1)} %get-tuple-element.25), channel_id=1, source_target_pairs={{0,64},{4,68},{8,72},{12,76},{16,80},{20,84},{24,88},{28,92},{32,9... | collective-permute-start | bytes 61448 | tf_op jit(solution)/shard_map/ppermute | solution.py:261
  37.0 0.7 %basis.1 = (bf16[256,2048]{1,0:T(8,128)(2,1)S(1)}, f32[8,2048]{1,0:T(8,128)S(1)}) custom-call(f32[136,64]{1,0:T(8,128)S(1)} %get-tuple-element.26.refs_0_, f32[200,192]{1,0:T(8,128)S(1)} %coefficients.1.refs_2_.refs_1_, bf16[384,2048]{1,0:T(8,128)(2,1)S(1)} %get-tuple-element.27.refs_2_, f32[8,2048]{1,0:T(8,128)S(1)} %get-tuple-element.28.refs_3_), custom_call_target="tpu_custom_call" | custom-call | tf_op jit(solution)/shard_map/basis/pallas_call | solution.py:245
  37.6 0.0 collective-permute-done.6.refs_2_
  37.6 0.0 collective-permute-done.5.refs_1_
  37.7 3.7 %collective-permute-done.4.refs_0_ = f32[40,128]{1,0:T(8,128)S(1)} collective-permute-done((f32[40,128]{1,0:T(8,128)S(1)}, f32[40,128]{1,0:T(8,128)S(1)}, u32[]{:S(2)}, u32[]{:S(2)}) %collective-permute-start.4) | collective-permute-done | bytes 20512 | tf_op jit(solution)/shard_map/ppermute | solution.py:261
  41.4 1.3 %last.1 = f32[8,2048]{1,0:T(8,128)} custom-call(f32[40,128]{1,0:T(8,128)S(1)} %collective-permute-done.4.refs_0_, f32[40,128]{1,0:T(8,128)S(1)} %collective-permute-done.5.refs_1_, f32[40,128]{1,0:T(8,128)S(1)} %collective-permute-done.6.refs_2_, bf16[256,2048]{1,0:T(8,128)(2,1)S(1)} %get-tuple-element.29.refs_3_, f32[8,2048]{1,0:T(8,128)S(1)} %get-tuple-element.30.refs_4_), custom_call_target="tpu_custom_call" | custom-call | tf_op jit(solution)/shard_map/last/pallas_call | solution.py:245
Async XLA Ops:
  8.4 1.5 %collective-permute-start = (f32[312,128]{1,0:T(8,128)S(1)}, f32[312,128]{1,0:T(8,128)S(1)}, u32[]{:S(2)}, u32[]{:S(2)}) collective-permute-start(f32[312,128]{1,0:T(8,128)S(1)} %get-tuple-element.18.refs_0_), channel_id=1, source_target_pairs={{0,4},{4,0},{8,12},{12,8},{16,20},{20,16},{24,28},{28,24},{32,36},... | collective-permute-start | bytes 479240 | tf_op jit(solution)/shard_map/ppermute | solution.py:256
  10.3 5.4 %collective-permute-start.1 = (f32[216,128]{1,0:T(8,128)S(1)}, f32[216,128]{1,0:T(8,128)S(1)}, u32[]{:S(2)}, u32[]{:S(2)}) collective-permute-start(f32[216,128]{1,0:T(8,128)S(1)} %get-tuple-element.19.refs_0_), channel_id=1, source_target_pairs={{0,8},{4,12},{8,0},{12,4},{16,24},{20,28},{24,16},{28,20},{32,40},... | collective-permute-start | bytes 331784 | tf_op jit(solution)/shard_map/ppermute | solution.py:256
  16.0 7.0 %collective-permute-start.2 = (f32[144,128]{1,0:T(8,128)S(1)}, f32[144,128]{1,0:T(8,128)S(1)}, u32[]{:S(2)}, u32[]{:S(2)}) collective-permute-start(f32[144,128]{1,0:T(8,128)S(1)} %get-tuple-element.20.refs_0_), channel_id=1, source_target_pairs={{0,16},{4,20},{8,24},{12,28},{16,0},{20,4},{24,8},{28,12},{32,48},... | collective-permute-start | bytes 221192 | tf_op jit(solution)/shard_map/ppermute | solution.py:256
  23.4 6.6 %collective-permute-start.3 = (f32[80,128]{1,0:T(8,128)S(1)}, f32[80,128]{1,0:T(8,128)S(1)}, u32[]{:S(2)}, u32[]{:S(2)}) collective-permute-start(f32[80,128]{1,0:T(8,128)S(1)} %get-tuple-element.21.refs_0_), channel_id=1, source_target_pairs={{0,48},{4,52},{8,56},{12,60},{16,32},{20,36},{24,40},{28,44},{32,1... | collective-permute-start | bytes 122888 | tf_op jit(solution)/shard_map/ppermute | solution.py:256
  30.3 7.3 %collective-permute-start.6 = (f32[40,128]{1,0:T(8,128)S(1)}, f32[40,128]{1,0:T(8,128)S(1)}, u32[]{:S(2)}, u32[]{:S(2)}) collective-permute-start(f32[40,128]{1,0:T(8,128)S(1)} %get-tuple-element.25), channel_id=1, source_target_pairs={{0,192},{4,196},{8,200},{12,204},{16,208},{20,212},{24,216},{28,22... | collective-permute-start | bytes 61448 | tf_op jit(solution)/shard_map/ppermute | solution.py:261
  33.7 3.9 %collective-permute-start.5 = (f32[40,128]{1,0:T(8,128)S(1)}, f32[40,128]{1,0:T(8,128)S(1)}, u32[]{:S(2)}, u32[]{:S(2)}) collective-permute-start(f32[40,128]{1,0:T(8,128)S(1)} %get-tuple-element.25), channel_id=1, source_target_pairs={{0,128},{4,132},{8,136},{12,140},{16,144},{20,148},{24,152},{28,15... | collective-permute-start | bytes 61448 | tf_op jit(solution)/shard_map/ppermute | solution.py:261
  35.7 5.7 %collective-permute-start.4 = (f32[40,128]{1,0:T(8,128)S(1)}, f32[40,128]{1,0:T(8,128)S(1)}, u32[]{:S(2)}, u32[]{:S(2)}) collective-permute-start(f32[40,128]{1,0:T(8,128)S(1)} %get-tuple-element.25), channel_id=1, source_target_pairs={{0,64},{4,68},{8,72},{12,76},{16,80},{20,84},{24,88},{28,92},{32,9... | collective-permute-start | bytes 61448 | tf_op jit(solution)/shard_map/ppermute | solution.py:261

commit v6 on v4

--- a/solution.py
+++ b/solution.py
@@ -89,9 +89,118 @@
     return ref[pl.ds(pl.multiple_of(RANK // 2 * index, RANK // 2), RANK // 2)]
 
 
-def first_kernel(ranks, b_hbm, d_hbm, u_hbm, v_hbm, mapped, base, send, d, u, v, b, x, acc, keeps, sems):
-    size = d.shape[0]
-    n = size // CHUNK
+def keep_row(ranks):
+    lane = lax.broadcasted_iota(jnp.int32, (8, STATE), 1)
+    keep = jnp.zeros((8, STATE), f32)
+    for level in range(LEVELS):
+        inside = (lane >= RANK * level) & (lane < RANK * level + jnp.minimum(ranks[level], RANK))
+        keep = jnp.where(inside, 1.0, keep)
+    return keep
+
+
+def turned_rhs(b):
+    wide = b[...].astype(f32)
+    gap = jnp.zeros((RANK - 8, wide.shape[1]), f32)
+    return jnp.concatenate([wide, gap, wide, gap], axis=0).T.astype(bf16)
+
+
+def few_ones(places, d, u, v, b, x, acc, rhs, copies, copy_u, copy_b, copy_v):
+    copy_u.start()
+    copy_b.start()
+    copies[0].start()
+    copy_v.start()
+    for c in copies[1:]:
+        c.start()
+    tile_0, tile_1, free = tiles_of(places)
+    copy_b.wait()
+    extra = turned_rhs(b)
+    copy_u.wait()
+    lane = lax.broadcasted_iota(jnp.int32, extra.shape, 1)
+    x[:, : 2 * RANK] = u[:, pl.ds(pl.multiple_of(2 * RANK * tile_0, 2 * RANK), 2 * RANK)]
+    second = u[:, pl.ds(pl.multiple_of(2 * RANK * tile_1, 2 * RANK), 2 * RANK)]
+    x[:, 2 * RANK :] = jnp.where(lane // RANK == free, extra, second)
+    count = len(copies)
+
+    def gather(i, joined):
+        total = mul(joined, v[CHUNK * i : CHUNK * (i + 1)])
+        if i == 0:
+            acc[: 4 * RANK + 16] = total
+        else:
+            acc[: 4 * RANK + 16] += total
+
+    joined = None
+    for i in range(count):
+        copies[i].wait()
+        if i == 1:
+            copy_v.wait()
+        middle = CHUNK * i + CHUNK // 2
+        ahead = [
+            mul(d[CHUNK * i : middle], x[...]),
+            mul(d[middle : CHUNK * (i + 1)], x[...]),
+        ]
+        if i > 0:
+            gather(i - 1, joined)
+        product = jnp.concatenate(ahead, axis=0)
+        base = product[:, 2 * RANK :].T
+        base = jnp.where(free == 1, base[RANK : RANK + 8], base[:8])
+        _, low, rest = thirds(base)
+        joined = jnp.concatenate([product.astype(bf16).T, low, rest], axis=0)
+    gather(count - 1, joined)
+    start = pl.multiple_of(2 * RANK + RANK * free, RANK)
+    rhs[...] = acc[pl.ds(start, 8)] + acc[4 * RANK : 4 * RANK + 8] + acc[4 * RANK + 8 : 4 * RANK + 16]
+
+
+def few_zeros(places, d, u, v, b, turned, z, acc, rhs, copies, copy_u, copy_b, copy_v):
+    copy_v.start()
+    copies[0].start()
+    copy_b.start()
+    for c in copies[1:]:
+        c.start()
+    copy_u.start()
+    zeros = [places.nth(n, 0) for n in range(3)]
+    copy_v.wait()
+    for i, c in enumerate(copies):
+        c.wait()
+        part = slice(CHUNK * i, CHUNK * (i + 1))
+        turned[...] = v[part].T
+        rows = [turned[pl.ds(pl.multiple_of(RANK * n, RANK), RANK)] for n in zeros]
+        product = mul(jnp.concatenate(rows, axis=0), d[part])
+        if i == 0:
+            z[...] = product
+        else:
+            z[...] += product
+    copy_b.wait()
+    copy_u.wait()
+    high, low = halves(z[...])
+    both = jnp.concatenate([high, low], axis=0)
+    product = mul(both, u[...])
+    product = product[: 3 * RANK] + product[3 * RANK :]
+    product = jnp.concatenate([product, jnp.zeros((RANK, STATE), f32)], axis=0)
+    acc[:STATE, : 4 * RANK] = product.T
+    twice = jnp.concatenate([b[...], b[...]], axis=0)
+    shares = mul(twice, both, NT)[:8]
+    shares = shares[:, : 3 * RANK] + shares[:, 3 * RANK :]
+    pieces = []
+    for k in range(LEVELS):
+        before = k - places.ones_before[k]
+        chosen = jnp.where(before == 1, shares[:, RANK : 2 * RANK], shares[:, :RANK])
+        pieces.append(jnp.where(before == 2, shares[:, 2 * RANK :], chosen))
+    rhs[...] = jnp.concatenate(pieces, axis=1)
+
+
+def tiles_of(places):
+    one_0, one_1 = places.nth(0, 1), places.nth(1, 1)
+    one_0 = jnp.where(places.ones > 0, one_0, 0)
+    one_1 = jnp.where(places.ones > 1, one_1, one_0)
+    tile_0, tile_1 = one_0 // 2, one_1 // 2
+    apart = tile_1 != tile_0
+    free = jnp.where(apart, 1 - one_1 % 2, 0)
+    tile_1 = jnp.where(apart, tile_1, (tile_0 + 1) % (LEVELS // 2))
+    return tile_0, tile_1, free
+
+
+def first_kernel(ranks, b_hbm, d_hbm, u_hbm, v_hbm, send, d, u, b, keeps, v, x, turned, z, acc, rhs, sems):
+    n = d.shape[0] // CHUNK
     copies = [
         pltpu.make_async_copy(d_hbm.at[pl.ds(CHUNK * i, CHUNK)], d.at[pl.ds(CHUNK * i, CHUNK)], sems.at[i])
         for i in range(n)
@@ -99,51 +208,46 @@
     copy_u = pltpu.make_async_copy(u_hbm, u, sems.at[n])
     copy_b = pltpu.make_async_copy(b_hbm, b, sems.at[n + 1])
     copy_v = pltpu.make_async_copy(v_hbm, v, sems.at[n + 2])
-    copy_u.start()
-    copy_b.start()
-    copies[0].start()
-    copy_v.start()
-    for c in copies[1:]:
-        c.start()
-    lane = lax.broadcasted_iota(jnp.int32, (1, STATE), 1)
-    keep = jnp.zeros((1, STATE), f32)
-    for level in range(LEVELS):
-        inside = (lane >= RANK * level) & (lane < RANK * level + jnp.minimum(ranks[level], RANK))
-        keep = jnp.where(inside, 1.0, keep)
-    keeps[...] = jnp.broadcast_to(keep, keeps.shape)
-    copy_u.wait()
-    copy_b.wait()
-    x[:STATE] = (u[...] * keep.astype(bf16)).T
-    x[STATE:] = jnp.concatenate([b[...], jnp.zeros((8, size), bf16)], axis=0)
-    for i in range(n):
-        rows = slice(CHUNK * i, CHUNK * (i + 1))
-        copies[i].wait()
-        if i == 0:
-            copy_v.wait()
-        product = mul(x[...], d[rows], NT)
-        rounded = product[:STATE].astype(bf16)
-        mapped[:, rows] = rounded
-        part = product[STATE : STATE + 8]
-        base[:, rows] = part
-        joined = jnp.concatenate([rounded, *thirds(part)], axis=0)
-        total = mul(joined, v[rows])
-        if i == 0:
-            acc[...] = total
-        else:
-            acc[...] += total
-    rhs = (acc[STATE : STATE + 8] + acc[STATE + 8 : STATE + 16] + acc[STATE + 16 :]) * keep
     places = Places(-1)
+    few = places.ones <= 2
+
+    @pl.when(few)
+    def _():
+        few_ones(places, d, u, v, b, x, acc, rhs, copies, copy_u, copy_b, copy_v)
+
+    @pl.when(jnp.logical_not(few))
+    def _():
+        few_zeros(places, d, u, v, b, turned, z, acc, rhs, copies, copy_u, copy_b, copy_v)
+
+    keeps[...] = keep_row(ranks)
+    tile_0, _, _ = tiles_of(places)
+    row_id = lax.broadcasted_iota(jnp.int32, (RANK, RANK), 0)
+    lane_id = lax.broadcasted_iota(jnp.int32, (RANK, RANK), 1)
     for position in range(PIECES[0]):
         one, zero, valid = places.next_piece(position)
-        m, lane_piece = places.nth(one, 1), places.nth(zero, 0)
-        rows = pl.ds(pl.multiple_of(RANK * m, RANK), RANK)
+        m, l = places.nth(one, 1), places.nth(zero, 0)
+        start = jnp.where(few, jnp.where(m // 2 == tile_0, 0, 2 * RANK) + RANK * (m % 2), RANK * m)
+        lane_piece = jnp.where(few, l, jnp.minimum(zero, 2))
+        rows = pl.ds(pl.multiple_of(start, RANK), RANK)
         lanes = pl.ds(pl.multiple_of(2 * RANK * (lane_piece // 2), 2 * RANK), 2 * RANK)
-        tile = acc[rows, lanes] * keeps[:1, lanes]
+        tile = acc[rows, lanes]
         block = jnp.where(lane_piece % 2 == 1, tile[:, RANK:], tile[:, :RANK])
-        send[RANK // 2 * position : RANK // 2 * (position + 1)] = folded(jnp.where(valid, block, 0.0))
+        used = (row_id < ranks[m]) & (lane_id < jnp.where(valid, ranks[l], 0))
+        send[RANK // 2 * position : RANK // 2 * (position + 1)] = folded(jnp.where(used, block, 0.0))
+    kept = rhs[...] * keeps[...]
     for tile in range(LEVELS // 2):
         row = RANK // 2 * PIECES[0] + 8 * tile
-        send[row : row + 8] = rhs[:, 2 * RANK * tile : 2 * RANK * (tile + 1)]
+        send[row : row + 8] = kept[:, 2 * RANK * tile : 2 * RANK * (tile + 1)]
+
+
+def mapped_kernel(half, d, u, b, keeps, mapped, base):
+    size = d.shape[0] // 2
+    joined = jnp.concatenate([u[...], turned_rhs(b)], axis=1)
+    for i in range(size // CHUNK):
+        part = slice(CHUNK * i, CHUNK * (i + 1))
+        product = mul(d[size * half + CHUNK * i : size * half + CHUNK * (i + 1)], joined)
+        mapped[:, part] = (product[:, :STATE] * keeps[:1]).astype(bf16).T
+        base[:, part] = product[:, STATE:].T[:8]
 
 
 def level_kernel(level, own, got, send, left):
@@ -200,15 +304,16 @@
     refs[-1][...] = t
 
 
-def basis_kernel(left, t_ref, mapped, base, out):
+def basis_kernel(left, t_ref, mapped_0, mapped_1, base_0, base_1, out):
     t = coefficients(left[...], t_ref[...])
-    w = mapped[...]
+    w = jnp.concatenate([mapped_0[...], mapped_1[...]], axis=1)
     high, low = halves(t)
     rows = t.shape[0]
     product = mul(jnp.concatenate([high, low], axis=0), w[: t.shape[1]])
     product = product[:rows] + product[rows:]
     out[: 2 * RANK] = w[4 * RANK :].astype(f32) + product[: 2 * RANK]
-    out[2 * RANK :] = base[...] + product[2 * RANK :]
+    base = jnp.concatenate([base_0[...], base_1[...]], axis=1)
+    out[2 * RANK :] = base + product[2 * RANK :]
 
 
 def late_kernel(left, basis, high_low, shifted):
@@ -255,43 +360,57 @@
     size = diag_inverse.shape[0]
     vmem = pl.BlockSpec(memory_space=pltpu.VMEM)
     hbm = pl.BlockSpec(memory_space=pltpu.HBM)
-    mapped, base, send = pl.pallas_call(
+    send, d, u, b, keeps = pl.pallas_call(
         first_kernel,
         name="first",
         in_specs=[pl.BlockSpec(memory_space=pltpu.SMEM), hbm, hbm, hbm, hbm],
-        out_specs=[vmem] * 3,
+        out_specs=[vmem] * 5,
         out_shape=[
-            jax.ShapeDtypeStruct((STATE, size), bf16),
-            jax.ShapeDtypeStruct((8, size), f32),
             jax.ShapeDtypeStruct(send_shape(0), f32),
+            jax.ShapeDtypeStruct((size, size), bf16),
+            jax.ShapeDtypeStruct((size, STATE), bf16),
+            jax.ShapeDtypeStruct((8, size), bf16),
+            jax.ShapeDtypeStruct((8, STATE), f32),
         ],
         scratch_shapes=[
-            pltpu.VMEM((size, size), bf16),
             pltpu.VMEM((size, STATE), bf16),
-            pltpu.VMEM((size, STATE), bf16),
-            pltpu.VMEM((8, size), bf16),
-            pltpu.VMEM((STATE + 16, size), bf16),
-            pltpu.VMEM((STATE + 24, STATE), f32),
+            pltpu.VMEM((size, 4 * RANK), bf16),
+            pltpu.VMEM((STATE, CHUNK), bf16),
+            pltpu.VMEM((3 * RANK, size), f32),
+            pltpu.VMEM((STATE, STATE), f32),
             pltpu.VMEM((8, STATE), f32),
             pltpu.SemaphoreType.DMA((size // CHUNK + 3,)),
         ],
-        compiler_params=pltpu.CompilerParams(vmem_limit_bytes=40 << 20),
+        compiler_params=pltpu.CompilerParams(vmem_limit_bytes=30 << 20),
     )(
         *(
             pltpu.with_memory_space_constraint(a, pltpu.HBM)
             for a in (ranks, rhs_vectors, diag_inverse, left_factors, right_factors)
         ),
     )
+    mapped = []
     lefts = []
     basis = t = None
     for level in range(LEVELS - 1):
         got = swapped(send, PARTNER[level])
         after = ()
+        if level in (1, 2):
+            after = call(
+                lambda *refs, half=level - 1: mapped_kernel(half, *refs),
+                f"mapped_{level}",
+                [((STATE, size // 2), bf16), ((8, size // 2), f32)],
+                d,
+                u,
+                b,
+                keeps,
+                after=(send,),
+            )
+            mapped.append(after)
         if level == 3:
             (t,) = after = call(coefficient_kernel, "coefficients", [((3 * RANK + 8, 3 * RANK), f32)], *lefts)
         if level == 4:
             (basis,) = after = call(
-                basis_kernel, "basis", [((2 * RANK + 8, size), f32)], lefts[3], t, mapped, base
+                basis_kernel, "basis", [((2 * RANK + 8, size), f32)], lefts[3], t, *(m[0] for m in mapped), *(m[1] for m in mapped)
             )
         send, left = call(
             lambda *refs, level=level: level_kernel(level, *refs),

time: 40.5 us -> 39.8 us (0.983)
  waiting for transfers between devices: 13 us -> 7.15 us
  Pallas kernels: 12.3 us -> 16.3 us
  starting transfers between devices: 15.1 us -> 16.1 us
    ppermute x6, waiting for transfers between devices: 13 us -> 7.15 us  [swapped(): lax.ppermute(x, 'leaf', [(i, i ^ distance) for i in range(lax.axis_size('...]
    pallas_call x9 -> x11, Pallas kernels: 3.9 us -> 8.92 us  [call(): pl.pallas_call(body, name=name, in_specs=[vmem] * count + [pl.BlockSpec(m...]
    pallas_call x1, Pallas kernels: 8.38 us -> 7.38 us  [on_device(): pl.pallas_call(first_kernel, name='first', in_specs=[pl.BlockSpec(memory_...]
    ppermute x6, starting transfers between devices: 15.1 us -> 16.1 us  [swapped(): lax.ppermute(x, 'leaf', [(i, i ^ distance) for i in range(lax.axis_size('...]
  transfers between devices with their start and end apart: 6 -> 6, of which waited for: 6 -> 5; matrix products, arithmetic and copies ran while one was open for 0% -> 0% of each run, Pallas kernels for 3% -> 16%
where the time goes in v6:
time: 39.8 us; the launch traced here: 39.6 us
  Pallas kernels  16.3 us (41%)
  starting transfers between devices  16.1 us (40%)
  waiting for transfers between devices  7.15 us (18%)
    ppermute x6, starting transfers between devices, swapped(): lax.ppermute(x, 'leaf', [(i, i ^ distance) for i in range(lax.axis_size('...  16.1 us
    pallas_call x11, Pallas kernels, call(): pl.pallas_call(body, name=name, in_specs=[vmem] * count + [pl.BlockSpec(m...  8.92 us
    pallas_call x1, Pallas kernels, on_device(): pl.pallas_call(first_kernel, name='first', in_specs=[pl.BlockSpec(memory_...  7.38 us
    ppermute x6, waiting for transfers between devices, swapped(): lax.ppermute(x, 'leaf', [(i, i ^ distance) for i in range(lax.axis_size('...  7.15 us
  transfers between devices with their start and end apart: 6, of which 5 were waited for; matrix products, arithmetic and copies ran while one was open for 0% of the time, Pallas kernels for 16%

profile of v6, /device:TPU:32, one launch (start us, length us, event | category | flops | bytes accessed | tf_op | source)
XLA Modules:
  0.0 39.6 jit_solution(815049185018290265)
XLA Ops:
  0.0 7.4 %first.1 = (f32[312,128]{1,0:T(8,128)S(1)}, bf16[2048,2048]{1,0:T(8,128)(2,1)S(1)}, bf16[2048,384]{1,0:T(8,128)(2,1)S(1)}, bf16[8,2048]{1,0:T(8,128)(2,1)S(1)}, f32[8,384]{1,0:T(8,128)S(1)}) custom-call(s32[6]{0:T(128)} %ranks.1, bf16[8,2048]{1,0:T(8,128)(2,1)} %b_hbm.1, bf16[2048,2048]{1,0:T(8,128)(2,1)} %d_hbm.1, bf16[2048,384]{1,0:T(8,128)(2,1)} %u_hbm.1, ...), custom_call_target="tpu_custom_call" | custom-call | tf_op jit(solution)/shard_map/first/pallas_call | solution.py:363
  7.4 0.1 collective-permute-start
  7.5 1.4 %collective-permute-done.refs_1_ = f32[312,128]{1,0:T(8,128)S(1)} collective-permute-done((f32[312,128]{1,0:T(8,128)S(1)}, f32[312,128]{1,0:T(8,128)S(1)}, u32[]{:S(2)}, u32[]{:S(2)}) %collective-permute-start) | collective-permute-done | bytes 159776 | tf_op jit(solution)/shard_map/ppermute | solution.py:356
  8.9 0.4 %level_0.1 = (f32[216,128]{1,0:T(8,128)S(1)}, f32[328,64]{1,0:T(8,128)S(1)}) custom-call(f32[312,128]{1,0:T(8,128)S(1)} %get-tuple-element.26.refs_0_, f32[312,128]{1,0:T(8,128)S(1)} %collective-permute-done.refs_1_), custom_call_target="tpu_custom_call" | custom-call | tf_op jit(solution)/shard_map/level_0/pallas_call | solution.py:345
  9.3 1.9 %collective-permute-start.1 = (f32[216,128]{1,0:T(8,128)S(1)}, f32[216,128]{1,0:T(8,128)S(1)}, u32[]{:S(2)}, u32[]{:S(2)}) collective-permute-start(f32[216,128]{1,0:T(8,128)S(1)} %get-tuple-element.27.refs_4_.refs_0_), channel_id=1, source_target_pairs={{0,8},{4,12},{8,0},{12,4},{16,24},{20,28},{24,16},{28,20},{32,40},... | collective-permute-start | bytes 331784 | tf_op jit(solution)/shard_map/ppermute | solution.py:356
  11.2 2.5 %mapped_1.1 = (bf16[384,1024]{1,0:T(8,128)(2,1)S(1)}, f32[8,1024]{1,0:T(8,128)S(1)}) custom-call(bf16[2048,2048]{1,0:T(8,128)(2,1)S(1)} %get-tuple-element.28.refs_0_, bf16[2048,384]{1,0:T(8,128)(2,1)S(1)} %get-tuple-element.29.refs_1_, bf16[8,2048]{1,0:T(8,128)(2,1)S(1)} %get-tuple-element.30.refs_2_, f32[8,384]{1,0:T(8,128)S(1)} %get-tuple-element.31.refs_3_, ...), custom_call_target="tpu_custom_call" | custom-call | tf_op jit(solution)/shard_map/mapped_1/pallas_call | solution.py:345
  13.7 0.9 %collective-permute-done.1.refs_1_ = f32[216,128]{1,0:T(8,128)S(1)} collective-permute-done((f32[216,128]{1,0:T(8,128)S(1)}, f32[216,128]{1,0:T(8,128)S(1)}, u32[]{:S(2)}, u32[]{:S(2)}) %collective-permute-start.1) | collective-permute-done | bytes 110624 | tf_op jit(solution)/shard_map/ppermute | solution.py:356
  14.6 0.4 level_1.1
  14.9 3.4 %collective-permute-start.2 = (f32[144,128]{1,0:T(8,128)S(1)}, f32[144,128]{1,0:T(8,128)S(1)}, u32[]{:S(2)}, u32[]{:S(2)}) collective-permute-start(f32[144,128]{1,0:T(8,128)S(1)} %get-tuple-element.34.refs_4_.refs_0_), channel_id=1, source_target_pairs={{0,16},{4,20},{8,24},{12,28},{16,0},{20,4},{24,8},{28,12},{32,48},... | collective-permute-start | bytes 221192 | tf_op jit(solution)/shard_map/ppermute | solution.py:356
  18.4 2.5 %mapped_2.1 = (bf16[384,1024]{1,0:T(8,128)(2,1)S(1)}, f32[8,1024]{1,0:T(8,128)S(1)}) custom-call(bf16[2048,2048]{1,0:T(8,128)(2,1)S(1)} %get-tuple-element.28.refs_0_, bf16[2048,384]{1,0:T(8,128)(2,1)S(1)} %get-tuple-element.29.refs_1_, bf16[8,2048]{1,0:T(8,128)(2,1)S(1)} %get-tuple-element.30.refs_2_, f32[8,384]{1,0:T(8,128)S(1)} %get-tuple-element.31.refs_3_, ...), custom_call_target="tpu_custom_call" | custom-call | tf_op jit(solution)/shard_map/mapped_2/pallas_call | solution.py:345
  20.9 0.0 collective-permute-done.2.refs_1_
  20.9 0.4 level_2.1
  21.3 6.1 %collective-permute-start.3 = (f32[80,128]{1,0:T(8,128)S(1)}, f32[80,128]{1,0:T(8,128)S(1)}, u32[]{:S(2)}, u32[]{:S(2)}) collective-permute-start(f32[80,128]{1,0:T(8,128)S(1)} %get-tuple-element.37.refs_0_), channel_id=1, source_target_pairs={{0,48},{4,52},{8,56},{12,60},{16,32},{20,36},{24,40},{28,44},{32,1... | collective-permute-start | bytes 122888 | tf_op jit(solution)/shard_map/ppermute | solution.py:356
  27.4 0.4 coefficients.1.refs_2_.refs_1_
  27.8 1.6 %collective-permute-done.3.refs_1_ = f32[80,128]{1,0:T(8,128)S(1)} collective-permute-done((f32[80,128]{1,0:T(8,128)S(1)}, f32[80,128]{1,0:T(8,128)S(1)}, u32[]{:S(2)}, u32[]{:S(2)}) %collective-permute-start.3) | collective-permute-done | bytes 40992 | tf_op jit(solution)/shard_map/ppermute | solution.py:356
  29.4 0.3 level_3.1
  29.7 1.6 %collective-permute-start.4 = (f32[40,128]{1,0:T(8,128)S(1)}, f32[40,128]{1,0:T(8,128)S(1)}, u32[]{:S(2)}, u32[]{:S(2)}) collective-permute-start(f32[40,128]{1,0:T(8,128)S(1)} %get-tuple-element.41.refs_0_), channel_id=1, source_target_pairs={{0,64},{4,68},{8,72},{12,76},{16,80},{20,84},{24,88},{28,92},{32,9... | collective-permute-start | bytes 61448 | tf_op jit(solution)/shard_map/ppermute | solution.py:356
  31.4 0.7 %basis.1.refs_2_.refs_1_ = f32[136,2048]{1,0:T(8,128)S(1)} custom-call(f32[136,64]{1,0:T(8,128)S(1)} %get-tuple-element.42.refs_0_, f32[200,192]{1,0:T(8,128)S(1)} %coefficients.1.refs_2_.refs_1_, bf16[384,1024]{1,0:T(8,128)(2,1)S(1)} %get-tuple-element.32.refs_2_, bf16[384,1024]{1,0:T(8,128)(2,1)S(1)} %get-tuple-element.35.refs_2_.refs_3_, ...), custom_call_target="tpu_custom_call" | custom-call | tf_op jit(solution)/shard_map/basis/pallas_call | solution.py:345
  32.0 1.6 %collective-permute-done.4.refs_1_ = f32[40,128]{1,0:T(8,128)S(1)} collective-permute-done((f32[40,128]{1,0:T(8,128)S(1)}, f32[40,128]{1,0:T(8,128)S(1)}, u32[]{:S(2)}, u32[]{:S(2)}) %collective-permute-start.4) | collective-permute-done | bytes 20512 | tf_op jit(solution)/shard_map/ppermute | solution.py:356
  33.6 0.3 level_4.1
  33.9 2.8 %collective-permute-start.5 = (f32[8,128]{1,0:T(8,128)S(1)}, f32[8,128]{1,0:T(8,128)S(1)}, u32[]{:S(2)}, u32[]{:S(2)}) collective-permute-start(f32[8,128]{1,0:T(8,128)S(1)} %get-tuple-element.43), channel_id=1, source_target_pairs={{0,192},{4,196},{8,200},{12,204},{16,208},{20,212},{24,216},{28,22... | collective-permute-start | bytes 12296 | tf_op jit(solution)/shard_map/ppermute | solution.py:356
  36.7 0.3 late.1
  37.0 1.7 %collective-permute-done.5.refs_0_ = f32[8,128]{1,0:T(8,128)S(1)} collective-permute-done((f32[8,128]{1,0:T(8,128)S(1)}, f32[8,128]{1,0:T(8,128)S(1)}, u32[]{:S(2)}, u32[]{:S(2)}) %collective-permute-start.5) | collective-permute-done | bytes 4128 | tf_op jit(solution)/shard_map/ppermute | solution.py:356
  38.7 0.9 %last.1 = f32[8,2048]{1,0:T(8,128)} custom-call(f32[8,128]{1,0:T(8,128)S(1)} %collective-permute-done.5.refs_0_, bf16[192,2048]{1,0:T(8,128)(2,1)S(1)} %get-tuple-element.45.refs_1_, f32[8,2048]{1,0:T(8,128)S(1)} %get-tuple-element.46.refs_2_), custom_call_target="tpu_custom_call" | custom-call | tf_op jit(solution)/shard_map/last/pallas_call | solution.py:345
Async XLA Ops:
  7.4 1.5 %collective-permute-start = (f32[312,128]{1,0:T(8,128)S(1)}, f32[312,128]{1,0:T(8,128)S(1)}, u32[]{:S(2)}, u32[]{:S(2)}) collective-permute-start(f32[312,128]{1,0:T(8,128)S(1)} %get-tuple-element.26.refs_0_), channel_id=1, source_target_pairs={{0,4},{4,0},{8,12},{12,8},{16,20},{20,16},{24,28},{28,24},{32,36},... | collective-permute-start | bytes 479240 | tf_op jit(solution)/shard_map/ppermute | solution.py:356
  9.3 5.3 %collective-permute-start.1 = (f32[216,128]{1,0:T(8,128)S(1)}, f32[216,128]{1,0:T(8,128)S(1)}, u32[]{:S(2)}, u32[]{:S(2)}) collective-permute-start(f32[216,128]{1,0:T(8,128)S(1)} %get-tuple-element.27.refs_4_.refs_0_), channel_id=1, source_target_pairs={{0,8},{4,12},{8,0},{12,4},{16,24},{20,28},{24,16},{28,20},{32,40},... | collective-permute-start | bytes 331784 | tf_op jit(solution)/shard_map/ppermute | solution.py:356
  14.9 5.9 %collective-permute-start.2 = (f32[144,128]{1,0:T(8,128)S(1)}, f32[144,128]{1,0:T(8,128)S(1)}, u32[]{:S(2)}, u32[]{:S(2)}) collective-permute-start(f32[144,128]{1,0:T(8,128)S(1)} %get-tuple-element.34.refs_4_.refs_0_), channel_id=1, source_target_pairs={{0,16},{4,20},{8,24},{12,28},{16,0},{20,4},{24,8},{28,12},{32,48},... | collective-permute-start | bytes 221192 | tf_op jit(solution)/shard_map/ppermute | solution.py:356
  21.3 8.2 %collective-permute-start.3 = (f32[80,128]{1,0:T(8,128)S(1)}, f32[80,128]{1,0:T(8,128)S(1)}, u32[]{:S(2)}, u32[]{:S(2)}) collective-permute-start(f32[80,128]{1,0:T(8,128)S(1)} %get-tuple-element.37.refs_0_), channel_id=1, source_target_pairs={{0,48},{4,52},{8,56},{12,60},{16,32},{20,36},{24,40},{28,44},{32,1... | collective-permute-start | bytes 122888 | tf_op jit(solution)/shard_map/ppermute | solution.py:356
  29.7 3.9 %collective-permute-start.4 = (f32[40,128]{1,0:T(8,128)S(1)}, f32[40,128]{1,0:T(8,128)S(1)}, u32[]{:S(2)}, u32[]{:S(2)}) collective-permute-start(f32[40,128]{1,0:T(8,128)S(1)} %get-tuple-element.41.refs_0_), channel_id=1, source_target_pairs={{0,64},{4,68},{8,72},{12,76},{16,80},{20,84},{24,88},{28,92},{32,9... | collective-permute-start | bytes 61448 | tf_op jit(solution)/shard_map/ppermute | solution.py:356
  33.9 4.8 %collective-permute-start.5 = (f32[8,128]{1,0:T(8,128)S(1)}, f32[8,128]{1,0:T(8,128)S(1)}, u32[]{:S(2)}, u32[]{:S(2)}) collective-permute-start(f32[8,128]{1,0:T(8,128)S(1)} %get-tuple-element.43), channel_id=1, source_target_pairs={{0,192},{4,196},{8,200},{12,204},{16,208},{20,212},{24,216},{28,22... | collective-permute-start | bytes 12296 | tf_op jit(solution)/shard_map/ppermute | solution.py:356

commit v7 on v6

--- a/solution.py
+++ b/solution.py
@@ -13,6 +13,8 @@
 LEVELS = 6
 STATE = RANK * LEVELS
 CHUNK = 512
+FEW_CHUNKS = (512, 768, 768)
+MANY_CHUNKS = (256, 256, 512, 512, 512)
 PARTNER = (1, 2, 4, 12, 16, 48)
 PIECES = (9, 6, 4, 2, 1, 0)
 
@@ -105,12 +107,6 @@
 
 
 def few_ones(places, d, u, v, b, x, acc, rhs, copies, copy_u, copy_b, copy_v):
-    copy_u.start()
-    copy_b.start()
-    copies[0].start()
-    copy_v.start()
-    for c in copies[1:]:
-        c.start()
     tile_0, tile_1, free = tiles_of(places)
     copy_b.wait()
     extra = turned_rhs(b)
@@ -120,9 +116,10 @@
     second = u[:, pl.ds(pl.multiple_of(2 * RANK * tile_1, 2 * RANK), 2 * RANK)]
     x[:, 2 * RANK :] = jnp.where(lane // RANK == free, extra, second)
     count = len(copies)
+    starts = [sum(FEW_CHUNKS[:i]) for i in range(count + 1)]
 
     def gather(i, joined):
-        total = mul(joined, v[CHUNK * i : CHUNK * (i + 1)])
+        total = mul(joined, v[starts[i] : starts[i + 1]])
         if i == 0:
             acc[: 4 * RANK + 16] = total
         else:
@@ -133,11 +130,8 @@
         copies[i].wait()
         if i == 1:
             copy_v.wait()
-        middle = CHUNK * i + CHUNK // 2
-        ahead = [
-            mul(d[CHUNK * i : middle], x[...]),
-            mul(d[middle : CHUNK * (i + 1)], x[...]),
-        ]
+        middle = (starts[i] + starts[i + 1]) // 2
+        ahead = [mul(d[starts[i] : middle], x[...]), mul(d[middle : starts[i + 1]], x[...])]
         if i > 0:
             gather(i - 1, joined)
         product = jnp.concatenate(ahead, axis=0)
@@ -151,20 +145,21 @@
 
 
 def few_zeros(places, d, u, v, b, turned, z, acc, rhs, copies, copy_u, copy_b, copy_v):
-    copy_v.start()
-    copies[0].start()
-    copy_b.start()
-    for c in copies[1:]:
-        c.start()
-    copy_u.start()
     zeros = [places.nth(n, 0) for n in range(3)]
+    starts = [sum(MANY_CHUNKS[:i]) for i in range(len(copies) + 1)]
+
+    def turn(i):
+        turned[:, starts[i] : starts[i + 1]] = v[starts[i] : starts[i + 1]].T
+
     copy_v.wait()
+    turn(0)
     for i, c in enumerate(copies):
         c.wait()
-        part = slice(CHUNK * i, CHUNK * (i + 1))
-        turned[...] = v[part].T
-        rows = [turned[pl.ds(pl.multiple_of(RANK * n, RANK), RANK)] for n in zeros]
+        part = slice(starts[i], starts[i + 1])
+        rows = [turned[pl.ds(pl.multiple_of(RANK * n, RANK), RANK), part] for n in zeros]
         product = mul(jnp.concatenate(rows, axis=0), d[part])
+        if i + 1 < len(copies):
+            turn(i + 1)
         if i == 0:
             z[...] = product
         else:
@@ -200,11 +195,12 @@
 
 
 def first_kernel(ranks, b_hbm, d_hbm, u_hbm, v_hbm, send, d, u, b, keeps, v, x, turned, z, acc, rhs, sems):
-    n = d.shape[0] // CHUNK
-    copies = [
-        pltpu.make_async_copy(d_hbm.at[pl.ds(CHUNK * i, CHUNK)], d.at[pl.ds(CHUNK * i, CHUNK)], sems.at[i])
-        for i in range(n)
-    ]
+    n = max(len(FEW_CHUNKS), len(MANY_CHUNKS))
+
+    def pieces_of(sizes):
+        parts = [pl.ds(sum(sizes[:i]), sizes[i]) for i in range(len(sizes))]
+        return [pltpu.make_async_copy(d_hbm.at[p], d.at[p], sems.at[i]) for i, p in enumerate(parts)]
+
     copy_u = pltpu.make_async_copy(u_hbm, u, sems.at[n])
     copy_b = pltpu.make_async_copy(b_hbm, b, sems.at[n + 1])
     copy_v = pltpu.make_async_copy(v_hbm, v, sems.at[n + 2])
@@ -213,26 +209,42 @@
 
     @pl.when(few)
     def _():
-        few_ones(places, d, u, v, b, x, acc, rhs, copies, copy_u, copy_b, copy_v)
+        copies = pieces_of(FEW_CHUNKS)
+        for c in (copy_b, copy_u, copies[0], copy_v, *copies[1:]):
+            c.start()
 
     @pl.when(jnp.logical_not(few))
     def _():
-        few_zeros(places, d, u, v, b, turned, z, acc, rhs, copies, copy_u, copy_b, copy_v)
-
-    keeps[...] = keep_row(ranks)
+        copies = pieces_of(MANY_CHUNKS)
+        for c in (copy_v, *copies, copy_u, copy_b):
+            c.start()
+
     tile_0, _, _ = tiles_of(places)
-    row_id = lax.broadcasted_iota(jnp.int32, (RANK, RANK), 0)
-    lane_id = lax.broadcasted_iota(jnp.int32, (RANK, RANK), 1)
+    plan = []
     for position in range(PIECES[0]):
         one, zero, valid = places.next_piece(position)
         m, l = places.nth(one, 1), places.nth(zero, 0)
         start = jnp.where(few, jnp.where(m // 2 == tile_0, 0, 2 * RANK) + RANK * (m % 2), RANK * m)
         lane_piece = jnp.where(few, l, jnp.minimum(zero, 2))
+        plan.append((start, lane_piece, ranks[m], jnp.where(valid, ranks[l], 0)))
+    keeps[...] = keep_row(ranks)
+
+    @pl.when(few)
+    def _():
+        few_ones(places, d, u, v, b, x, acc, rhs, pieces_of(FEW_CHUNKS), copy_u, copy_b, copy_v)
+
+    @pl.when(jnp.logical_not(few))
+    def _():
+        few_zeros(places, d, u, v, b, turned, z, acc, rhs, pieces_of(MANY_CHUNKS), copy_u, copy_b, copy_v)
+
+    row_id = lax.broadcasted_iota(jnp.int32, (RANK, RANK), 0)
+    lane_id = lax.broadcasted_iota(jnp.int32, (RANK, RANK), 1)
+    for position, (start, lane_piece, rank_m, rank_l) in enumerate(plan):
         rows = pl.ds(pl.multiple_of(start, RANK), RANK)
         lanes = pl.ds(pl.multiple_of(2 * RANK * (lane_piece // 2), 2 * RANK), 2 * RANK)
         tile = acc[rows, lanes]
         block = jnp.where(lane_piece % 2 == 1, tile[:, RANK:], tile[:, :RANK])
-        used = (row_id < ranks[m]) & (lane_id < jnp.where(valid, ranks[l], 0))
+        used = (row_id < rank_m) & (lane_id < rank_l)
         send[RANK // 2 * position : RANK // 2 * (position + 1)] = folded(jnp.where(used, block, 0.0))
     kept = rhs[...] * keeps[...]
     for tile in range(LEVELS // 2):
@@ -375,11 +387,11 @@
         scratch_shapes=[
             pltpu.VMEM((size, STATE), bf16),
             pltpu.VMEM((size, 4 * RANK), bf16),
-            pltpu.VMEM((STATE, CHUNK), bf16),
+            pltpu.VMEM((STATE, size), bf16),
             pltpu.VMEM((3 * RANK, size), f32),
             pltpu.VMEM((STATE, STATE), f32),
             pltpu.VMEM((8, STATE), f32),
-            pltpu.SemaphoreType.DMA((size // CHUNK + 3,)),
+            pltpu.SemaphoreType.DMA((max(len(FEW_CHUNKS), len(MANY_CHUNKS)) + 3,)),
         ],
         compiler_params=pltpu.CompilerParams(vmem_limit_bytes=30 << 20),
     )(

time: 39.8 us -> 39.9 us (level)
  starting transfers between devices: 16.1 us -> 15.5 us
  waiting for transfers between devices: 7.15 us -> 7.71 us
    ppermute x6, waiting for transfers between devices: 7.15 us -> 7.71 us  [swapped(): lax.ppermute(x, 'leaf', [(i, i ^ distance) for i in range(lax.axis_size('...]
    ppermute x6, starting transfers between devices: 16.1 us -> 15.5 us  [swapped(): lax.ppermute(x, 'leaf', [(i, i ^ distance) for i in range(lax.axis_size('...]
where the time goes in v7:
time: 39.9 us; the launch traced here: 39.8 us
  Pallas kernels  16.5 us (41%)
  starting transfers between devices  15.5 us (39%)
  waiting for transfers between devices  7.71 us (19%)
    ppermute x6, starting transfers between devices, swapped(): lax.ppermute(x, 'leaf', [(i, i ^ distance) for i in range(lax.axis_size('...  15.5 us
    pallas_call x11, Pallas kernels, call(): pl.pallas_call(body, name=name, in_specs=[vmem] * count + [pl.BlockSpec(m...  8.92 us
    ppermute x6, waiting for transfers between devices, swapped(): lax.ppermute(x, 'leaf', [(i, i ^ distance) for i in range(lax.axis_size('...  7.71 us
    pallas_call x1, Pallas kernels, on_device(): pl.pallas_call(first_kernel, name='first', in_specs=[pl.BlockSpec(memory_...  7.56 us
  transfers between devices with their start and end apart: 6, of which 5 were waited for; matrix products, arithmetic and copies ran while one was open for 0% of the time, Pallas kernels for 16%

profile of v7, /device:TPU:32, one launch (start us, length us, event | category | flops | bytes accessed | tf_op | source)
XLA Modules:
  0.0 39.8 jit_solution(1266738297698862115)
XLA Ops:
  0.0 7.6 %first.1 = (f32[312,128]{1,0:T(8,128)S(1)}, bf16[2048,2048]{1,0:T(8,128)(2,1)S(1)}, bf16[2048,384]{1,0:T(8,128)(2,1)S(1)}, bf16[8,2048]{1,0:T(8,128)(2,1)S(1)}, f32[8,384]{1,0:T(8,128)S(1)}) custom-call(s32[6]{0:T(128)} %ranks.1, bf16[8,2048]{1,0:T(8,128)(2,1)} %b_hbm.1, bf16[2048,2048]{1,0:T(8,128)(2,1)} %d_hbm.1, bf16[2048,384]{1,0:T(8,128)(2,1)} %u_hbm.1, ...), custom_call_target="tpu_custom_call" | custom-call | tf_op jit(solution)/shard_map/first/pallas_call | solution.py:375
  7.6 0.1 collective-permute-start
  7.7 1.4 %collective-permute-done.refs_1_ = f32[312,128]{1,0:T(8,128)S(1)} collective-permute-done((f32[312,128]{1,0:T(8,128)S(1)}, f32[312,128]{1,0:T(8,128)S(1)}, u32[]{:S(2)}, u32[]{:S(2)}) %collective-permute-start) | collective-permute-done | bytes 159776 | tf_op jit(solution)/shard_map/ppermute | solution.py:368
  9.0 0.4 %level_0.1 = (f32[216,128]{1,0:T(8,128)S(1)}, f32[328,64]{1,0:T(8,128)S(1)}) custom-call(f32[312,128]{1,0:T(8,128)S(1)} %get-tuple-element.26.refs_0_, f32[312,128]{1,0:T(8,128)S(1)} %collective-permute-done.refs_1_), custom_call_target="tpu_custom_call" | custom-call | tf_op jit(solution)/shard_map/level_0/pallas_call | solution.py:357
  9.5 1.9 %collective-permute-start.1 = (f32[216,128]{1,0:T(8,128)S(1)}, f32[216,128]{1,0:T(8,128)S(1)}, u32[]{:S(2)}, u32[]{:S(2)}) collective-permute-start(f32[216,128]{1,0:T(8,128)S(1)} %get-tuple-element.27.refs_4_.refs_0_), channel_id=1, source_target_pairs={{0,8},{4,12},{8,0},{12,4},{16,24},{20,28},{24,16},{28,20},{32,40},... | collective-permute-start | bytes 331784 | tf_op jit(solution)/shard_map/ppermute | solution.py:368
  11.4 2.5 %mapped_1.1 = (bf16[384,1024]{1,0:T(8,128)(2,1)S(1)}, f32[8,1024]{1,0:T(8,128)S(1)}) custom-call(bf16[2048,2048]{1,0:T(8,128)(2,1)S(1)} %get-tuple-element.28.refs_0_, bf16[2048,384]{1,0:T(8,128)(2,1)S(1)} %get-tuple-element.29.refs_1_, bf16[8,2048]{1,0:T(8,128)(2,1)S(1)} %get-tuple-element.30.refs_2_, f32[8,384]{1,0:T(8,128)S(1)} %get-tuple-element.31.refs_3_, ...), custom_call_target="tpu_custom_call" | custom-call | tf_op jit(solution)/shard_map/mapped_1/pallas_call | solution.py:357
  13.8 0.9 %collective-permute-done.1.refs_1_ = f32[216,128]{1,0:T(8,128)S(1)} collective-permute-done((f32[216,128]{1,0:T(8,128)S(1)}, f32[216,128]{1,0:T(8,128)S(1)}, u32[]{:S(2)}, u32[]{:S(2)}) %collective-permute-start.1) | collective-permute-done | bytes 110624 | tf_op jit(solution)/shard_map/ppermute | solution.py:368
  14.7 0.4 level_1.1
  15.1 3.5 %collective-permute-start.2 = (f32[144,128]{1,0:T(8,128)S(1)}, f32[144,128]{1,0:T(8,128)S(1)}, u32[]{:S(2)}, u32[]{:S(2)}) collective-permute-start(f32[144,128]{1,0:T(8,128)S(1)} %get-tuple-element.34.refs_4_.refs_0_), channel_id=1, source_target_pairs={{0,16},{4,20},{8,24},{12,28},{16,0},{20,4},{24,8},{28,12},{32,48},... | collective-permute-start | bytes 221192 | tf_op jit(solution)/shard_map/ppermute | solution.py:368
  18.6 2.5 %mapped_2.1 = (bf16[384,1024]{1,0:T(8,128)(2,1)S(1)}, f32[8,1024]{1,0:T(8,128)S(1)}) custom-call(bf16[2048,2048]{1,0:T(8,128)(2,1)S(1)} %get-tuple-element.28.refs_0_, bf16[2048,384]{1,0:T(8,128)(2,1)S(1)} %get-tuple-element.29.refs_1_, bf16[8,2048]{1,0:T(8,128)(2,1)S(1)} %get-tuple-element.30.refs_2_, f32[8,384]{1,0:T(8,128)S(1)} %get-tuple-element.31.refs_3_, ...), custom_call_target="tpu_custom_call" | custom-call | tf_op jit(solution)/shard_map/mapped_2/pallas_call | solution.py:357
  21.1 0.0 collective-permute-done.2.refs_1_
  21.1 0.4 level_2.1
  21.4 5.9 %collective-permute-start.3 = (f32[80,128]{1,0:T(8,128)S(1)}, f32[80,128]{1,0:T(8,128)S(1)}, u32[]{:S(2)}, u32[]{:S(2)}) collective-permute-start(f32[80,128]{1,0:T(8,128)S(1)} %get-tuple-element.37.refs_0_), channel_id=1, source_target_pairs={{0,48},{4,52},{8,56},{12,60},{16,32},{20,36},{24,40},{28,44},{32,1... | collective-permute-start | bytes 122888 | tf_op jit(solution)/shard_map/ppermute | solution.py:368
  27.4 0.4 coefficients.1.refs_2_.refs_1_
  27.8 1.8 %collective-permute-done.3.refs_1_ = f32[80,128]{1,0:T(8,128)S(1)} collective-permute-done((f32[80,128]{1,0:T(8,128)S(1)}, f32[80,128]{1,0:T(8,128)S(1)}, u32[]{:S(2)}, u32[]{:S(2)}) %collective-permute-start.3) | collective-permute-done | bytes 40992 | tf_op jit(solution)/shard_map/ppermute | solution.py:368
  29.6 0.3 level_3.1
  29.9 1.5 %collective-permute-start.4 = (f32[40,128]{1,0:T(8,128)S(1)}, f32[40,128]{1,0:T(8,128)S(1)}, u32[]{:S(2)}, u32[]{:S(2)}) collective-permute-start(f32[40,128]{1,0:T(8,128)S(1)} %get-tuple-element.41.refs_0_), channel_id=1, source_target_pairs={{0,64},{4,68},{8,72},{12,76},{16,80},{20,84},{24,88},{28,92},{32,9... | collective-permute-start | bytes 61448 | tf_op jit(solution)/shard_map/ppermute | solution.py:368
  31.4 0.7 %basis.1.refs_2_.refs_1_ = f32[136,2048]{1,0:T(8,128)S(1)} custom-call(f32[136,64]{1,0:T(8,128)S(1)} %get-tuple-element.42.refs_0_, f32[200,192]{1,0:T(8,128)S(1)} %coefficients.1.refs_2_.refs_1_, bf16[384,1024]{1,0:T(8,128)(2,1)S(1)} %get-tuple-element.32.refs_2_, bf16[384,1024]{1,0:T(8,128)(2,1)S(1)} %get-tuple-element.35.refs_2_.refs_3_, ...), custom_call_target="tpu_custom_call" | custom-call | tf_op jit(solution)/shard_map/basis/pallas_call | solution.py:357
  32.0 1.7 %collective-permute-done.4.refs_1_ = f32[40,128]{1,0:T(8,128)S(1)} collective-permute-done((f32[40,128]{1,0:T(8,128)S(1)}, f32[40,128]{1,0:T(8,128)S(1)}, u32[]{:S(2)}, u32[]{:S(2)}) %collective-permute-start.4) | collective-permute-done | bytes 20512 | tf_op jit(solution)/shard_map/ppermute | solution.py:368
  33.8 0.3 level_4.1
  34.0 2.6 %collective-permute-start.5 = (f32[8,128]{1,0:T(8,128)S(1)}, f32[8,128]{1,0:T(8,128)S(1)}, u32[]{:S(2)}, u32[]{:S(2)}) collective-permute-start(f32[8,128]{1,0:T(8,128)S(1)} %get-tuple-element.43), channel_id=1, source_target_pairs={{0,192},{4,196},{8,200},{12,204},{16,208},{20,212},{24,216},{28,22... | collective-permute-start | bytes 12296 | tf_op jit(solution)/shard_map/ppermute | solution.py:368
  36.7 0.3 late.1
  37.0 1.9 %collective-permute-done.5.refs_0_ = f32[8,128]{1,0:T(8,128)S(1)} collective-permute-done((f32[8,128]{1,0:T(8,128)S(1)}, f32[8,128]{1,0:T(8,128)S(1)}, u32[]{:S(2)}, u32[]{:S(2)}) %collective-permute-start.5) | collective-permute-done | bytes 4128 | tf_op jit(solution)/shard_map/ppermute | solution.py:368
  38.9 0.9 %last.1 = f32[8,2048]{1,0:T(8,128)} custom-call(f32[8,128]{1,0:T(8,128)S(1)} %collective-permute-done.5.refs_0_, bf16[192,2048]{1,0:T(8,128)(2,1)S(1)} %get-tuple-element.45.refs_1_, f32[8,2048]{1,0:T(8,128)S(1)} %get-tuple-element.46.refs_2_), custom_call_target="tpu_custom_call" | custom-call | tf_op jit(solution)/shard_map/last/pallas_call | solution.py:357
Async XLA Ops:
  7.6 1.5 %collective-permute-start = (f32[312,128]{1,0:T(8,128)S(1)}, f32[312,128]{1,0:T(8,128)S(1)}, u32[]{:S(2)}, u32[]{:S(2)}) collective-permute-start(f32[312,128]{1,0:T(8,128)S(1)} %get-tuple-element.26.refs_0_), channel_id=1, source_target_pairs={{0,4},{4,0},{8,12},{12,8},{16,20},{20,16},{24,28},{28,24},{32,36},... | collective-permute-start | bytes 479240 | tf_op jit(solution)/shard_map/ppermute | solution.py:368
  9.5 5.3 %collective-permute-start.1 = (f32[216,128]{1,0:T(8,128)S(1)}, f32[216,128]{1,0:T(8,128)S(1)}, u32[]{:S(2)}, u32[]{:S(2)}) collective-permute-start(f32[216,128]{1,0:T(8,128)S(1)} %get-tuple-element.27.refs_4_.refs_0_), channel_id=1, source_target_pairs={{0,8},{4,12},{8,0},{12,4},{16,24},{20,28},{24,16},{28,20},{32,40},... | collective-permute-start | bytes 331784 | tf_op jit(solution)/shard_map/ppermute | solution.py:368
  15.1 5.9 %collective-permute-start.2 = (f32[144,128]{1,0:T(8,128)S(1)}, f32[144,128]{1,0:T(8,128)S(1)}, u32[]{:S(2)}, u32[]{:S(2)}) collective-permute-start(f32[144,128]{1,0:T(8,128)S(1)} %get-tuple-element.34.refs_4_.refs_0_), channel_id=1, source_target_pairs={{0,16},{4,20},{8,24},{12,28},{16,0},{20,4},{24,8},{28,12},{32,48},... | collective-permute-start | bytes 221192 | tf_op jit(solution)/shard_map/ppermute | solution.py:368
  21.4 8.2 %collective-permute-start.3 = (f32[80,128]{1,0:T(8,128)S(1)}, f32[80,128]{1,0:T(8,128)S(1)}, u32[]{:S(2)}, u32[]{:S(2)}) collective-permute-start(f32[80,128]{1,0:T(8,128)S(1)} %get-tuple-element.37.refs_0_), channel_id=1, source_target_pairs={{0,48},{4,52},{8,56},{12,60},{16,32},{20,36},{24,40},{28,44},{32,1... | collective-permute-start | bytes 122888 | tf_op jit(solution)/shard_map/ppermute | solution.py:368
  29.9 3.9 %collective-permute-start.4 = (f32[40,128]{1,0:T(8,128)S(1)}, f32[40,128]{1,0:T(8,128)S(1)}, u32[]{:S(2)}, u32[]{:S(2)}) collective-permute-start(f32[40,128]{1,0:T(8,128)S(1)} %get-tuple-element.41.refs_0_), channel_id=1, source_target_pairs={{0,64},{4,68},{8,72},{12,76},{16,80},{20,84},{24,88},{28,92},{32,9... | collective-permute-start | bytes 61448 | tf_op jit(solution)/shard_map/ppermute | solution.py:368
  34.0 4.8 %collective-permute-start.5 = (f32[8,128]{1,0:T(8,128)S(1)}, f32[8,128]{1,0:T(8,128)S(1)}, u32[]{:S(2)}, u32[]{:S(2)}) collective-permute-start(f32[8,128]{1,0:T(8,128)S(1)} %get-tuple-element.43), channel_id=1, source_target_pairs={{0,192},{4,196},{8,200},{12,204},{16,208},{20,212},{24,216},{28,22... | collective-permute-start | bytes 12296 | tf_op jit(solution)/shard_map/ppermute | solution.py:368

commit v8 on v7

--- a/solution.py
+++ b/solution.py
@@ -13,7 +13,7 @@
 LEVELS = 6
 STATE = RANK * LEVELS
 CHUNK = 512
-FEW_CHUNKS = (512, 768, 768)
+FEW_CHUNKS = (512, 512, 512, 512)
 MANY_CHUNKS = (256, 256, 512, 512, 512)
 PARTNER = (1, 2, 4, 12, 16, 48)
 PIECES = (9, 6, 4, 2, 1, 0)
@@ -106,11 +106,12 @@
     return jnp.concatenate([wide, gap, wide, gap], axis=0).T.astype(bf16)
 
 
-def few_ones(places, d, u, v, b, x, acc, rhs, copies, copy_u, copy_b, copy_v):
+def few_ones(places, d, u, v, b, x, acc, rhs, copies, copies_u, copy_b, copy_v):
     tile_0, tile_1, free = tiles_of(places)
     copy_b.wait()
     extra = turned_rhs(b)
-    copy_u.wait()
+    copies_u[0].wait()
+    copies_u[1].wait()
     lane = lax.broadcasted_iota(jnp.int32, extra.shape, 1)
     x[:, : 2 * RANK] = u[:, pl.ds(pl.multiple_of(2 * RANK * tile_0, 2 * RANK), 2 * RANK)]
     second = u[:, pl.ds(pl.multiple_of(2 * RANK * tile_1, 2 * RANK), 2 * RANK)]
@@ -139,22 +140,25 @@
         base = jnp.where(free == 1, base[RANK : RANK + 8], base[:8])
         _, low, rest = thirds(base)
         joined = jnp.concatenate([product.astype(bf16).T, low, rest], axis=0)
+    copies_u[2].wait()
     gather(count - 1, joined)
     start = pl.multiple_of(2 * RANK + RANK * free, RANK)
     rhs[...] = acc[pl.ds(start, 8)] + acc[4 * RANK : 4 * RANK + 8] + acc[4 * RANK + 8 : 4 * RANK + 16]
 
 
-def few_zeros(places, d, u, v, b, turned, z, acc, rhs, copies, copy_u, copy_b, copy_v):
+def few_zeros(places, d, u, v, b, turned, z, acc, rhs, copies, copy_u, copy_b, copies_v):
     zeros = [places.nth(n, 0) for n in range(3)]
     starts = [sum(MANY_CHUNKS[:i]) for i in range(len(copies) + 1)]
 
     def turn(i):
         turned[:, starts[i] : starts[i + 1]] = v[starts[i] : starts[i + 1]].T
 
-    copy_v.wait()
+    copies_v[0].wait()
     turn(0)
     for i, c in enumerate(copies):
         c.wait()
+        if i + 1 < len(copies):
+            copies_v[i + 1].wait()
         part = slice(starts[i], starts[i + 1])
         rows = [turned[pl.ds(pl.multiple_of(RANK * n, RANK), RANK), part] for n in zeros]
         product = mul(jnp.concatenate(rows, axis=0), d[part])
@@ -201,25 +205,41 @@
         parts = [pl.ds(sum(sizes[:i]), sizes[i]) for i in range(len(sizes))]
         return [pltpu.make_async_copy(d_hbm.at[p], d.at[p], sems.at[i]) for i, p in enumerate(parts)]
 
-    copy_u = pltpu.make_async_copy(u_hbm, u, sems.at[n])
-    copy_b = pltpu.make_async_copy(b_hbm, b, sems.at[n + 1])
-    copy_v = pltpu.make_async_copy(v_hbm, v, sems.at[n + 2])
+    def pieces_of_v(sizes):
+        parts = [pl.ds(sum(sizes[:i]), sizes[i]) for i in range(len(sizes))]
+        return [pltpu.make_async_copy(v_hbm.at[p], v.at[p], sems.at[n + i]) for i, p in enumerate(parts)]
+
     places = Places(-1)
     few = places.ones <= 2
+    tile_0, tile_1, _ = tiles_of(places)
+
+    def tiles_of_u():
+        parts = [
+            pl.ds(pl.multiple_of(2 * RANK * t, 2 * RANK), 2 * RANK)
+            for t in (tile_0, tile_1, LEVELS // 2 - tile_0 - tile_1)
+        ]
+        return [
+            pltpu.make_async_copy(u_hbm.at[:, p], u.at[:, p], sems.at[2 * n + i]) for i, p in enumerate(parts)
+        ]
+
+    copy_u = pltpu.make_async_copy(u_hbm, u, sems.at[2 * n])
+    copy_b = pltpu.make_async_copy(b_hbm, b, sems.at[2 * n + 3])
+    copy_v = pltpu.make_async_copy(v_hbm, v, sems.at[n])
 
     @pl.when(few)
     def _():
-        copies = pieces_of(FEW_CHUNKS)
-        for c in (copy_b, copy_u, copies[0], copy_v, *copies[1:]):
+        copies, tiles = pieces_of(FEW_CHUNKS), tiles_of_u()
+        for c in (copy_b, *tiles[:2], copies[0], copy_v, *copies[1:], tiles[2]):
             c.start()
 
     @pl.when(jnp.logical_not(few))
     def _():
-        copies = pieces_of(MANY_CHUNKS)
-        for c in (copy_v, *copies, copy_u, copy_b):
-            c.start()
-
-    tile_0, _, _ = tiles_of(places)
+        for pair in zip(pieces_of_v(MANY_CHUNKS), pieces_of(MANY_CHUNKS)):
+            for c in pair:
+                c.start()
+        copy_u.start()
+        copy_b.start()
+
     plan = []
     for position in range(PIECES[0]):
         one, zero, valid = places.next_piece(position)
@@ -231,11 +251,11 @@
 
     @pl.when(few)
     def _():
-        few_ones(places, d, u, v, b, x, acc, rhs, pieces_of(FEW_CHUNKS), copy_u, copy_b, copy_v)
+        few_ones(places, d, u, v, b, x, acc, rhs, pieces_of(FEW_CHUNKS), tiles_of_u(), copy_b, copy_v)
 
     @pl.when(jnp.logical_not(few))
     def _():
-        few_zeros(places, d, u, v, b, turned, z, acc, rhs, pieces_of(MANY_CHUNKS), copy_u, copy_b, copy_v)
+        few_zeros(places, d, u, v, b, turned, z, acc, rhs, pieces_of(MANY_CHUNKS), copy_u, copy_b, pieces_of_v(MANY_CHUNKS))
 
     row_id = lax.broadcasted_iota(jnp.int32, (RANK, RANK), 0)
     lane_id = lax.broadcasted_iota(jnp.int32, (RANK, RANK), 1)
@@ -391,7 +411,7 @@
             pltpu.VMEM((3 * RANK, size), f32),
             pltpu.VMEM((STATE, STATE), f32),
             pltpu.VMEM((8, STATE), f32),
-            pltpu.SemaphoreType.DMA((max(len(FEW_CHUNKS), len(MANY_CHUNKS)) + 3,)),
+            pltpu.SemaphoreType.DMA((2 * max(len(FEW_CHUNKS), len(MANY_CHUNKS)) + 4,)),
         ],
         compiler_params=pltpu.CompilerParams(vmem_limit_bytes=30 << 20),
     )(

time: 39.9 us -> 39.9 us (level)
  starting transfers between devices: 15.5 us -> 16.2 us
  waiting for transfers between devices: 7.71 us -> 7.05 us
    ppermute x6, starting transfers between devices: 15.5 us -> 16.2 us  [swapped(): lax.ppermute(x, 'leaf', [(i, i ^ distance) for i in range(lax.axis_size('...]
    ppermute x6, waiting for transfers between devices: 7.71 us -> 7.05 us  [swapped(): lax.ppermute(x, 'leaf', [(i, i ^ distance) for i in range(lax.axis_size('...]
where the time goes in v8:
time: 39.9 us; the launch traced here: 39.7 us
  Pallas kernels  16.4 us (41%)
  starting transfers between devices  16.2 us (41%)
  waiting for transfers between devices  7.05 us (18%)
    ppermute x6, starting transfers between devices, swapped(): lax.ppermute(x, 'leaf', [(i, i ^ distance) for i in range(lax.axis_size('...  16.2 us
    pallas_call x11, Pallas kernels, call(): pl.pallas_call(body, name=name, in_specs=[vmem] * count + [pl.BlockSpec(m...  8.92 us
    pallas_call x1, Pallas kernels, on_device(): pl.pallas_call(first_kernel, name='first', in_specs=[pl.BlockSpec(memory_...  7.45 us
    ppermute x6, waiting for transfers between devices, swapped(): lax.ppermute(x, 'leaf', [(i, i ^ distance) for i in range(lax.axis_size('...  7.05 us
  transfers between devices with their start and end apart: 6, of which 5 were waited for; matrix products, arithmetic and copies ran while one was open for 0% of the time, Pallas kernels for 16%

profile of v8, /device:TPU:32, one launch (start us, length us, event | category | flops | bytes accessed | tf_op | source)
XLA Modules:
  0.0 39.7 jit_solution(15571094562428790685)
XLA Ops:
  0.0 7.5 %first.1 = (f32[312,128]{1,0:T(8,128)S(1)}, bf16[2048,2048]{1,0:T(8,128)(2,1)S(1)}, bf16[2048,384]{1,0:T(8,128)(2,1)S(1)}, bf16[8,2048]{1,0:T(8,128)(2,1)S(1)}, f32[8,384]{1,0:T(8,128)S(1)}) custom-call(s32[6]{0:T(128)} %ranks.1, bf16[8,2048]{1,0:T(8,128)(2,1)} %b_hbm.1, bf16[2048,2048]{1,0:T(8,128)(2,1)} %d_hbm.1, bf16[2048,384]{1,0:T(8,128)(2,1)} %u_hbm.1, ...), custom_call_target="tpu_custom_call" | custom-call | tf_op jit(solution)/shard_map/first/pallas_call | solution.py:395
  7.5 0.1 collective-permute-start
  7.6 1.4 %collective-permute-done.refs_1_ = f32[312,128]{1,0:T(8,128)S(1)} collective-permute-done((f32[312,128]{1,0:T(8,128)S(1)}, f32[312,128]{1,0:T(8,128)S(1)}, u32[]{:S(2)}, u32[]{:S(2)}) %collective-permute-start) | collective-permute-done | bytes 159776 | tf_op jit(solution)/shard_map/ppermute | solution.py:388
  8.9 0.4 %level_0.1 = (f32[216,128]{1,0:T(8,128)S(1)}, f32[328,64]{1,0:T(8,128)S(1)}) custom-call(f32[312,128]{1,0:T(8,128)S(1)} %get-tuple-element.26.refs_0_, f32[312,128]{1,0:T(8,128)S(1)} %collective-permute-done.refs_1_), custom_call_target="tpu_custom_call" | custom-call | tf_op jit(solution)/shard_map/level_0/pallas_call | solution.py:377
  9.4 1.9 %collective-permute-start.1 = (f32[216,128]{1,0:T(8,128)S(1)}, f32[216,128]{1,0:T(8,128)S(1)}, u32[]{:S(2)}, u32[]{:S(2)}) collective-permute-start(f32[216,128]{1,0:T(8,128)S(1)} %get-tuple-element.27.refs_4_.refs_0_), channel_id=1, source_target_pairs={{0,8},{4,12},{8,0},{12,4},{16,24},{20,28},{24,16},{28,20},{32,40},... | collective-permute-start | bytes 331784 | tf_op jit(solution)/shard_map/ppermute | solution.py:388
  11.3 2.5 %mapped_1.1 = (bf16[384,1024]{1,0:T(8,128)(2,1)S(1)}, f32[8,1024]{1,0:T(8,128)S(1)}) custom-call(bf16[2048,2048]{1,0:T(8,128)(2,1)S(1)} %get-tuple-element.28.refs_0_, bf16[2048,384]{1,0:T(8,128)(2,1)S(1)} %get-tuple-element.29.refs_1_, bf16[8,2048]{1,0:T(8,128)(2,1)S(1)} %get-tuple-element.30.refs_2_, f32[8,384]{1,0:T(8,128)S(1)} %get-tuple-element.31.refs_3_, ...), custom_call_target="tpu_custom_call" | custom-call | tf_op jit(solution)/shard_map/mapped_1/pallas_call | solution.py:377
  13.7 0.9 %collective-permute-done.1.refs_1_ = f32[216,128]{1,0:T(8,128)S(1)} collective-permute-done((f32[216,128]{1,0:T(8,128)S(1)}, f32[216,128]{1,0:T(8,128)S(1)}, u32[]{:S(2)}, u32[]{:S(2)}) %collective-permute-start.1) | collective-permute-done | bytes 110624 | tf_op jit(solution)/shard_map/ppermute | solution.py:388
  14.6 0.4 level_1.1
  15.0 3.5 %collective-permute-start.2 = (f32[144,128]{1,0:T(8,128)S(1)}, f32[144,128]{1,0:T(8,128)S(1)}, u32[]{:S(2)}, u32[]{:S(2)}) collective-permute-start(f32[144,128]{1,0:T(8,128)S(1)} %get-tuple-element.34.refs_4_.refs_0_), channel_id=1, source_target_pairs={{0,16},{4,20},{8,24},{12,28},{16,0},{20,4},{24,8},{28,12},{32,48},... | collective-permute-start | bytes 221192 | tf_op jit(solution)/shard_map/ppermute | solution.py:388
  18.5 2.5 %mapped_2.1 = (bf16[384,1024]{1,0:T(8,128)(2,1)S(1)}, f32[8,1024]{1,0:T(8,128)S(1)}) custom-call(bf16[2048,2048]{1,0:T(8,128)(2,1)S(1)} %get-tuple-element.28.refs_0_, bf16[2048,384]{1,0:T(8,128)(2,1)S(1)} %get-tuple-element.29.refs_1_, bf16[8,2048]{1,0:T(8,128)(2,1)S(1)} %get-tuple-element.30.refs_2_, f32[8,384]{1,0:T(8,128)S(1)} %get-tuple-element.31.refs_3_, ...), custom_call_target="tpu_custom_call" | custom-call | tf_op jit(solution)/shard_map/mapped_2/pallas_call | solution.py:377
  21.0 0.0 collective-permute-done.2.refs_1_
  21.0 0.4 level_2.1
  21.3 6.2 %collective-permute-start.3 = (f32[80,128]{1,0:T(8,128)S(1)}, f32[80,128]{1,0:T(8,128)S(1)}, u32[]{:S(2)}, u32[]{:S(2)}) collective-permute-start(f32[80,128]{1,0:T(8,128)S(1)} %get-tuple-element.37.refs_0_), channel_id=1, source_target_pairs={{0,48},{4,52},{8,56},{12,60},{16,32},{20,36},{24,40},{28,44},{32,1... | collective-permute-start | bytes 122888 | tf_op jit(solution)/shard_map/ppermute | solution.py:388
  27.5 0.4 coefficients.1.refs_2_.refs_1_
  27.9 1.6 %collective-permute-done.3.refs_1_ = f32[80,128]{1,0:T(8,128)S(1)} collective-permute-done((f32[80,128]{1,0:T(8,128)S(1)}, f32[80,128]{1,0:T(8,128)S(1)}, u32[]{:S(2)}, u32[]{:S(2)}) %collective-permute-start.3) | collective-permute-done | bytes 40992 | tf_op jit(solution)/shard_map/ppermute | solution.py:388
  29.5 0.3 level_3.1
  29.8 1.7 %collective-permute-start.4 = (f32[40,128]{1,0:T(8,128)S(1)}, f32[40,128]{1,0:T(8,128)S(1)}, u32[]{:S(2)}, u32[]{:S(2)}) collective-permute-start(f32[40,128]{1,0:T(8,128)S(1)} %get-tuple-element.41.refs_0_), channel_id=1, source_target_pairs={{0,64},{4,68},{8,72},{12,76},{16,80},{20,84},{24,88},{28,92},{32,9... | collective-permute-start | bytes 61448 | tf_op jit(solution)/shard_map/ppermute | solution.py:388
  31.5 0.7 %basis.1.refs_2_.refs_1_ = f32[136,2048]{1,0:T(8,128)S(1)} custom-call(f32[136,64]{1,0:T(8,128)S(1)} %get-tuple-element.42.refs_0_, f32[200,192]{1,0:T(8,128)S(1)} %coefficients.1.refs_2_.refs_1_, bf16[384,1024]{1,0:T(8,128)(2,1)S(1)} %get-tuple-element.32.refs_2_, bf16[384,1024]{1,0:T(8,128)(2,1)S(1)} %get-tuple-element.35.refs_2_.refs_3_, ...), custom_call_target="tpu_custom_call" | custom-call | tf_op jit(solution)/shard_map/basis/pallas_call | solution.py:377
  32.1 1.5 %collective-permute-done.4.refs_1_ = f32[40,128]{1,0:T(8,128)S(1)} collective-permute-done((f32[40,128]{1,0:T(8,128)S(1)}, f32[40,128]{1,0:T(8,128)S(1)}, u32[]{:S(2)}, u32[]{:S(2)}) %collective-permute-start.4) | collective-permute-done | bytes 20512 | tf_op jit(solution)/shard_map/ppermute | solution.py:388
  33.7 0.3 level_4.1
  33.9 2.9 %collective-permute-start.5 = (f32[8,128]{1,0:T(8,128)S(1)}, f32[8,128]{1,0:T(8,128)S(1)}, u32[]{:S(2)}, u32[]{:S(2)}) collective-permute-start(f32[8,128]{1,0:T(8,128)S(1)} %get-tuple-element.43), channel_id=1, source_target_pairs={{0,192},{4,196},{8,200},{12,204},{16,208},{20,212},{24,216},{28,22... | collective-permute-start | bytes 12296 | tf_op jit(solution)/shard_map/ppermute | solution.py:388
  36.8 0.3 late.1
  37.1 1.7 %collective-permute-done.5.refs_0_ = f32[8,128]{1,0:T(8,128)S(1)} collective-permute-done((f32[8,128]{1,0:T(8,128)S(1)}, f32[8,128]{1,0:T(8,128)S(1)}, u32[]{:S(2)}, u32[]{:S(2)}) %collective-permute-start.5) | collective-permute-done | bytes 4128 | tf_op jit(solution)/shard_map/ppermute | solution.py:388
  38.8 0.9 %last.1 = f32[8,2048]{1,0:T(8,128)} custom-call(f32[8,128]{1,0:T(8,128)S(1)} %collective-permute-done.5.refs_0_, bf16[192,2048]{1,0:T(8,128)(2,1)S(1)} %get-tuple-element.45.refs_1_, f32[8,2048]{1,0:T(8,128)S(1)} %get-tuple-element.46.refs_2_), custom_call_target="tpu_custom_call" | custom-call | tf_op jit(solution)/shard_map/last/pallas_call | solution.py:377
Async XLA Ops:
  7.5 1.5 %collective-permute-start = (f32[312,128]{1,0:T(8,128)S(1)}, f32[312,128]{1,0:T(8,128)S(1)}, u32[]{:S(2)}, u32[]{:S(2)}) collective-permute-start(f32[312,128]{1,0:T(8,128)S(1)} %get-tuple-element.26.refs_0_), channel_id=1, source_target_pairs={{0,4},{4,0},{8,12},{12,8},{16,20},{20,16},{24,28},{28,24},{32,36},... | collective-permute-start | bytes 479240 | tf_op jit(solution)/shard_map/ppermute | solution.py:388
  9.4 5.3 %collective-permute-start.1 = (f32[216,128]{1,0:T(8,128)S(1)}, f32[216,128]{1,0:T(8,128)S(1)}, u32[]{:S(2)}, u32[]{:S(2)}) collective-permute-start(f32[216,128]{1,0:T(8,128)S(1)} %get-tuple-element.27.refs_4_.refs_0_), channel_id=1, source_target_pairs={{0,8},{4,12},{8,0},{12,4},{16,24},{20,28},{24,16},{28,20},{32,40},... | collective-permute-start | bytes 331784 | tf_op jit(solution)/shard_map/ppermute | solution.py:388
  15.0 6.0 %collective-permute-start.2 = (f32[144,128]{1,0:T(8,128)S(1)}, f32[144,128]{1,0:T(8,128)S(1)}, u32[]{:S(2)}, u32[]{:S(2)}) collective-permute-start(f32[144,128]{1,0:T(8,128)S(1)} %get-tuple-element.34.refs_4_.refs_0_), channel_id=1, source_target_pairs={{0,16},{4,20},{8,24},{12,28},{16,0},{20,4},{24,8},{28,12},{32,48},... | collective-permute-start | bytes 221192 | tf_op jit(solution)/shard_map/ppermute | solution.py:388
  21.3 8.1 %collective-permute-start.3 = (f32[80,128]{1,0:T(8,128)S(1)}, f32[80,128]{1,0:T(8,128)S(1)}, u32[]{:S(2)}, u32[]{:S(2)}) collective-permute-start(f32[80,128]{1,0:T(8,128)S(1)} %get-tuple-element.37.refs_0_), channel_id=1, source_target_pairs={{0,48},{4,52},{8,56},{12,60},{16,32},{20,36},{24,40},{28,44},{32,1... | collective-permute-start | bytes 122888 | tf_op jit(solution)/shard_map/ppermute | solution.py:388
  29.8 3.9 %collective-permute-start.4 = (f32[40,128]{1,0:T(8,128)S(1)}, f32[40,128]{1,0:T(8,128)S(1)}, u32[]{:S(2)}, u32[]{:S(2)}) collective-permute-start(f32[40,128]{1,0:T(8,128)S(1)} %get-tuple-element.41.refs_0_), channel_id=1, source_target_pairs={{0,64},{4,68},{8,72},{12,76},{16,80},{20,84},{24,88},{28,92},{32,9... | collective-permute-start | bytes 61448 | tf_op jit(solution)/shard_map/ppermute | solution.py:388
  33.9 4.8 %collective-permute-start.5 = (f32[8,128]{1,0:T(8,128)S(1)}, f32[8,128]{1,0:T(8,128)S(1)}, u32[]{:S(2)}, u32[]{:S(2)}) collective-permute-start(f32[8,128]{1,0:T(8,128)S(1)} %get-tuple-element.43), channel_id=1, source_target_pairs={{0,192},{4,196},{8,200},{12,204},{16,208},{20,212},{24,216},{28,22... | collective-permute-start | bytes 12296 | tf_op jit(solution)/shard_map/ppermute | solution.py:388

commit v9 on v8

--- a/solution.py
+++ b/solution.py
@@ -198,7 +198,7 @@
     return tile_0, tile_1, free
 
 
-def first_kernel(ranks, b_hbm, d_hbm, u_hbm, v_hbm, send, d, u, b, keeps, v, x, turned, z, acc, rhs, sems):
+def first_kernel(ranks, b_hbm, d_hbm, u_hbm, v_hbm, send, d, u, b, keeps, v, x, turned, z, acc, rhs, plan, sems):
     n = max(len(FEW_CHUNKS), len(MANY_CHUNKS))
 
     def pieces_of(sizes):
@@ -240,26 +240,34 @@
         copy_u.start()
         copy_b.start()
 
-    plan = []
-    for position in range(PIECES[0]):
-        one, zero, valid = places.next_piece(position)
-        m, l = places.nth(one, 1), places.nth(zero, 0)
-        start = jnp.where(few, jnp.where(m // 2 == tile_0, 0, 2 * RANK) + RANK * (m % 2), RANK * m)
-        lane_piece = jnp.where(few, l, jnp.minimum(zero, 2))
-        plan.append((start, lane_piece, ranks[m], jnp.where(valid, ranks[l], 0)))
-    keeps[...] = keep_row(ranks)
+    def write_plan(few):
+        for position in range(PIECES[0]):
+            one, zero, valid = places.next_piece(position)
+            m, l = places.nth(one, 1), places.nth(zero, 0)
+            if few:
+                plan[4 * position] = jnp.where(m // 2 == tile_0, 0, 2 * RANK) + RANK * (m % 2)
+                plan[4 * position + 1] = l
+            else:
+                plan[4 * position] = RANK * m
+                plan[4 * position + 1] = jnp.minimum(zero, 2)
+            plan[4 * position + 2] = ranks[m]
+            plan[4 * position + 3] = jnp.where(valid, ranks[l], 0)
+        keeps[...] = keep_row(ranks)
 
     @pl.when(few)
     def _():
+        write_plan(True)
         few_ones(places, d, u, v, b, x, acc, rhs, pieces_of(FEW_CHUNKS), tiles_of_u(), copy_b, copy_v)
 
     @pl.when(jnp.logical_not(few))
     def _():
+        write_plan(False)
         few_zeros(places, d, u, v, b, turned, z, acc, rhs, pieces_of(MANY_CHUNKS), copy_u, copy_b, pieces_of_v(MANY_CHUNKS))
 
     row_id = lax.broadcasted_iota(jnp.int32, (RANK, RANK), 0)
     lane_id = lax.broadcasted_iota(jnp.int32, (RANK, RANK), 1)
-    for position, (start, lane_piece, rank_m, rank_l) in enumerate(plan):
+    for position in range(PIECES[0]):
+        start, lane_piece, rank_m, rank_l = [plan[4 * position + k] for k in range(4)]
         rows = pl.ds(pl.multiple_of(start, RANK), RANK)
         lanes = pl.ds(pl.multiple_of(2 * RANK * (lane_piece // 2), 2 * RANK), 2 * RANK)
         tile = acc[rows, lanes]
@@ -411,6 +419,7 @@
             pltpu.VMEM((3 * RANK, size), f32),
             pltpu.VMEM((STATE, STATE), f32),
             pltpu.VMEM((8, STATE), f32),
+            pltpu.SMEM((4 * PIECES[0],), jnp.int32),
             pltpu.SemaphoreType.DMA((2 * max(len(FEW_CHUNKS), len(MANY_CHUNKS)) + 4,)),
         ],
         compiler_params=pltpu.CompilerParams(vmem_limit_bytes=30 << 20),

time: 39.9 us -> 39.6 us (level)
  starting transfers between devices: 16.2 us -> 15.8 us
    ppermute x6, starting transfers between devices: 16.2 us -> 15.8 us  [swapped(): lax.ppermute(x, 'leaf', [(i, i ^ distance) for i in range(lax.axis_size('...]
where the time goes in v9:
time: 39.6 us; the launch traced here: 39.5 us
  Pallas kernels  16.2 us (41%)
  starting transfers between devices  15.8 us (40%)
  waiting for transfers between devices  7.44 us (19%)
    ppermute x6, starting transfers between devices, swapped(): lax.ppermute(x, 'leaf', [(i, i ^ distance) for i in range(lax.axis_size('...  15.8 us
    pallas_call x11, Pallas kernels, call(): pl.pallas_call(body, name=name, in_specs=[vmem] * count + [pl.BlockSpec(m...  8.91 us
    ppermute x6, waiting for transfers between devices, swapped(): lax.ppermute(x, 'leaf', [(i, i ^ distance) for i in range(lax.axis_size('...  7.44 us
    pallas_call x1, Pallas kernels, on_device(): pl.pallas_call(first_kernel, name='first', in_specs=[pl.BlockSpec(memory_...  7.29 us
  transfers between devices with their start and end apart: 6, of which 5 were waited for; matrix products, arithmetic and copies ran while one was open for 0% of the time, Pallas kernels for 16%

profile of v9, /device:TPU:32, one launch (start us, length us, event | category | flops | bytes accessed | tf_op | source)
XLA Modules:
  0.0 39.5 jit_solution(1009012289993674803)
XLA Ops:
  0.0 7.3 %first.1 = (f32[312,128]{1,0:T(8,128)S(1)}, bf16[2048,2048]{1,0:T(8,128)(2,1)S(1)}, bf16[2048,384]{1,0:T(8,128)(2,1)S(1)}, bf16[8,2048]{1,0:T(8,128)(2,1)S(1)}, f32[8,384]{1,0:T(8,128)S(1)}) custom-call(s32[6]{0:T(128)} %ranks.1, bf16[8,2048]{1,0:T(8,128)(2,1)} %b_hbm.1, bf16[2048,2048]{1,0:T(8,128)(2,1)} %d_hbm.1, bf16[2048,384]{1,0:T(8,128)(2,1)} %u_hbm.1, ...), custom_call_target="tpu_custom_call" | custom-call | tf_op jit(solution)/shard_map/first/pallas_call | solution.py:403
  7.3 0.1 collective-permute-start
  7.4 1.4 %collective-permute-done.refs_1_ = f32[312,128]{1,0:T(8,128)S(1)} collective-permute-done((f32[312,128]{1,0:T(8,128)S(1)}, f32[312,128]{1,0:T(8,128)S(1)}, u32[]{:S(2)}, u32[]{:S(2)}) %collective-permute-start) | collective-permute-done | bytes 159776 | tf_op jit(solution)/shard_map/ppermute | solution.py:396
  8.8 0.4 %level_0.1 = (f32[216,128]{1,0:T(8,128)S(1)}, f32[328,64]{1,0:T(8,128)S(1)}) custom-call(f32[312,128]{1,0:T(8,128)S(1)} %get-tuple-element.26.refs_0_, f32[312,128]{1,0:T(8,128)S(1)} %collective-permute-done.refs_1_), custom_call_target="tpu_custom_call" | custom-call | tf_op jit(solution)/shard_map/level_0/pallas_call | solution.py:385
  9.2 1.9 %collective-permute-start.1 = (f32[216,128]{1,0:T(8,128)S(1)}, f32[216,128]{1,0:T(8,128)S(1)}, u32[]{:S(2)}, u32[]{:S(2)}) collective-permute-start(f32[216,128]{1,0:T(8,128)S(1)} %get-tuple-element.27.refs_4_.refs_0_), channel_id=1, source_target_pairs={{0,8},{4,12},{8,0},{12,4},{16,24},{20,28},{24,16},{28,20},{32,40},... | collective-permute-start | bytes 331784 | tf_op jit(solution)/shard_map/ppermute | solution.py:396
  11.1 2.5 %mapped_1.1 = (bf16[384,1024]{1,0:T(8,128)(2,1)S(1)}, f32[8,1024]{1,0:T(8,128)S(1)}) custom-call(bf16[2048,2048]{1,0:T(8,128)(2,1)S(1)} %get-tuple-element.28.refs_0_, bf16[2048,384]{1,0:T(8,128)(2,1)S(1)} %get-tuple-element.29.refs_1_, bf16[8,2048]{1,0:T(8,128)(2,1)S(1)} %get-tuple-element.30.refs_2_, f32[8,384]{1,0:T(8,128)S(1)} %get-tuple-element.31.refs_3_, ...), custom_call_target="tpu_custom_call" | custom-call | tf_op jit(solution)/shard_map/mapped_1/pallas_call | solution.py:385
  13.6 0.9 %collective-permute-done.1.refs_1_ = f32[216,128]{1,0:T(8,128)S(1)} collective-permute-done((f32[216,128]{1,0:T(8,128)S(1)}, f32[216,128]{1,0:T(8,128)S(1)}, u32[]{:S(2)}, u32[]{:S(2)}) %collective-permute-start.1) | collective-permute-done | bytes 110624 | tf_op jit(solution)/shard_map/ppermute | solution.py:396
  14.5 0.4 level_1.1
  14.8 3.5 %collective-permute-start.2 = (f32[144,128]{1,0:T(8,128)S(1)}, f32[144,128]{1,0:T(8,128)S(1)}, u32[]{:S(2)}, u32[]{:S(2)}) collective-permute-start(f32[144,128]{1,0:T(8,128)S(1)} %get-tuple-element.34.refs_4_.refs_0_), channel_id=1, source_target_pairs={{0,16},{4,20},{8,24},{12,28},{16,0},{20,4},{24,8},{28,12},{32,48},... | collective-permute-start | bytes 221192 | tf_op jit(solution)/shard_map/ppermute | solution.py:396
  18.3 2.5 %mapped_2.1 = (bf16[384,1024]{1,0:T(8,128)(2,1)S(1)}, f32[8,1024]{1,0:T(8,128)S(1)}) custom-call(bf16[2048,2048]{1,0:T(8,128)(2,1)S(1)} %get-tuple-element.28.refs_0_, bf16[2048,384]{1,0:T(8,128)(2,1)S(1)} %get-tuple-element.29.refs_1_, bf16[8,2048]{1,0:T(8,128)(2,1)S(1)} %get-tuple-element.30.refs_2_, f32[8,384]{1,0:T(8,128)S(1)} %get-tuple-element.31.refs_3_, ...), custom_call_target="tpu_custom_call" | custom-call | tf_op jit(solution)/shard_map/mapped_2/pallas_call | solution.py:385
  20.8 0.0 collective-permute-done.2.refs_1_
  20.8 0.4 level_2.1
  21.2 6.0 %collective-permute-start.3 = (f32[80,128]{1,0:T(8,128)S(1)}, f32[80,128]{1,0:T(8,128)S(1)}, u32[]{:S(2)}, u32[]{:S(2)}) collective-permute-start(f32[80,128]{1,0:T(8,128)S(1)} %get-tuple-element.37.refs_0_), channel_id=1, source_target_pairs={{0,48},{4,52},{8,56},{12,60},{16,32},{20,36},{24,40},{28,44},{32,1... | collective-permute-start | bytes 122888 | tf_op jit(solution)/shard_map/ppermute | solution.py:396
  27.2 0.4 coefficients.1.refs_2_.refs_1_
  27.6 1.7 %collective-permute-done.3.refs_1_ = f32[80,128]{1,0:T(8,128)S(1)} collective-permute-done((f32[80,128]{1,0:T(8,128)S(1)}, f32[80,128]{1,0:T(8,128)S(1)}, u32[]{:S(2)}, u32[]{:S(2)}) %collective-permute-start.3) | collective-permute-done | bytes 40992 | tf_op jit(solution)/shard_map/ppermute | solution.py:396
  29.3 0.3 level_3.1
  29.6 1.6 %collective-permute-start.4 = (f32[40,128]{1,0:T(8,128)S(1)}, f32[40,128]{1,0:T(8,128)S(1)}, u32[]{:S(2)}, u32[]{:S(2)}) collective-permute-start(f32[40,128]{1,0:T(8,128)S(1)} %get-tuple-element.41.refs_0_), channel_id=1, source_target_pairs={{0,64},{4,68},{8,72},{12,76},{16,80},{20,84},{24,88},{28,92},{32,9... | collective-permute-start | bytes 61448 | tf_op jit(solution)/shard_map/ppermute | solution.py:396
  31.2 0.7 %basis.1.refs_2_.refs_1_ = f32[136,2048]{1,0:T(8,128)S(1)} custom-call(f32[136,64]{1,0:T(8,128)S(1)} %get-tuple-element.42.refs_0_, f32[200,192]{1,0:T(8,128)S(1)} %coefficients.1.refs_2_.refs_1_, bf16[384,1024]{1,0:T(8,128)(2,1)S(1)} %get-tuple-element.32.refs_2_, bf16[384,1024]{1,0:T(8,128)(2,1)S(1)} %get-tuple-element.35.refs_2_.refs_3_, ...), custom_call_target="tpu_custom_call" | custom-call | tf_op jit(solution)/shard_map/basis/pallas_call | solution.py:385
  31.8 1.7 %collective-permute-done.4.refs_1_ = f32[40,128]{1,0:T(8,128)S(1)} collective-permute-done((f32[40,128]{1,0:T(8,128)S(1)}, f32[40,128]{1,0:T(8,128)S(1)}, u32[]{:S(2)}, u32[]{:S(2)}) %collective-permute-start.4) | collective-permute-done | bytes 20512 | tf_op jit(solution)/shard_map/ppermute | solution.py:396
  33.5 0.3 level_4.1
  33.8 2.7 %collective-permute-start.5 = (f32[8,128]{1,0:T(8,128)S(1)}, f32[8,128]{1,0:T(8,128)S(1)}, u32[]{:S(2)}, u32[]{:S(2)}) collective-permute-start(f32[8,128]{1,0:T(8,128)S(1)} %get-tuple-element.43), channel_id=1, source_target_pairs={{0,192},{4,196},{8,200},{12,204},{16,208},{20,212},{24,216},{28,22... | collective-permute-start | bytes 12296 | tf_op jit(solution)/shard_map/ppermute | solution.py:396
  36.5 0.3 late.1
  36.8 1.8 %collective-permute-done.5.refs_0_ = f32[8,128]{1,0:T(8,128)S(1)} collective-permute-done((f32[8,128]{1,0:T(8,128)S(1)}, f32[8,128]{1,0:T(8,128)S(1)}, u32[]{:S(2)}, u32[]{:S(2)}) %collective-permute-start.5) | collective-permute-done | bytes 4128 | tf_op jit(solution)/shard_map/ppermute | solution.py:396
  38.6 0.9 %last.1 = f32[8,2048]{1,0:T(8,128)} custom-call(f32[8,128]{1,0:T(8,128)S(1)} %collective-permute-done.5.refs_0_, bf16[192,2048]{1,0:T(8,128)(2,1)S(1)} %get-tuple-element.45.refs_1_, f32[8,2048]{1,0:T(8,128)S(1)} %get-tuple-element.46.refs_2_), custom_call_target="tpu_custom_call" | custom-call | tf_op jit(solution)/shard_map/last/pallas_call | solution.py:385
Async XLA Ops:
  7.3 1.5 %collective-permute-start = (f32[312,128]{1,0:T(8,128)S(1)}, f32[312,128]{1,0:T(8,128)S(1)}, u32[]{:S(2)}, u32[]{:S(2)}) collective-permute-start(f32[312,128]{1,0:T(8,128)S(1)} %get-tuple-element.26.refs_0_), channel_id=1, source_target_pairs={{0,4},{4,0},{8,12},{12,8},{16,20},{20,16},{24,28},{28,24},{32,36},... | collective-permute-start | bytes 479240 | tf_op jit(solution)/shard_map/ppermute | solution.py:396
  9.2 5.3 %collective-permute-start.1 = (f32[216,128]{1,0:T(8,128)S(1)}, f32[216,128]{1,0:T(8,128)S(1)}, u32[]{:S(2)}, u32[]{:S(2)}) collective-permute-start(f32[216,128]{1,0:T(8,128)S(1)} %get-tuple-element.27.refs_4_.refs_0_), channel_id=1, source_target_pairs={{0,8},{4,12},{8,0},{12,4},{16,24},{20,28},{24,16},{28,20},{32,40},... | collective-permute-start | bytes 331784 | tf_op jit(solution)/shard_map/ppermute | solution.py:396
  14.8 5.9 %collective-permute-start.2 = (f32[144,128]{1,0:T(8,128)S(1)}, f32[144,128]{1,0:T(8,128)S(1)}, u32[]{:S(2)}, u32[]{:S(2)}) collective-permute-start(f32[144,128]{1,0:T(8,128)S(1)} %get-tuple-element.34.refs_4_.refs_0_), channel_id=1, source_target_pairs={{0,16},{4,20},{8,24},{12,28},{16,0},{20,4},{24,8},{28,12},{32,48},... | collective-permute-start | bytes 221192 | tf_op jit(solution)/shard_map/ppermute | solution.py:396
  21.2 8.2 %collective-permute-start.3 = (f32[80,128]{1,0:T(8,128)S(1)}, f32[80,128]{1,0:T(8,128)S(1)}, u32[]{:S(2)}, u32[]{:S(2)}) collective-permute-start(f32[80,128]{1,0:T(8,128)S(1)} %get-tuple-element.37.refs_0_), channel_id=1, source_target_pairs={{0,48},{4,52},{8,56},{12,60},{16,32},{20,36},{24,40},{28,44},{32,1... | collective-permute-start | bytes 122888 | tf_op jit(solution)/shard_map/ppermute | solution.py:396
  29.6 3.9 %collective-permute-start.4 = (f32[40,128]{1,0:T(8,128)S(1)}, f32[40,128]{1,0:T(8,128)S(1)}, u32[]{:S(2)}, u32[]{:S(2)}) collective-permute-start(f32[40,128]{1,0:T(8,128)S(1)} %get-tuple-element.41.refs_0_), channel_id=1, source_target_pairs={{0,64},{4,68},{8,72},{12,76},{16,80},{20,84},{24,88},{28,92},{32,9... | collective-permute-start | bytes 61448 | tf_op jit(solution)/shard_map/ppermute | solution.py:396
  33.8 4.8 %collective-permute-start.5 = (f32[8,128]{1,0:T(8,128)S(1)}, f32[8,128]{1,0:T(8,128)S(1)}, u32[]{:S(2)}, u32[]{:S(2)}) collective-permute-start(f32[8,128]{1,0:T(8,128)S(1)} %get-tuple-element.43), channel_id=1, source_target_pairs={{0,192},{4,196},{8,200},{12,204},{16,208},{20,212},{24,216},{28,22... | collective-permute-start | bytes 12296 | tf_op jit(solution)/shard_map/ppermute | solution.py:396
